TPU v7x, 32 devices: a whole 2x2x4 slice. The times are simulated.
32 devices in a mesh: seq: 32 (over z, y, x, core).
Axes of the slice: x: 2, y: 2, z: 4, core: 2. Of those that a mesh axis runs over, the one named last changes fastest.
Arguments:
- queries: bfloat16 [8192, 2048], P('seq'), may hold values from -30 to 30
- keys: bfloat16 [8192, 2048], P('seq'), may hold values from -9 to 9
- values: bfloat16 [8192, 2048], P('seq'), may hold values from -6 to 6
- grad_out: bfloat16 [8192, 2048], P('seq'), may hold values from -6 to 6
- proj_weight: bfloat16 [16, 128, 256], replicated, may hold values from -2.734375 to 2.734375
Outputs:
- grad_queries: bfloat16 [8192, 2048], P('seq')
- grad_keys: bfloat16 [8192, 2048], P('seq')
- grad_values: bfloat16 [8192, 2048], P('seq')
- grad_proj: float32 [2048, 256], P('seq')
All inputs are finite; a program needn't handle non-finite values.
Results may differ from a plain program's by a relative error of at most 0.01.
Values may be sent and summed in bfloat16 or wider, within the bound.
No kernel may reach another device: no remote copies, remote signals or barrier semaphores. Data moves between devices by JAX's collectives and lax.ppermute only.
A program may use at most 128 MiB of HBM per device.

v0:
```python
import math

import jax
import jax.numpy as jnp
from jax import lax
from jax.experimental import pallas as pl
from jax.experimental.pallas import tpu as pltpu
from jax.sharding import PartitionSpec as P


SEG = 256
STAT_ROWS = 8
DOT_ROWS = 16
HIDDEN = -1e30
BF = jnp.bfloat16
FL = jnp.float32


def dot_nn(a, b):
    return lax.dot_general(a, b, (((1,), (0,)), ((), ())), preferred_element_type=FL)


def dot_nt(a, b):
    return lax.dot_general(a, b, (((1,), (1,)), ((), ())), preferred_element_type=FL)


def dot_tn(a, b):
    return lax.dot_general(a, b, (((0,), (0,)), ((), ())), preferred_element_type=FL)


def struct(shape, dtype):
    return jax.ShapeDtypeStruct(shape, dtype)


def size_of(x):
    dtype = jnp.dtype(x.dtype)
    return math.prod(x.shape) * dtype.itemsize


def call(kernel, pos, ins, outs, scratch=(), spare=4):
    on_chip = pl.BlockSpec(memory_space=pltpu.VMEM)
    need = sum(size_of(x) for x in (*ins, *outs, *scratch))
    return pl.pallas_call(
        kernel,
        in_specs=[pl.BlockSpec(memory_space=pltpu.SMEM)] + [on_chip] * len(ins),
        out_specs=[on_chip] * len(outs),
        out_shape=list(outs),
        scratch_shapes=list(scratch),
        compiler_params=pltpu.CompilerParams(vmem_limit_bytes=need + spare * 2**20),
    )(pos, *ins)


class Plan:
    def __init__(self, devices, tokens_here, head_count, head_size, rank):
        self.inner = math.gcd(max(head_count // 2, 1), devices)
        self.outer = devices // self.inner
        self.heads = head_count // self.inner
        self.tokens = tokens_here
        self.group = tokens_here * self.inner
        self.head_size = head_size
        self.rank = rank
        self.pair = 2 * head_size
        self.width = self.heads * self.pair
        self.rows = self.heads * rank // self.outer
        self.margin = SEG // 2
        self.scale = head_size ** (-0.5)


def pack_kernel(plan, pos, a_ref, b_ref, *outs):
    hd, pair = plan.head_size, plan.pair
    for k, out in enumerate(outs):
        dest = pos[1] ^ k
        for h in range(plan.heads):
            col = pl.multiple_of((dest * plan.heads + h) * hd, hd)
            out[:, h * pair : h * pair + hd] = a_ref[:, pl.ds(col, hd)]
            out[:, h * pair + hd : (h + 1) * pair] = b_ref[:, pl.ds(col, hd)]


def unpack_pair_kernel(plan, pos, *refs):
    ins, (a_ref, b_ref) = refs[: plan.inner], refs[plan.inner :]
    hd, pair = plan.head_size, plan.pair
    for k, src in enumerate(ins):
        dest = pos[1] ^ k
        for h in range(plan.heads):
            col = pl.multiple_of((dest * plan.heads + h) * hd, hd)
            a_ref[:, pl.ds(col, hd)] = src[:, h * pair : h * pair + hd]
            b_ref[:, pl.ds(col, hd)] = src[:, h * pair + hd : (h + 1) * pair]


def unpack_kernel(plan, pos, *refs):
    ins, a_ref = refs[: plan.inner], refs[plan.inner]
    wide = plan.heads * plan.head_size
    for k, src in enumerate(ins):
        col = pl.multiple_of((pos[1] ^ k) * wide, wide)
        a_ref[:, pl.ds(col, wide)] = src[...]


def stats_kernel(plan, pos, *refs):
    pieces, w_ref = refs[: plan.inner], refs[plan.inner]
    kv_ref, first_ref, last_ref = refs[plan.inner + 1 : plan.inner + 4]
    outs = refs[plan.inner + 4 : plan.inner + 4 + plan.outer]
    logit_ref, expo_ref, part_ref = refs[plan.inner + 4 + plan.outer :]
    hd, pair, rank = plan.head_size, plan.pair, plan.rank
    for k, src in enumerate(pieces):
        row = pl.multiple_of((pos[1] ^ k) * plan.tokens, plan.tokens)
        kv_ref[pl.ds(row, plan.tokens), :] = src[...]
    first_ref[...] = kv_ref[: plan.margin, :]
    last_ref[...] = kv_ref[plan.group - plan.margin :, :]
    steps = plan.group // SEG
    tops, sums = [], []
    for h in range(plan.heads):

        def logits_step(i, top):
            at = pl.multiple_of(i * SEG, SEG)
            block = dot_nn(kv_ref[pl.ds(at, SEG), h * pair : h * pair + hd], w_ref[h])
            logit_ref[pl.ds(at, SEG), :] = block
            return jnp.maximum(top, jnp.max(block.reshape(SEG // 8, 8, rank), axis=0))

        top = lax.fori_loop(0, steps, logits_step, jnp.full((8, rank), -jnp.inf, FL))
        top = jnp.max(top, axis=0, keepdims=True)

        def expo_step(i, total):
            at = pl.multiple_of(i * SEG, SEG)
            block = jnp.exp(logit_ref[pl.ds(at, SEG), :] - top)
            expo_ref[pl.ds(at, SEG), :] = block.astype(BF)
            return total + jnp.sum(block.reshape(SEG // 8, 8, rank), axis=0)

        total = lax.fori_loop(0, steps, expo_step, jnp.zeros((8, rank), FL))
        total = jnp.sum(total, axis=0, keepdims=True)
        part_ref[h * rank : (h + 1) * rank, :] = dot_tn(
            expo_ref[...], kv_ref[:, h * pair : (h + 1) * pair]
        )
        tops.append(top)
        sums.append(total)
    pad = jnp.zeros((STAT_ROWS - 2 * plan.heads, rank), FL)
    stats = jnp.concatenate(tops + sums + [pad], axis=0)
    for k, out in enumerate(outs):
        row = pl.multiple_of((pos[0] ^ k) * plan.rows, plan.rows)
        out[: plan.rows, :] = part_ref[pl.ds(row, plan.rows), :]
        out[plan.rows :, :] = stats


def own_columns(plan, pos, wide):
    start = (pos[0] * plan.rows) % plan.rank
    row_at = lax.broadcasted_iota(jnp.int32, (plan.rows, wide), 0)
    col_at = lax.broadcasted_iota(jnp.int32, (plan.rows, wide), 1)
    return col_at == row_at + start


def combine_kernel(plan, pos, *refs):
    ins = refs[: plan.outer]
    full_ref, half_ref, stat_ref = refs[plan.outer :]
    heads, rows = plan.heads, plan.rows
    stats = [r[rows:, :] for r in ins]
    tops = [s[:heads, :] for s in stats]
    top = tops[0]
    for t in tops[1:]:
        top = jnp.maximum(top, t)
    weights = [jnp.exp(t - top) for t in tops]
    total = weights[0] * stats[0][heads : 2 * heads, :]
    for w, s in zip(weights[1:], stats[1:]):
        total = total + w * s[heads : 2 * heads, :]
    inverse = 1.0 / total
    stat_ref[:heads, :] = top
    stat_ref[heads : 2 * heads, :] = inverse
    stat_ref[2 * heads :, :] = jnp.zeros((STAT_ROWS - 2 * heads, plan.rank), FL)
    own = own_columns(plan, pos, plan.rank)
    head_at = (pos[0] * rows) // plan.rank

    def column(field):
        row = field[:1, :]
        for h in range(1, heads):
            row = jnp.where(head_at == h, field[h : h + 1, :], row)
        return jnp.sum(jnp.where(own, row, 0.0), axis=1, keepdims=True)

    result = ins[0][:rows, :] * column(weights[0])
    for w, r in zip(weights[1:], ins[1:]):
        result = result + r[:rows, :] * column(w)
    result = result * column(inverse)
    full_ref[...] = result
    half_ref[...] = result.astype(BF)


def attend_kernel(plan, total_groups, pos, *refs):
    outer, inner, heads = plan.outer, plan.inner, plan.heads
    kv_ref, before_ref, after_ref = refs[:3]
    bars = refs[3 : 3 + outer]
    qg = refs[3 + outer : 3 + outer + inner]
    at = 3 + outer + inner
    dq_outs = refs[at : at + inner]
    bar_outs = refs[at + inner : at + inner + outer]
    wg_ref, wg_before_ref, wg_after_ref = refs[at + inner + outer : at + inner + outer + 3]
    ext_ref, bar_ref, q_ref, acc_ref, dbar_ref, dq_ref = refs[
        at + inner + outer + 3 :
    ]
    hd, pair, rank, margin, group = plan.head_size, plan.pair, plan.rank, plan.margin, plan.group
    ext_ref[:margin, :] = before_ref[...]
    ext_ref[margin : margin + group, :] = kv_ref[...]
    ext_ref[margin + group :, :] = after_ref[...]
    for k, src in enumerate(bars):
        row = pl.multiple_of((pos[0] ^ k) * plan.rows, plan.rows)
        bar_ref[pl.ds(row, plan.rows), :] = src[...]
    for k, src in enumerate(qg):
        row = pl.multiple_of((pos[1] ^ k) * plan.tokens, plan.tokens)
        q_ref[pl.ds(row, plan.tokens), :] = src[...]
    acc_ref[...] = jnp.zeros(acc_ref.shape, FL)
    dbar_ref[...] = jnp.zeros(dbar_ref.shape, FL)
    segs = group // SEG
    at_start = pos[0] == 0
    at_end = pos[0] == total_groups - 1
    factor = plan.scale / math.log(2.0)

    def step(j, carry):
        row = pl.multiple_of(j * SEG, SEG)
        hide_low = jnp.where(jnp.logical_and(at_start, j == 0), HIDDEN, 0.0)
        hide_high = jnp.where(jnp.logical_and(at_end, j == segs - 1), HIDDEN, 0.0)
        loaded, scored = [], []
        for h in range(heads):
            low, mid, high = h * pair, h * pair + hd, (h + 1) * pair
            bar = slice(h * rank, (h + 1) * rank)
            key = jnp.concatenate([bar_ref[bar, :hd], ext_ref[pl.ds(row, 2 * SEG), low:mid]], axis=0)
            val = jnp.concatenate([bar_ref[bar, hd:], ext_ref[pl.ds(row, 2 * SEG), mid:high]], axis=0)
            query = q_ref[pl.ds(row, SEG), low:mid]
            grad = q_ref[pl.ds(row, SEG), mid:high]
            loaded.append((key, query, grad))
            scored.append((dot_nt(key, query), dot_nt(val, grad)))
        for h in range(heads):
            low, mid, high = h * pair, h * pair + hd, (h + 1) * pair
            bar = slice(h * rank, (h + 1) * rank)
            key, query, grad = loaded[h]
            scores, dprob = scored[h]
            scores = jnp.concatenate(
                [
                    scores[:rank],
                    scores[rank : rank + margin] + hide_low,
                    scores[rank + margin : rank + 2 * SEG - margin],
                    scores[rank + 2 * SEG - margin :] + hide_high,
                ],
                axis=0,
            )
            expo = jnp.exp2((scores - jnp.max(scores, axis=0, keepdims=True)) * factor)
            prob = expo * (1.0 / jnp.sum(expo, axis=0, keepdims=True))
            prob_b = prob.astype(BF)
            row_dot = jnp.sum(prob_b.astype(FL) * dprob, axis=0, keepdims=True)
            dscore = (prob * (dprob - row_dot)).astype(BF)
            dquery = dot_tn(key, dscore) * plan.scale
            dq_ref[pl.ds(row, SEG), h * hd : (h + 1) * hd] = jnp.transpose(dquery).astype(BF)
            dkey = dot_nn(dscore, query)
            dval = dot_nn(prob_b, grad)
            dbar_ref[bar, :hd] += dkey[:rank, :]
            dbar_ref[bar, hd:] += dval[:rank, :]
            acc_ref[pl.ds(row, 2 * SEG), low:mid] += dkey[rank:, :]
            acc_ref[pl.ds(row, 2 * SEG), mid:high] += dval[rank:, :]
        return carry

    lax.fori_loop(0, segs, step, 0)
    for h in range(heads):
        bar = slice(h * rank, (h + 1) * rank)
        dbar_ref[bar, :hd] = dbar_ref[bar, :hd] * plan.scale
        acc_ref[:, h * pair : h * pair + hd] = acc_ref[:, h * pair : h * pair + hd] * plan.scale
    for k, out in enumerate(dq_outs):
        row = pl.multiple_of((pos[1] ^ k) * plan.tokens, plan.tokens)
        out[...] = dq_ref[pl.ds(row, plan.tokens), :]
    for k, out in enumerate(bar_outs):
        row = pl.multiple_of((pos[0] ^ k) * plan.rows, plan.rows)
        out[...] = dbar_ref[pl.ds(row, plan.rows), :].astype(BF)
    wg_ref[...] = acc_ref[margin : margin + group, :]
    wg_before_ref[...] = acc_ref[:margin, :].astype(BF)
    wg_after_ref[...] = acc_ref[margin + group :, :].astype(BF)


def combine_grad_kernel(plan, pos, *refs):
    full_ref, ins = refs[0], refs[1 : 1 + plan.outer]
    out_ref = refs[1 + plan.outer]
    total = ins[0][...].astype(FL)
    for r in ins[1:]:
        total = total + r[...].astype(FL)
    half = total.astype(BF)
    out_ref[: plan.rows, :] = half
    column = jnp.sum(full_ref[...] * half.astype(FL), axis=1, keepdims=True)
    own = own_columns(plan, pos, plan.rank)
    rest = jnp.sum(jnp.where(own, column, 0.0), axis=0, keepdims=True)
    parts = []
    for _ in range(3):
        part = rest.astype(BF).astype(FL)
        parts.append(part)
        rest = rest - part
    parts.append(jnp.zeros((DOT_ROWS - 3, plan.rank), FL))
    out_ref[plan.rows :, :] = jnp.concatenate(parts, axis=0).astype(BF)


def finish_kernel(plan, pos, *refs):
    outer, inner, heads = plan.outer, plan.inner, plan.heads
    kv_ref, w_ref, stat_ref, wg_ref, before_ref, after_ref = refs[:6]
    bars = refs[6 : 6 + outer]
    at = 6 + outer
    outs = refs[at : at + inner]
    logit_grad_ref, bar_ref, grad_ref, sum_ref = refs[at + inner :]
    hd, pair, rank, margin, group = plan.head_size, plan.pair, plan.rank, plan.margin, plan.group
    dots = []
    for k, src in enumerate(bars):
        row = pl.multiple_of((pos[0] ^ k) * plan.rows, plan.rows)
        bar_ref[pl.ds(row, plan.rows), :] = src[: plan.rows, :]
        dots.append(jnp.sum(src[plan.rows :, :].astype(FL), axis=0, keepdims=True))
    segs = group // SEG
    for h in range(heads):
        low, high = h * pair, (h + 1) * pair
        column_dot = jnp.zeros((1, rank), FL)
        for k, d in enumerate(dots):
            here = ((pos[0] ^ k) * plan.rows) // rank == h
            column_dot = column_dot + jnp.where(here, d, 0.0)
        top = stat_ref[h : h + 1, :]
        inverse = stat_ref[heads + h : heads + h + 1, :]

        def step(i, carry):
            row = pl.multiple_of(i * SEG, SEG)
            both = kv_ref[pl.ds(row, SEG), low:high]
            key = both[:, :hd]
            dbar = bar_ref[h * rank : (h + 1) * rank, :]
            expo = jnp.exp(dot_nn(key, w_ref[h]) - top).astype(BF).astype(FL)
            prob = expo * inverse
            dprob = dot_nt(both, dbar)
            logit_grad = (prob * (dprob - column_dot)).astype(BF)
            sum_ref[...] = dot_nn(prob.astype(BF), dbar) + wg_ref[pl.ds(row, SEG), low:high]
            sum_ref[:, :hd] += dot_nt(logit_grad, w_ref[h])

            @pl.when(i == 0)
            def _():
                sum_ref[:margin, :] += before_ref[:, low:high].astype(FL)

            @pl.when(i == segs - 1)
            def _():
                sum_ref[SEG - margin :, :] += after_ref[:, low:high].astype(FL)

            grad_ref[pl.ds(row, SEG), low:high] = sum_ref[...].astype(BF)
            logit_grad_ref[pl.ds(row, SEG), h * rank : (h + 1) * rank] = logit_grad
            return carry

        lax.fori_loop(0, segs, step, 0)
    for k, out in enumerate(outs):
        row = pl.multiple_of((pos[1] ^ k) * plan.tokens, plan.tokens)
        out[...] = grad_ref[pl.ds(row, plan.tokens), :]


def proj_kernel(plan, pos, kv_ref, logit_grad_ref, *refs):
    outs, proj_ref = refs[: plan.outer], refs[plan.outer]
    hd, pair, rank = plan.head_size, plan.pair, plan.rank
    for h in range(plan.heads):
        proj_ref[h * hd : (h + 1) * hd, :] = dot_tn(
            kv_ref[:, h * pair : h * pair + hd], logit_grad_ref[:, h * rank : (h + 1) * rank]
        )
    piece = plan.heads * hd // plan.outer
    for k, out in enumerate(outs):
        row = pl.multiple_of((pos[0] ^ k) * piece, piece)
        out[...] = proj_ref[pl.ds(row, piece), :]


def exchange(fields, devices, stride):
    out = [fields[0]]
    for k in range(1, len(fields)):
        flip = [(i, i ^ (k * stride)) for i in range(devices)]
        out.append(lax.ppermute(fields[k], "seq", flip))
    return out


def swap_edges(upward, downward, devices, stride):
    up = [(i, i + stride) for i in range(devices - stride)]
    down = [(j, i) for i, j in up]
    return lax.ppermute(upward, "seq", up), lax.ppermute(downward, "seq", down)


def per_device(queries, keys, values, grad_out, proj_weight):
    tokens_here, row_width = queries.shape
    head_count, head_size, rank = proj_weight.shape
    devices = lax.axis_size("seq")
    plan = Plan(devices, tokens_here, head_count, head_size, rank)
    inner, outer, heads = plan.inner, plan.outer, plan.heads
    group, width, rows, margin = plan.group, plan.width, plan.rows, plan.margin
    me = lax.axis_index("seq")
    pos = jnp.stack([me // inner, me % inner]).astype(jnp.int32)

    def bind(kernel, *more):
        return lambda pos_ref, *refs: kernel(plan, *more, pos_ref, *refs)

    weight = lax.dynamic_slice_in_dim(proj_weight, (me % inner) * heads, heads, axis=0)
    wide_piece = struct((tokens_here, width), BF)
    kv_send = call(bind(pack_kernel), pos, [keys, values], [wide_piece] * inner)
    qg_send = call(bind(pack_kernel), pos, [queries, grad_out], [wide_piece] * inner)
    kv_pieces = exchange(kv_send, devices, 1)
    qg_pieces = exchange(qg_send, devices, 1)

    stat_piece = struct((rows + STAT_ROWS, rank), FL)
    kv_all, kv_first, kv_last, *part_send = call(
        bind(stats_kernel),
        pos,
        [*kv_pieces, weight],
        [struct((group, width), BF), struct((margin, width), BF), struct((margin, width), BF)]
        + [stat_piece] * outer,
        [
            pltpu.VMEM((group, rank), FL),
            pltpu.VMEM((group, rank), BF),
            pltpu.VMEM((heads * rank, plan.pair), FL),
        ],
    )
    parts = exchange(part_send, devices, inner)
    kv_before, kv_after = swap_edges(kv_last, kv_first, devices, inner)
    bar_full, bar_half, stats = call(
        bind(combine_kernel),
        pos,
        parts,
        [struct((rows, plan.pair), FL), struct((rows, plan.pair), BF), struct((STAT_ROWS, rank), FL)],
    )
    bars = exchange([bar_half] * outer, devices, inner)

    dq_piece = struct((tokens_here, heads * head_size), BF)
    edge = struct((margin, width), BF)
    results = call(
        bind(attend_kernel, outer),
        pos,
        [kv_all, kv_before, kv_after, *bars, *qg_pieces],
        [dq_piece] * inner
        + [struct((rows, plan.pair), BF)] * outer
        + [struct((group, width), FL), edge, edge],
        [
            pltpu.VMEM((group + 2 * margin, width), BF),
            pltpu.VMEM((heads * rank, plan.pair), BF),
            pltpu.VMEM((group, width), BF),
            pltpu.VMEM((group + 2 * margin, width), FL),
            pltpu.VMEM((heads * rank, plan.pair), FL),
            pltpu.VMEM((group, heads * head_size), BF),
        ],
    )
    dq_send = results[:inner]
    dbar_send = results[inner : inner + outer]
    wg, wg_before, wg_after = results[inner + outer :]
    dbar_parts = exchange(dbar_send, devices, inner)
    wg_from_before, wg_from_after = swap_edges(wg_after, wg_before, devices, inner)
    (dbar_half,) = call(
        bind(combine_grad_kernel),
        pos,
        [bar_full, *dbar_parts],
        [struct((rows + DOT_ROWS, plan.pair), BF)],
    )
    dbars = exchange([dbar_half] * outer, devices, inner)
    dq_pieces = exchange(dq_send, devices, 1)

    proj_piece = struct((heads * head_size // outer, rank), FL)
    results = call(
        bind(finish_kernel),
        pos,
        [kv_all, weight, stats, wg, wg_from_before, wg_from_after, *dbars],
        [wide_piece] * inner + [struct((group, heads * rank), BF)],
        [
            pltpu.VMEM((heads * rank, plan.pair), BF),
            pltpu.VMEM((group, width), BF),
            pltpu.VMEM((SEG, plan.pair), FL),
        ],
    )
    dkv_pieces = exchange(results[:inner], devices, 1)
    proj_send = call(
        bind(proj_kernel),
        pos,
        [kv_all, results[inner]],
        [proj_piece] * outer,
        [pltpu.VMEM((heads * head_size, rank), FL)],
    )
    proj_parts = exchange(proj_send, devices, inner)
    whole = struct((tokens_here, row_width), BF)
    (grad_queries,) = call(bind(unpack_kernel), pos, dq_pieces, [whole])
    proj_sum = proj_parts[0]
    for part in proj_parts[1:]:
        proj_sum = proj_sum + part
    place = [(o * inner + p, p * outer + o) for o in range(outer) for p in range(inner)]
    grad_proj = lax.ppermute(proj_sum, "seq", place)
    grad_keys, grad_values = call(bind(unpack_pair_kernel), pos, dkv_pieces, [whole, whole])
    return (grad_queries, grad_keys, grad_values, grad_proj)


def solution(mesh):
    in_specs = (P("seq", None), P("seq", None), P("seq", None), P("seq", None), P())
    out_specs = (P("seq", None), P("seq", None), P("seq", None), P("seq", None))
    return jax.shard_map(
        per_device, mesh=mesh, in_specs=in_specs, out_specs=out_specs, check_vma=False
    )
```

profile of v0, /device:TPU:0, one launch (start us, length us, event | category | flops | bytes accessed | tf_op | source)
XLA Modules:
  0.0 173.2 jit_solution(6988159402258727792)
XLA Ops:
  5.6 2.5 %collective-permute-start.1 = (bf16[256,512]{1,0:T(8,128)(2,1)S(1)}, bf16[256,512]{1,0:T(8,128)(2,1)S(1)}, u32[]{:S(2)}, u32[]{:S(2)}) collective-permute-start(bf16[256,512]{1,0:T(8,128)(2,1)S(1)} %get-tuple-element.62), channel_id=1, source_target_pairs={{0,2},{1,3},{2,0},{3,1},{4,6},{5,7},{6,4},{7,5},{8,10},{9,11},{10,... | collective-permute-start | bytes 786440 | tf_op jit(solution)/shard_map/ppermute | solution.py:362
  9.9 2.6 %collective-permute-start.5 = (bf16[256,512]{1,0:T(8,128)(2,1)S(1)}, bf16[256,512]{1,0:T(8,128)(2,1)S(1)}, u32[]{:S(2)}, u32[]{:S(2)}) collective-permute-start(bf16[256,512]{1,0:T(8,128)(2,1)S(1)} %get-tuple-element.66), channel_id=1, source_target_pairs={{0,6},{1,7},{2,4},{3,5},{4,2},{5,3},{6,0},{7,1},{8,14},{9,15},{10,... | collective-permute-start | bytes 786440 | tf_op jit(solution)/shard_map/ppermute | solution.py:362
  12.5 2.7 %collective-permute-done.1.refs_2_ = bf16[256,512]{1,0:T(8,128)(2,1)S(1)} collective-permute-done((bf16[256,512]{1,0:T(8,128)(2,1)S(1)}, bf16[256,512]{1,0:T(8,128)(2,1)S(1)}, u32[]{:S(2)}, u32[]{:S(2)}) %collective-permute-start.1) | collective-permute-done | bytes 262176 | tf_op jit(solution)/shard_map/ppermute | solution.py:362
  23.7 9.1 %collective-permute-done.4.refs_5_ = bf16[256,512]{1,0:T(8,128)(2,1)S(1)} collective-permute-done((bf16[256,512]{1,0:T(8,128)(2,1)S(1)}, bf16[256,512]{1,0:T(8,128)(2,1)S(1)}, u32[]{:S(2)}, u32[]{:S(2)}) %collective-permute-start.4) | collective-permute-done | bytes 262176 | tf_op jit(solution)/shard_map/ppermute | solution.py:362
  33.5 2.2 %collective-permute-start.17 = (bf16[256,512]{1,0:T(8,128)(2,1)}, bf16[256,512]{1,0:T(8,128)(2,1)S(1)}, u32[]{:S(2)}, u32[]{:S(2)}) collective-permute-start(bf16[256,512]{1,0:T(8,128)(2,1)} %get-tuple-element.79), channel_id=1, source_target_pairs={{0,3},{1,2},{2,1},{3,0},{4,7},{5,6},{6,5},{7,4},{8,11},{9,10},{10,... | collective-permute-start | bytes 786440 | tf_op jit(solution)/shard_map/ppermute | solution.py:362
  40.8 5.8 %shard_map.85 = (bf16[2048,512]{1,0:T(8,128)(2,1)S(1)}, bf16[128,512]{1,0:T(8,128)(2,1)S(1)}, bf16[128,512]{1,0:T(8,128)(2,1)S(1)}, f32[136,256]{1,0:T(8,128)S(1...) custom-call(s32[2]{0:T(128)S(1)} %pad_add_fusion.pos_ref, ...), custom_call_target="tpu_custom_call" | custom-call | tf_op jit(solution)/shard_map/pallas_call | solution.py:43
  51.2 2.6 %collective-permute-start.10 = (f32[136,256]{1,0:T(8,128)S(1)}, f32[136,256]{1,0:T(8,128)S(1)}, u32[]{:S(2)}, u32[]{:S(2)}) collective-permute-start(f32[136,256]{1,0:T(8,128)S(1)} %get-tuple-element.73), channel_id=1, source_target_pairs={{0,16},{1,17},{2,18},{3,19},{4,20},{5,21},{6,22},{7,23},{8,24},{9,... | collective-permute-start | bytes 417800 | tf_op jit(solution)/shard_map/ppermute | solution.py:362
  55.3 8.5 %collective-permute-done.10.refs_2_ = f32[136,256]{1,0:T(8,128)S(1)} collective-permute-done((f32[136,256]{1,0:T(8,128)S(1)}, f32[136,256]{1,0:T(8,128)S(1)}, u32[]{:S(2)}, u32[]{:S(2)}) %collective-permute-start.10) | collective-permute-done | bytes 139296 | tf_op jit(solution)/shard_map/ppermute | solution.py:362
  63.8 2.3 %collective-permute-start.7 = (bf16[128,512]{1,0:T(8,128)(2,1)S(1)}, bf16[128,512]{1,0:T(8,128)(2,1)S(1)}, u32[]{:S(2)}, u32[]{:S(2)}) collective-permute-start(bf16[128,512]{1,0:T(8,128)(2,1)S(1)} %get-tuple-element.69), channel_id=1, source_target_pairs={{0,8},{1,9},{2,10},{3,11},{4,12},{5,13},{6,14},{7,15},{8,16},{9,17... | collective-permute-start | bytes 393224 | tf_op jit(solution)/shard_map/ppermute | solution.py:369
  68.2 5.5 %collective-permute-start.14 = (bf16[128,256]{1,0:T(8,128)(2,1)S(1)}, bf16[128,256]{1,0:T(8,128)(2,1)S(1)}, u32[]{:S(2)}, u32[]{:S(2)}) collective-permute-start(bf16[128,256]{1,0:T(8,128)(2,1)S(1)} %get-tuple-element.75.refs_3_), channel_id=1, source_target_pairs={{0,24},{1,25},{2,26},{3,27},{4,28},{5,29},{6,30},{7,31},{8,16},{9,... | collective-permute-start | bytes 196616 | tf_op jit(solution)/shard_map/ppermute | solution.py:362
  74.4 3.6 %collective-permute-done.14.refs_6_ = bf16[128,256]{1,0:T(8,128)(2,1)S(1)} collective-permute-done((bf16[128,256]{1,0:T(8,128)(2,1)S(1)}, bf16[128,256]{1,0:T(8,128)(2,1)S(1)}, u32[]{:S(2)}, u32[]{:S(2)}) %collective-permute-start.14) | collective-permute-done | bytes 65568 | tf_op jit(solution)/shard_map/ppermute | solution.py:362
  79.7 15.1 %shard_map.88 = (bf16[256,256]{1,0:T(8,128)(2,1)S(1)}, bf16[256,256]{1,0:T(8,128)(2,1)S(1)}, bf16[256,256]{1,0:T(8,128)(2,1)S(1)}, bf16[256,256]{1,0:T(8,128)(2,...) custom-call(s32[2]{0:T(128)S(1)} %pad_add_fusion.pos_ref, ...), custom_call_target="tpu_custom_call" | custom-call | tf_op jit(solution)/shard_map/pallas_call | solution.py:43
  98.6 2.5 %collective-permute-start.33 = (bf16[128,256]{1,0:T(8,128)(2,1)S(1)}, bf16[128,256]{1,0:T(8,128)(2,1)S(1)}, u32[]{:S(2)}, u32[]{:S(2)}) collective-permute-start(bf16[128,256]{1,0:T(8,128)(2,1)S(1)} %get-tuple-element.100), channel_id=1, source_target_pairs={{0,24},{1,25},{2,26},{3,27},{4,28},{5,29},{6,30},{7,31},{8,16},{9,... | collective-permute-start | bytes 196616 | tf_op jit(solution)/shard_map/ppermute | solution.py:362
  102.3 3.3 %collective-permute-done.32.refs_3_ = bf16[128,256]{1,0:T(8,128)(2,1)S(1)} collective-permute-done((bf16[128,256]{1,0:T(8,128)(2,1)S(1)}, bf16[128,256]{1,0:T(8,128)(2,1)S(1)}, u32[]{:S(2)}, u32[]{:S(2)}) %collective-permute-start.32) | collective-permute-done | bytes 65568 | tf_op jit(solution)/shard_map/ppermute | solution.py:362
  107.9 3.4 %collective-permute-start.35 = (bf16[144,256]{1,0:T(8,128)(2,1)S(1)}, bf16[144,256]{1,0:T(8,128)(2,1)S(1)}, u32[]{:S(2)}, u32[]{:S(2)}) collective-permute-start(bf16[144,256]{1,0:T(8,128)(2,1)S(1)} %shard_map.90.refs_6_), channel_id=1, source_target_pairs={{0,16},{1,17},{2,18},{3,19},{4,20},{5,21},{6,22},{7,23},{8,24},{9,... | collective-permute-start | bytes 221192 | tf_op jit(solution)/shard_map/ppermute | solution.py:362
  116.8 7.2 %shard_map.91 = (bf16[256,512]{1,0:T(8,128)(2,1)S(1)}, bf16[256,512]{1,0:T(8,128)(2,1)S(1)}, bf16[256,512]{1,0:T(8,128)(2,1)S(1)}, bf16[256,512]{1,0:T(8,128)(2,...) custom-call(s32[2]{0:T(128)S(1)} %pad_add_fusion.pos_ref, ...), custom_call_target="tpu_custom_call" | custom-call | tf_op jit(solution)/shard_map/pallas_call | solution.py:43
  127.5 2.1 %collective-permute-start.46 = (f32[64,256]{1,0:T(8,128)S(1)}, f32[64,256]{1,0:T(8,128)S(1)}, u32[]{:S(2)}, u32[]{:S(2)}) collective-permute-start(f32[64,256]{1,0:T(8,128)S(1)} %get-tuple-element.115), channel_id=1, source_target_pairs={{0,24},{1,25},{2,26},{3,27},{4,28},{5,29},{6,30},{7,31},{8,16},{9,... | collective-permute-start | bytes 196616 | tf_op jit(solution)/shard_map/ppermute | solution.py:362
  134.5 6.0 %collective-permute-done.26.refs_5_ = bf16[256,256]{1,0:T(8,128)(2,1)S(1)} collective-permute-done((bf16[256,256]{1,0:T(8,128)(2,1)S(1)}, bf16[256,256]{1,0:T(8,128)(2,1)S(1)}, u32[]{:S(2)}, u32[]{:S(2)}) %collective-permute-start.26) | collective-permute-done | bytes 131104 | tf_op jit(solution)/shard_map/ppermute | solution.py:362
  141.3 2.5 %collective-permute-start.39 = (bf16[256,512]{1,0:T(8,128)(2,1)S(1)}, bf16[256,512]{1,0:T(8,128)(2,1)S(1)}, u32[]{:S(2)}, u32[]{:S(2)}) collective-permute-start(bf16[256,512]{1,0:T(8,128)(2,1)S(1)} %get-tuple-element.104), channel_id=1, source_target_pairs={{0,3},{1,2},{2,1},{3,0},{4,7},{5,6},{6,5},{7,4},{8,11},{9,10},{10,... | collective-permute-start | bytes 786440 | tf_op jit(solution)/shard_map/ppermute | solution.py:362
  143.7 2.7 %collective-permute-start.40 = (bf16[256,512]{1,0:T(8,128)(2,1)S(1)}, bf16[256,512]{1,0:T(8,128)(2,1)S(1)}, u32[]{:S(2)}, u32[]{:S(2)}) collective-permute-start(bf16[256,512]{1,0:T(8,128)(2,1)S(1)} %get-tuple-element.105), channel_id=1, source_target_pairs={{0,4},{1,5},{2,6},{3,7},{4,0},{5,1},{6,2},{7,3},{8,12},{9,13},{10,... | collective-permute-start | bytes 786440 | tf_op jit(solution)/shard_map/ppermute | solution.py:362
  147.1 5.2 %collective-permute-start.42 = (bf16[256,512]{1,0:T(8,128)(2,1)S(1)}, bf16[256,512]{1,0:T(8,128)(2,1)S(1)}, u32[]{:S(2)}, u32[]{:S(2)}) collective-permute-start(bf16[256,512]{1,0:T(8,128)(2,1)S(1)} %get-tuple-element.107), channel_id=1, source_target_pairs={{0,6},{1,7},{2,4},{3,5},{4,2},{5,3},{6,0},{7,1},{8,14},{9,15},{10,... | collective-permute-start | bytes 786440 | tf_op jit(solution)/shard_map/ppermute | solution.py:362
  154.5 9.9 %collective-permute-done.40.refs_4_ = bf16[256,512]{1,0:T(8,128)(2,1)S(1)} collective-permute-done((bf16[256,512]{1,0:T(8,128)(2,1)S(1)}, bf16[256,512]{1,0:T(8,128)(2,1)S(1)}, u32[]{:S(2)}, u32[]{:S(2)}) %collective-permute-start.40) | collective-permute-done | bytes 262176 | tf_op jit(solution)/shard_map/ppermute | solution.py:362
  164.4 5.7 %collective-permute-done.41.refs_5_ = bf16[256,512]{1,0:T(8,128)(2,1)S(1)} collective-permute-done((bf16[256,512]{1,0:T(8,128)(2,1)S(1)}, bf16[256,512]{1,0:T(8,128)(2,1)S(1)}, u32[]{:S(2)}, u32[]{:S(2)}) %collective-permute-start.41) | collective-permute-done | bytes 262176 | tf_op jit(solution)/shard_map/ppermute | solution.py:362
  170.1 2.5 %shard_map.92 = (bf16[256,2048]{1,0:T(8,128)(2,1)}, bf16[256,2048]{1,0:T(8,128)(2,1)}) custom-call(s32[2]{0:T(128)S(1)} %pad_add_fusion.pos_ref, bf16[256,512]{1,0:T(8,128)(2,1)S(1)} %get-tuple-element.101.refs_0_, bf16[256,512]{1,0:T(8,128)(2,1)S(1)} %collective-permute-done.37.refs_1_, bf16[256,512]{1,0:T(8,128)(2,1)S(1)} %collective-permute-done.38.refs_2_, ...), custom_call_target="tpu_custom_call" | custom-call | tf_op jit(solution)/shard_map/pallas_call | solution.py:43
  (120 shorter events, 56.8 us)
Async XLA Ops:
  8.0 13.1 %collective-permute-start.2 = (bf16[256,512]{1,0:T(8,128)(2,1)S(1)}, bf16[256,512]{1,0:T(8,128)(2,1)S(1)}, u32[]{:S(2)}, u32[]{:S(2)}) collective-permute-start(bf16[256,512]{1,0:T(8,128)(2,1)S(1)} %get-tuple-element.63), channel_id=1, source_target_pairs={{0,3},{1,2},{2,1},{3,0},{4,7},{5,6},{6,5},{7,4},{8,11},{9,10},{10,... | collective-permute-start | bytes 786440 | tf_op jit(solution)/shard_map/ppermute | solution.py:362
  8.2 14.3 %collective-permute-start.3 = (bf16[256,512]{1,0:T(8,128)(2,1)S(1)}, bf16[256,512]{1,0:T(8,128)(2,1)S(1)}, u32[]{:S(2)}, u32[]{:S(2)}) collective-permute-start(bf16[256,512]{1,0:T(8,128)(2,1)S(1)} %get-tuple-element.64), channel_id=1, source_target_pairs={{0,4},{1,5},{2,6},{3,7},{4,0},{5,1},{6,2},{7,3},{8,12},{9,13},{10,... | collective-permute-start | bytes 786440 | tf_op jit(solution)/shard_map/ppermute | solution.py:362
  9.9 22.9 %collective-permute-start.4 = (bf16[256,512]{1,0:T(8,128)(2,1)S(1)}, bf16[256,512]{1,0:T(8,128)(2,1)S(1)}, u32[]{:S(2)}, u32[]{:S(2)}) collective-permute-start(bf16[256,512]{1,0:T(8,128)(2,1)S(1)} %get-tuple-element.65), channel_id=1, source_target_pairs={{0,5},{1,4},{2,7},{3,6},{4,1},{5,0},{6,3},{7,2},{8,13},{9,12},{10,... | collective-permute-start | bytes 786440 | tf_op jit(solution)/shard_map/ppermute | solution.py:362
  9.9 25.7 %collective-permute-start.5 = (bf16[256,512]{1,0:T(8,128)(2,1)S(1)}, bf16[256,512]{1,0:T(8,128)(2,1)S(1)}, u32[]{:S(2)}, u32[]{:S(2)}) collective-permute-start(bf16[256,512]{1,0:T(8,128)(2,1)S(1)} %get-tuple-element.66), channel_id=1, source_target_pairs={{0,6},{1,7},{2,4},{3,5},{4,2},{5,3},{6,0},{7,1},{8,14},{9,15},{10,... | collective-permute-start | bytes 786440 | tf_op jit(solution)/shard_map/ppermute | solution.py:362
  15.2 22.7 %collective-permute-start.6 = (bf16[256,512]{1,0:T(8,128)(2,1)}, bf16[256,512]{1,0:T(8,128)(2,1)}, u32[]{:S(2)}, u32[]{:S(2)}) collective-permute-start(bf16[256,512]{1,0:T(8,128)(2,1)} %get-tuple-element.67), channel_id=1, source_target_pairs={{0,7},{1,6},{2,5},{3,4},{4,3},{5,2},{6,1},{7,0},{8,15},{9,14},{10,... | collective-permute-start | bytes 786440 | tf_op jit(solution)/shard_map/ppermute | solution.py:362
  21.1 27.2 %collective-permute-start.15 = (bf16[256,512]{1,0:T(8,128)(2,1)}, bf16[256,512]{1,0:T(8,128)(2,1)S(1)}, u32[]{:S(2)}, u32[]{:S(2)}) collective-permute-start(bf16[256,512]{1,0:T(8,128)(2,1)} %get-tuple-element.77), channel_id=1, source_target_pairs={{0,1},{1,0},{2,3},{3,2},{4,5},{5,4},{6,7},{7,6},{8,9},{9,8},{10,11... | collective-permute-start | bytes 786440 | tf_op jit(solution)/shard_map/ppermute | solution.py:362
  23.1 25.1 %collective-permute-start.16 = (bf16[256,512]{1,0:T(8,128)(2,1)}, bf16[256,512]{1,0:T(8,128)(2,1)S(1)}, u32[]{:S(2)}, u32[]{:S(2)}) collective-permute-start(bf16[256,512]{1,0:T(8,128)(2,1)} %get-tuple-element.78), channel_id=1, source_target_pairs={{0,2},{1,3},{2,0},{3,1},{4,6},{5,7},{6,4},{7,5},{8,10},{9,11},{10,... | collective-permute-start | bytes 786440 | tf_op jit(solution)/shard_map/ppermute | solution.py:362
  33.5 15.7 %collective-permute-start.17 = (bf16[256,512]{1,0:T(8,128)(2,1)}, bf16[256,512]{1,0:T(8,128)(2,1)S(1)}, u32[]{:S(2)}, u32[]{:S(2)}) collective-permute-start(bf16[256,512]{1,0:T(8,128)(2,1)} %get-tuple-element.79), channel_id=1, source_target_pairs={{0,3},{1,2},{2,1},{3,0},{4,7},{5,6},{6,5},{7,4},{8,11},{9,10},{10,... | collective-permute-start | bytes 786440 | tf_op jit(solution)/shard_map/ppermute | solution.py:362
  36.4 14.8 %collective-permute-start.18 = (bf16[256,512]{1,0:T(8,128)(2,1)}, bf16[256,512]{1,0:T(8,128)(2,1)S(1)}, u32[]{:S(2)}, u32[]{:S(2)}) collective-permute-start(bf16[256,512]{1,0:T(8,128)(2,1)} %get-tuple-element.80), channel_id=1, source_target_pairs={{0,4},{1,5},{2,6},{3,7},{4,0},{5,1},{6,2},{7,3},{8,12},{9,13},{10,... | collective-permute-start | bytes 786440 | tf_op jit(solution)/shard_map/ppermute | solution.py:362
  48.3 19.9 %collective-permute-start.19 = (bf16[256,512]{1,0:T(8,128)(2,1)S(1)}, bf16[256,512]{1,0:T(8,128)(2,1)S(1)}, u32[]{:S(2)}, u32[]{:S(2)}) collective-permute-start(bf16[256,512]{1,0:T(8,128)(2,1)S(1)} %copy-done.16), channel_id=1, source_target_pairs={{0,5},{1,4},{2,7},{3,6},{4,1},{5,0},{6,3},{7,2},{8,13},{9,12},{10,... | collective-permute-start | bytes 786440 | tf_op jit(solution)/shard_map/ppermute | solution.py:362
  48.3 25.4 %collective-permute-start.20 = (bf16[256,512]{1,0:T(8,128)(2,1)S(1)}, bf16[256,512]{1,0:T(8,128)(2,1)S(1)}, u32[]{:S(2)}, u32[]{:S(2)}) collective-permute-start(bf16[256,512]{1,0:T(8,128)(2,1)S(1)} %copy-done.14), channel_id=1, source_target_pairs={{0,6},{1,7},{2,4},{3,5},{4,2},{5,3},{6,0},{7,1},{8,14},{9,15},{10,... | collective-permute-start | bytes 786440 | tf_op jit(solution)/shard_map/ppermute | solution.py:362
  49.2 24.5 %collective-permute-start.21 = (bf16[256,512]{1,0:T(8,128)(2,1)S(1)}, bf16[256,512]{1,0:T(8,128)(2,1)S(1)}, u32[]{:S(2)}, u32[]{:S(2)}) collective-permute-start(bf16[256,512]{1,0:T(8,128)(2,1)S(1)} %copy-done.12), channel_id=1, source_target_pairs={{0,7},{1,6},{2,5},{3,4},{4,3},{5,2},{6,1},{7,0},{8,15},{9,14},{10,... | collective-permute-start | bytes 786440 | tf_op jit(solution)/shard_map/ppermute | solution.py:362
  94.8 16.6 %collective-permute-start.29 = (bf16[128,512]{1,0:T(8,128)(2,1)S(1)}, bf16[128,512]{1,0:T(8,128)(2,1)S(1)}, u32[]{:S(2)}, u32[]{:S(2)}) collective-permute-start(bf16[128,512]{1,0:T(8,128)(2,1)S(1)} %get-tuple-element.94), channel_id=1, source_target_pairs={{0,8},{1,9},{2,10},{3,11},{4,12},{5,13},{6,14},{7,15},{8,16},{9,17... | collective-permute-start | bytes 393224 | tf_op jit(solution)/shard_map/ppermute | solution.py:369
  111.3 14.3 %collective-permute-start.22 = (bf16[256,256]{1,0:T(8,128)(2,1)S(1)}, bf16[256,256]{1,0:T(8,128)(2,1)S(1)}, u32[]{:S(2)}, u32[]{:S(2)}) collective-permute-start(bf16[256,256]{1,0:T(8,128)(2,1)S(1)} %get-tuple-element.85), channel_id=1, source_target_pairs={{0,1},{1,0},{2,3},{3,2},{4,5},{5,4},{6,7},{7,6},{8,9},{9,8},{10,11... | collective-permute-start | bytes 393224 | tf_op jit(solution)/shard_map/ppermute | solution.py:362
  111.4 16.1 %collective-permute-start.23 = (bf16[256,256]{1,0:T(8,128)(2,1)S(1)}, bf16[256,256]{1,0:T(8,128)(2,1)S(1)}, u32[]{:S(2)}, u32[]{:S(2)}) collective-permute-start(bf16[256,256]{1,0:T(8,128)(2,1)S(1)} %get-tuple-element.86), channel_id=1, source_target_pairs={{0,2},{1,3},{2,0},{3,1},{4,6},{5,7},{6,4},{7,5},{8,10},{9,11},{10,... | collective-permute-start | bytes 393224 | tf_op jit(solution)/shard_map/ppermute | solution.py:362
  112.5 17.1 %collective-permute-start.24 = (bf16[256,256]{1,0:T(8,128)(2,1)S(1)}, bf16[256,256]{1,0:T(8,128)(2,1)S(1)}, u32[]{:S(2)}, u32[]{:S(2)}) collective-permute-start(bf16[256,256]{1,0:T(8,128)(2,1)S(1)} %get-tuple-element.87), channel_id=1, source_target_pairs={{0,3},{1,2},{2,1},{3,0},{4,7},{5,6},{6,5},{7,4},{8,11},{9,10},{10,... | collective-permute-start | bytes 393224 | tf_op jit(solution)/shard_map/ppermute | solution.py:362
  115.4 14.2 %collective-permute-start.25 = (bf16[256,256]{1,0:T(8,128)(2,1)S(1)}, bf16[256,256]{1,0:T(8,128)(2,1)S(1)}, u32[]{:S(2)}, u32[]{:S(2)}) collective-permute-start(bf16[256,256]{1,0:T(8,128)(2,1)S(1)} %get-tuple-element.88), channel_id=1, source_target_pairs={{0,4},{1,5},{2,6},{3,7},{4,0},{5,1},{6,2},{7,3},{8,12},{9,13},{10,... | collective-permute-start | bytes 393224 | tf_op jit(solution)/shard_map/ppermute | solution.py:362
  133.0 14.1 %collective-permute-start.37 = (bf16[256,512]{1,0:T(8,128)(2,1)S(1)}, bf16[256,512]{1,0:T(8,128)(2,1)S(1)}, u32[]{:S(2)}, u32[]{:S(2)}) collective-permute-start(bf16[256,512]{1,0:T(8,128)(2,1)S(1)} %get-tuple-element.102), channel_id=1, source_target_pairs={{0,1},{1,0},{2,3},{3,2},{4,5},{5,4},{6,7},{7,6},{8,9},{9,8},{10,11... | collective-permute-start | bytes 786440 | tf_op jit(solution)/shard_map/ppermute | solution.py:362
  133.6 18.7 %collective-permute-start.38 = (bf16[256,512]{1,0:T(8,128)(2,1)S(1)}, bf16[256,512]{1,0:T(8,128)(2,1)S(1)}, u32[]{:S(2)}, u32[]{:S(2)}) collective-permute-start(bf16[256,512]{1,0:T(8,128)(2,1)S(1)} %get-tuple-element.103), channel_id=1, source_target_pairs={{0,2},{1,3},{2,0},{3,1},{4,6},{5,7},{6,4},{7,5},{8,10},{9,11},{10,... | collective-permute-start | bytes 786440 | tf_op jit(solution)/shard_map/ppermute | solution.py:362
  141.3 13.2 %collective-permute-start.39 = (bf16[256,512]{1,0:T(8,128)(2,1)S(1)}, bf16[256,512]{1,0:T(8,128)(2,1)S(1)}, u32[]{:S(2)}, u32[]{:S(2)}) collective-permute-start(bf16[256,512]{1,0:T(8,128)(2,1)S(1)} %get-tuple-element.104), channel_id=1, source_target_pairs={{0,3},{1,2},{2,1},{3,0},{4,7},{5,6},{6,5},{7,4},{8,11},{9,10},{10,... | collective-permute-start | bytes 786440 | tf_op jit(solution)/shard_map/ppermute | solution.py:362
  143.7 20.7 %collective-permute-start.40 = (bf16[256,512]{1,0:T(8,128)(2,1)S(1)}, bf16[256,512]{1,0:T(8,128)(2,1)S(1)}, u32[]{:S(2)}, u32[]{:S(2)}) collective-permute-start(bf16[256,512]{1,0:T(8,128)(2,1)S(1)} %get-tuple-element.105), channel_id=1, source_target_pairs={{0,4},{1,5},{2,6},{3,7},{4,0},{5,1},{6,2},{7,3},{8,12},{9,13},{10,... | collective-permute-start | bytes 786440 | tf_op jit(solution)/shard_map/ppermute | solution.py:362
  146.5 23.6 %collective-permute-start.41 = (bf16[256,512]{1,0:T(8,128)(2,1)S(1)}, bf16[256,512]{1,0:T(8,128)(2,1)S(1)}, u32[]{:S(2)}, u32[]{:S(2)}) collective-permute-start(bf16[256,512]{1,0:T(8,128)(2,1)S(1)} %get-tuple-element.106), channel_id=1, source_target_pairs={{0,5},{1,4},{2,7},{3,6},{4,1},{5,0},{6,3},{7,2},{8,13},{9,12},{10,... | collective-permute-start | bytes 786440 | tf_op jit(solution)/shard_map/ppermute | solution.py:362
  147.1 23.0 %collective-permute-start.42 = (bf16[256,512]{1,0:T(8,128)(2,1)S(1)}, bf16[256,512]{1,0:T(8,128)(2,1)S(1)}, u32[]{:S(2)}, u32[]{:S(2)}) collective-permute-start(bf16[256,512]{1,0:T(8,128)(2,1)S(1)} %get-tuple-element.107), channel_id=1, source_target_pairs={{0,6},{1,7},{2,4},{3,5},{4,2},{5,3},{6,0},{7,1},{8,14},{9,15},{10,... | collective-permute-start | bytes 786440 | tf_op jit(solution)/shard_map/ppermute | solution.py:362
  152.3 17.8 %collective-permute-start.43 = (bf16[256,512]{1,0:T(8,128)(2,1)S(1)}, bf16[256,512]{1,0:T(8,128)(2,1)S(1)}, u32[]{:S(2)}, u32[]{:S(2)}) collective-permute-start(bf16[256,512]{1,0:T(8,128)(2,1)S(1)} %get-tuple-element.108), channel_id=1, source_target_pairs={{0,7},{1,6},{2,5},{3,4},{4,3},{5,2},{6,1},{7,0},{8,15},{9,14},{10,... | collective-permute-start | bytes 786440 | tf_op jit(solution)/shard_map/ppermute | solution.py:362
  (41 other events, 297.7 us)
where the time goes:
time: 174 us; the launch traced here: 173 us
  starting transfers between devices  69.5 us (40%)
  waiting for transfers between devices  54 us (31%)
  Pallas kernels  38.5 us (22%)
  local copies, waits for them, and re-layouts  10.3 us (6%)
    ppermute x43, starting transfers between devices, exchange(): out.append(lax.ppermute(fields[k], 'seq', flip))  62.2 us
    ppermute x43, waiting for transfers between devices, exchange(): out.append(lax.ppermute(fields[k], 'seq', flip))  54 us
    pallas_call x10, Pallas kernels, call(): pl.pallas_call(kernel, in_specs=[pl.BlockSpec(memory_space=pltpu.SMEM)] +...  38.5 us
    unnamed x35, local copies, waits for them, and re-layouts  10.3 us
    ppermute x2, starting transfers between devices, swap_edges(): lax.ppermute(upward, 'seq', up)  4.08 us
  transfers between devices with their start and end apart: 48, of which 12 were waited for; matrix products, arithmetic and copies ran while one was open for 0% of the time, Pallas kernels for 11%

commit v1 on v0

v1 whole, which is shorter than its diff:
```python
import math

import jax
import jax.numpy as jnp
from jax import lax
from jax.experimental import pallas as pl
from jax.experimental.pallas import tpu as pltpu
from jax.sharding import PartitionSpec as P


SEG = 256
STAT_ROWS = 8
DOT_ROWS = 16
HIDDEN = -1e30
HEADS_PER_DEVICE = 2
BF = jnp.bfloat16
FL = jnp.float32


def dot_nn(a, b):
    return lax.dot_general(a, b, (((1,), (0,)), ((), ())), preferred_element_type=FL)


def dot_nt(a, b):
    return lax.dot_general(a, b, (((1,), (1,)), ((), ())), preferred_element_type=FL)


def dot_tn(a, b):
    return lax.dot_general(a, b, (((0,), (0,)), ((), ())), preferred_element_type=FL)


def struct(shape, dtype):
    return jax.ShapeDtypeStruct(shape, dtype)


def size_of(x):
    dtype = jnp.dtype(x.dtype)
    return math.prod(x.shape) * dtype.itemsize


def call(kernel, pos, ins, outs, scratch=(), spare=4, copies=0, far=""):
    near = pl.BlockSpec(memory_space=pltpu.VMEM)
    hbm = pl.BlockSpec(memory_space=pltpu.HBM)
    if copies:
        scratch = [pltpu.SemaphoreType.DMA((copies,))]
        need = sum(size_of(x) for x in (ins if far == "outs" else outs))
    else:
        need = sum(size_of(x) for x in (*ins, *outs, *scratch))
    if far == "ins":
        ins = [pltpu.with_memory_space_constraint(x, pltpu.HBM) for x in ins]
    return pl.pallas_call(
        kernel,
        in_specs=[pl.BlockSpec(memory_space=pltpu.SMEM)]
        + [hbm if far == "ins" else near] * len(ins),
        out_specs=[hbm if far == "outs" else near] * len(outs),
        out_shape=list(outs),
        scratch_shapes=list(scratch),
        compiler_params=pltpu.CompilerParams(vmem_limit_bytes=need + spare * 2**20),
    )(pos, *ins)


class Plan:
    def __init__(self, devices, tokens_here, head_count, head_size, rank):
        self.inner = math.gcd(head_count // HEADS_PER_DEVICE, devices)
        self.outer = devices // self.inner
        self.heads = head_count // self.inner
        self.tokens = tokens_here
        self.group = tokens_here * self.inner
        self.head_size = head_size
        self.rank = rank
        self.pair = 2 * head_size
        self.width = self.heads * self.pair
        self.rows = rank // self.outer
        self.margin = SEG // 2
        self.scale = head_size ** (-0.5)


def run_copies(sems, moves):
    copies = [pltpu.make_async_copy(a, b, sems.at[i]) for i, (a, b) in enumerate(moves)]
    for copy in copies:
        copy.start()
    for copy in copies:
        copy.wait()


def head_slices(plan, other, h):
    return pl.ds(pl.multiple_of((other * plan.heads + h) * plan.head_size, plan.head_size), plan.head_size)


def pack_kernel(plan, pos, a_ref, b_ref, *refs):
    outs, sems = refs[:-1], refs[-1]
    hd = plan.head_size
    moves = []
    for k, out in enumerate(outs):
        for h in range(plan.heads):
            cols = head_slices(plan, pos[1] ^ k, h)
            moves.append((a_ref.at[:, cols], out.at[:, pl.ds(2 * h * hd, hd)]))
            moves.append((b_ref.at[:, cols], out.at[:, pl.ds((2 * h + 1) * hd, hd)]))
    run_copies(sems, moves)


def unpack_pair_kernel(plan, pos, *refs):
    ins, proj_ref, (a_ref, b_ref, out_ref, sems) = refs[: plan.inner], refs[plan.inner], refs[plan.inner + 1 :]
    hd = plan.head_size
    moves = [(proj_ref, out_ref)]
    for k, src in enumerate(ins):
        for h in range(plan.heads):
            cols = head_slices(plan, pos[1] ^ k, h)
            moves.append((src.at[:, pl.ds(2 * h * hd, hd)], a_ref.at[:, cols]))
            moves.append((src.at[:, pl.ds((2 * h + 1) * hd, hd)], b_ref.at[:, cols]))
    run_copies(sems, moves)


def unpack_kernel(plan, pos, *refs):
    ins, a_ref, sems = refs[: plan.inner], refs[plan.inner], refs[plan.inner + 1]
    wide = plan.heads * plan.head_size
    moves = []
    for k, src in enumerate(ins):
        cols = pl.ds(pl.multiple_of((pos[1] ^ k) * wide, wide), wide)
        moves.append((src, a_ref.at[:, cols]))
    run_copies(sems, moves)


def column_of(mask, row):
    return jnp.sum(jnp.where(mask, row, 0.0), axis=1, keepdims=True)


def head_part(plan, h, pieces, w_ref, logit_ref, expo_ref, floor):
    hd, pair, rank, tokens = plan.head_size, plan.pair, plan.rank, plan.tokens
    top = jnp.broadcast_to(floor, (8, rank))
    for i, src in enumerate(pieces):
        block = dot_nn(src[:, h * pair : h * pair + hd], w_ref[h])
        logit_ref[i * tokens : (i + 1) * tokens, :] = block
        top = jnp.maximum(top, jnp.max(block.reshape(tokens // 8, 8, rank), axis=0))
    top = jnp.max(top, axis=0, keepdims=True)

    def expo_step(i, total):
        at = pl.multiple_of(i * SEG, SEG)
        block = jnp.exp(logit_ref[pl.ds(at, SEG), :] - top)
        expo_ref[pl.ds(at, SEG), :] = block.astype(BF)
        return total + jnp.sum(block.reshape(SEG // 8, 8, rank), axis=0)

    steps = len(pieces) * tokens // SEG
    total = lax.fori_loop(0, steps, expo_step, jnp.zeros((8, rank), FL))
    both = jnp.concatenate([src[:, h * pair : (h + 1) * pair] for src in pieces], axis=0)
    return top, jnp.sum(total, axis=0, keepdims=True), dot_tn(expo_ref[...], both)


def stats_early_kernel(plan, pos, *refs):
    pieces, (w_ref, part_ref, stat_ref, logit_ref, expo_ref) = refs[:-5], refs[-5:]
    heads = plan.heads
    stat_ref[2 * heads :, :] = jnp.zeros((STAT_ROWS - 2 * heads, plan.rank), FL)
    floor = jnp.full((1, plan.rank), -jnp.inf, FL)
    for h in range(heads):
        top, total, part = head_part(plan, h, pieces, w_ref, logit_ref, expo_ref, floor)
        stat_ref[h : h + 1, :] = top
        stat_ref[heads + h : heads + h + 1, :] = total
        part_ref[h] = part


def stats_late_kernel(plan, pos, *refs):
    inner, outer, heads, rank, rows = plan.inner, plan.outer, plan.heads, plan.rank, plan.rows
    pieces, (w_ref, old_ref, old_stat_ref, first_ref, last_ref), refs = (
        refs[:inner],
        refs[inner : inner + 5],
        refs[inner + 5 :],
    )
    outs, (logit_ref, expo_ref, part_ref) = refs[:outer], refs[outer:]
    for k, src in enumerate(pieces):

        @pl.when(pos[1] == k)
        def _():
            first_ref[...] = src[: plan.margin, :]

        @pl.when((pos[1] ^ k) == inner - 1)
        def _():
            last_ref[...] = src[plan.tokens - plan.margin :, :]

    same = lax.broadcasted_iota(jnp.int32, (rank, rank), 0) == lax.broadcasted_iota(
        jnp.int32, (rank, rank), 1
    )
    tops, totals = [], []
    for h in range(heads):
        old_top = old_stat_ref[h : h + 1, :]
        top, total, part = head_part(
            plan, h, pieces[late_from(inner) :], w_ref, logit_ref, expo_ref, old_top
        )
        weight = jnp.exp(old_top - top)
        tops.append(top)
        totals.append(total + weight * old_stat_ref[heads + h : heads + h + 1, :])
        part_ref[h] = part + old_ref[h] * column_of(same, weight)
    stats = jnp.concatenate(
        tops + totals + [jnp.zeros((STAT_ROWS - 2 * heads, rank), FL)], axis=0
    )
    for k, out in enumerate(outs):
        row = pl.multiple_of((pos[0] ^ k) * rows, rows)
        for h in range(heads):
            out[h * rows : (h + 1) * rows, :] = part_ref[h, pl.ds(row, rows), :]
        out[heads * rows :, :] = stats


def late_from(inner):
    return inner // 2 + 1


def own_columns(plan, pos):
    row_at = lax.broadcasted_iota(jnp.int32, (plan.rows, plan.rank), 0)
    col_at = lax.broadcasted_iota(jnp.int32, (plan.rows, plan.rank), 1)
    return col_at == row_at + pos[0] * plan.rows


def combine_kernel(plan, pos, *refs):
    ins, (full_ref, half_ref, stat_ref) = refs[: plan.outer], refs[plan.outer :]
    heads, rows = plan.heads, plan.rows
    own = own_columns(plan, pos)
    stats = [r[heads * rows :, :] for r in ins]
    stat_ref[2 * heads :, :] = jnp.zeros((STAT_ROWS - 2 * heads, plan.rank), FL)
    for h in range(heads):
        tops = [stat[h : h + 1, :] for stat in stats]
        top = tops[0]
        for t in tops[1:]:
            top = jnp.maximum(top, t)
        weights = [jnp.exp(t - top) for t in tops]
        total = weights[0] * stats[0][heads + h : heads + h + 1, :]
        for w, stat in zip(weights[1:], stats[1:]):
            total = total + w * stat[heads + h : heads + h + 1, :]
        inverse = 1.0 / total
        stat_ref[h : h + 1, :] = top
        stat_ref[heads + h : heads + h + 1, :] = inverse
        here = slice(h * rows, (h + 1) * rows)
        result = ins[0][here, :] * column_of(own, weights[0])
        for w, r in zip(weights[1:], ins[1:]):
            result = result + r[here, :] * column_of(own, w)
        result = result * column_of(own, inverse)
        full_ref[here, :] = result
        half_ref[here, :] = result.astype(BF)


def attend_kernel(plan, total_groups, pos, *refs):
    outer, inner, heads = plan.outer, plan.inner, plan.heads
    kv_refs, (before_ref, after_ref), refs = refs[:inner], refs[inner : inner + 2], refs[inner + 2 :]
    bars, qg, refs = refs[:outer], refs[outer : outer + inner], refs[outer + inner :]
    dq_outs, bar_outs, refs = refs[:inner], refs[inner : inner + outer], refs[inner + outer :]
    acc_ref, wg_before_ref, wg_after_ref, ext_ref, bar_ref, q_ref, dbar_ref, dq_ref = refs
    hd, pair, rank, margin, group = plan.head_size, plan.pair, plan.rank, plan.margin, plan.group
    rows = plan.rows
    ext_ref[:margin, :] = before_ref[...]
    for k, src in enumerate(kv_refs):
        row = pl.multiple_of((pos[1] ^ k) * plan.tokens + margin, margin)
        ext_ref[pl.ds(row, plan.tokens), :] = src[...]
    ext_ref[margin + group :, :] = after_ref[...]
    for k, src in enumerate(bars):
        row = pl.multiple_of((pos[0] ^ k) * rows, rows)
        for h in range(heads):
            bar_ref[h, pl.ds(row, rows), :] = src[h * rows : (h + 1) * rows, :]
    for k, src in enumerate(qg):
        row = pl.multiple_of((pos[1] ^ k) * plan.tokens, plan.tokens)
        q_ref[pl.ds(row, plan.tokens), :] = src[...]
    acc_ref[:SEG, :] = jnp.zeros((SEG, plan.width), FL)
    dbar_ref[...] = jnp.zeros(dbar_ref.shape, FL)
    segs = group // SEG
    at_start = pos[0] == 0
    at_end = pos[0] == total_groups - 1
    factor = plan.scale / math.log(2.0)

    def step(j, carry):
        row = pl.multiple_of(j * SEG, SEG)
        hide_low = jnp.where(jnp.logical_and(at_start, j == 0), HIDDEN, 0.0)
        hide_high = jnp.where(jnp.logical_and(at_end, j == segs - 1), HIDDEN, 0.0)
        loaded, scored = [], []
        for h in range(heads):
            low, mid, high = h * pair, h * pair + hd, (h + 1) * pair
            key = jnp.concatenate([bar_ref[h, :, :hd], ext_ref[pl.ds(row, 2 * SEG), low:mid]], axis=0)
            val = jnp.concatenate([bar_ref[h, :, hd:], ext_ref[pl.ds(row, 2 * SEG), mid:high]], axis=0)
            query = q_ref[pl.ds(row, SEG), low:mid]
            grad = q_ref[pl.ds(row, SEG), mid:high]
            loaded.append((key, query, grad))
            scored.append((dot_nt(key, query), dot_nt(val, grad)))
        for h in range(heads):
            low, mid, high = h * pair, h * pair + hd, (h + 1) * pair
            key, query, grad = loaded[h]
            scores, dprob = scored[h]
            scores = jnp.concatenate(
                [
                    scores[:rank],
                    scores[rank : rank + margin] + hide_low,
                    scores[rank + margin : rank + 2 * SEG - margin],
                    scores[rank + 2 * SEG - margin :] + hide_high,
                ],
                axis=0,
            )
            expo = jnp.exp2((scores - jnp.max(scores, axis=0, keepdims=True)) * factor)
            prob = expo * (1.0 / jnp.sum(expo, axis=0, keepdims=True))
            prob_b = prob.astype(BF)
            row_dot = jnp.sum(prob_b.astype(FL) * dprob, axis=0, keepdims=True)
            dscore = (prob * (dprob - row_dot)).astype(BF)
            dquery = dot_tn(key, dscore) * plan.scale
            dq_ref[pl.ds(row, SEG), h * hd : (h + 1) * hd] = jnp.transpose(dquery).astype(BF)
            dkey = dot_nn(dscore, query)
            dval = dot_nn(prob_b, grad)
            dbar_ref[h, :, :hd] += dkey[:rank, :]
            dbar_ref[h, :, hd:] += dval[:rank, :]
            new = pl.multiple_of(row + SEG, SEG)
            acc_ref[pl.ds(row, SEG), low:mid] += dkey[rank : rank + SEG, :]
            acc_ref[pl.ds(row, SEG), mid:high] += dval[rank : rank + SEG, :]
            acc_ref[pl.ds(new, SEG), low:mid] = dkey[rank + SEG :, :]
            acc_ref[pl.ds(new, SEG), mid:high] = dval[rank + SEG :, :]
        return carry

    lax.fori_loop(0, segs, step, 0)
    for h in range(heads):
        low, mid, high = h * pair, h * pair + hd, (h + 1) * pair
        dbar_ref[h, :, :hd] = dbar_ref[h, :, :hd] * plan.scale
        wg_before_ref[:, low:mid] = (acc_ref[:margin, low:mid] * plan.scale).astype(BF)
        wg_before_ref[:, mid:high] = acc_ref[:margin, mid:high].astype(BF)
        wg_after_ref[:, low:mid] = (acc_ref[margin + group :, low:mid] * plan.scale).astype(BF)
        wg_after_ref[:, mid:high] = acc_ref[margin + group :, mid:high].astype(BF)
    for k, out in enumerate(dq_outs):
        row = pl.multiple_of((pos[1] ^ k) * plan.tokens, plan.tokens)
        out[...] = dq_ref[pl.ds(row, plan.tokens), :]
    for k, out in enumerate(bar_outs):
        row = pl.multiple_of((pos[0] ^ k) * rows, rows)
        for h in range(heads):
            out[h * rows : (h + 1) * rows, :] = dbar_ref[h, pl.ds(row, rows), :].astype(BF)


def combine_grad_kernel(plan, pos, *refs):
    full_ref, ins = refs[0], refs[1 : 1 + plan.outer]
    out_ref = refs[1 + plan.outer]
    heads, rows = plan.heads, plan.rows
    total = ins[0][...].astype(FL)
    for r in ins[1:]:
        total = total + r[...].astype(FL)
    half = total.astype(BF)
    out_ref[: heads * rows, :] = half
    column = jnp.sum(full_ref[...] * half.astype(FL), axis=1, keepdims=True)
    own = own_columns(plan, pos)
    parts = []
    for h in range(heads):
        rest = jnp.sum(jnp.where(own, column[h * rows : (h + 1) * rows, :], 0.0), axis=0, keepdims=True)
        for _ in range(3):
            part = rest.astype(BF).astype(FL)
            parts.append(part)
            rest = rest - part
    parts.append(jnp.zeros((DOT_ROWS - 3 * heads, plan.rank), FL))
    out_ref[heads * rows :, :] = jnp.concatenate(parts, axis=0).astype(BF)


def finish_kernel(plan, wave, pos, *refs):
    outer, heads, count = plan.outer, plan.heads, len(wave)
    kv_refs, refs = refs[:count], refs[count:]
    w_ref, stat_ref, wg_ref, before_ref, after_ref = refs[:5]
    bars, refs = refs[5 : 5 + outer], refs[5 + outer :]
    outs, (logit_grad_ref, bar_ref, sum_ref) = refs[:count], refs[count:]
    hd, pair, rank, margin, rows = plan.head_size, plan.pair, plan.rank, plan.margin, plan.rows
    dots = [jnp.zeros((1, rank), FL)] * heads
    for k, src in enumerate(bars):
        row = pl.multiple_of((pos[0] ^ k) * rows, rows)
        sent = src[heads * rows :, :].astype(FL)
        for h in range(heads):
            bar_ref[h, pl.ds(row, rows), :] = src[h * rows : (h + 1) * rows, :]
            dots[h] = dots[h] + jnp.sum(sent[3 * h : 3 * h + 3, :], axis=0, keepdims=True)
    subs = plan.tokens // SEG
    for i, k in enumerate(wave):
        piece_at = pos[1] ^ k
        for sub in range(subs):
            here = slice(sub * SEG, (sub + 1) * SEG)
            from_row = pl.multiple_of(piece_at * plan.tokens + sub * SEG + margin, margin)
            for h in range(heads):
                low, mid, high = h * pair, h * pair + hd, (h + 1) * pair
                both = kv_refs[i][here, low:high]
                dbar = bar_ref[h]
                top = stat_ref[h : h + 1, :]
                inverse = stat_ref[heads + h : heads + h + 1, :]
                expo = jnp.exp(dot_nn(both[:, :hd], w_ref[h]) - top).astype(BF).astype(FL)
                prob = expo * inverse
                dprob = dot_nt(both, dbar)
                logit_grad = (prob * (dprob - dots[h])).astype(BF)
                lines = slice(i * plan.tokens + sub * SEG, i * plan.tokens + (sub + 1) * SEG)
                logit_grad_ref[lines, h * rank : (h + 1) * rank] = logit_grad
                from_prob = dot_nn(prob.astype(BF), dbar)
                window_key = wg_ref[pl.ds(from_row, SEG), low:mid] * plan.scale
                sum_ref[h, :, :hd] = from_prob[:, :hd] + window_key + dot_nt(logit_grad, w_ref[h])
                sum_ref[h, :, hd:] = from_prob[:, hd:] + wg_ref[pl.ds(from_row, SEG), mid:high]
            if sub == 0:

                @pl.when(piece_at == 0)
                def _():
                    for h in range(heads):
                        edge = before_ref[:, h * pair : (h + 1) * pair]
                        sum_ref[h, :margin, :] += edge.astype(FL)

            if sub == subs - 1:

                @pl.when(piece_at == plan.inner - 1)
                def _():
                    for h in range(heads):
                        edge = after_ref[:, h * pair : (h + 1) * pair]
                        sum_ref[h, SEG - margin :, :] += edge.astype(FL)

            for h in range(heads):
                outs[i][here, h * pair : (h + 1) * pair] = sum_ref[h].astype(BF)


def proj_kernel(plan, waves, pos, *refs):
    heads, hd, pair, rank = plan.heads, plan.head_size, plan.pair, plan.rank
    kv_refs, refs = refs[: plan.inner], refs[plan.inner :]
    grad_refs, refs = refs[: len(waves)], refs[len(waves) :]
    outs, proj_ref = refs[: plan.outer], refs[plan.outer]
    for h in range(heads):
        total = jnp.zeros((hd, rank), FL)
        for wave, grad_ref in zip(waves, grad_refs):
            key = jnp.concatenate([kv_refs[k][:, h * pair : h * pair + hd] for k in wave], axis=0)
            total = total + dot_tn(key, grad_ref[:, h * rank : (h + 1) * rank])
        proj_ref[h * hd : (h + 1) * hd, :] = total
    piece = heads * hd // plan.outer
    for k, out in enumerate(outs):
        row = pl.multiple_of((pos[0] ^ k) * piece, piece)
        out[...] = proj_ref[pl.ds(row, piece), :]


def finish_waves(inner):
    quarter = inner // 4
    return (
        tuple(range(inner - quarter, inner)),
        tuple(range(quarter, inner - quarter)),
        tuple(range(quarter)),
    )


def put(items, which, values):
    for k, value in zip(which, values):
        items[k] = value


def exchange(fields, devices, stride, which=None):
    out = []
    for k, field in zip(which or range(len(fields)), fields):
        flip = [(i, i ^ (k * stride)) for i in range(devices)]
        out.append(lax.ppermute(field, "seq", flip) if k else field)
    return out


def swap_edges(upward, downward, devices, stride):
    up = [(i, i + stride) for i in range(devices - stride)]
    down = [(j, i) for i, j in up]
    return lax.ppermute(upward, "seq", up), lax.ppermute(downward, "seq", down)


def per_device(queries, keys, values, grad_out, proj_weight):
    tokens_here, row_width = queries.shape
    head_count, head_size, rank = proj_weight.shape
    devices = lax.axis_size("seq")
    plan = Plan(devices, tokens_here, head_count, head_size, rank)
    inner, outer, heads = plan.inner, plan.outer, plan.heads
    group, width, rows, margin = plan.group, plan.width, plan.rows, plan.margin
    me = lax.axis_index("seq")
    pos = jnp.stack([me // inner, me % inner]).astype(jnp.int32)

    def bind(kernel, *more):
        return lambda pos_ref, *refs: kernel(plan, *more, pos_ref, *refs)

    weight = lax.dynamic_slice_in_dim(proj_weight, (me % inner) * heads, heads, axis=0)
    pair = plan.pair
    piece = struct((tokens_here, width), BF)

    waves = finish_waves(inner)

    def pack(first, second):
        return call(
            bind(pack_kernel),
            pos,
            [first, second],
            [piece] * inner,
            copies=2 * inner * heads,
            far="ins",
        )

    kv_pieces = exchange(pack(keys, values), devices, 1)
    qg_pieces = exchange(pack(queries, grad_out), devices, 1)

    early = late_from(inner)
    old_part, old_stat = call(
        bind(stats_early_kernel),
        pos,
        [*kv_pieces[:early], weight],
        [struct((heads, rank, pair), FL), struct((STAT_ROWS, rank), FL)],
        [pltpu.VMEM((early * tokens_here, rank), FL), pltpu.VMEM((early * tokens_here, rank), BF)],
    )
    late = inner - early
    kv_first, kv_last, *part_send = call(
        bind(stats_late_kernel),
        pos,
        [*kv_pieces, weight, old_part, old_stat],
        [struct((margin, width), BF)] * 2
        + [struct((heads * rows + STAT_ROWS, pair), FL)] * outer,
        [
            pltpu.VMEM((late * tokens_here, rank), FL),
            pltpu.VMEM((late * tokens_here, rank), BF),
            pltpu.VMEM((heads, rank, pair), FL),
        ],
    )
    parts = exchange(part_send, devices, inner)
    kv_before, kv_after = swap_edges(kv_last, kv_first, devices, inner)
    bar_full, bar_half, stats = call(
        bind(combine_kernel),
        pos,
        parts,
        [
            struct((heads * rows, pair), FL),
            struct((heads * rows, pair), BF),
            struct((STAT_ROWS, rank), FL),
        ],
    )
    bars = exchange([bar_half] * outer, devices, inner)

    edge = struct((margin, width), BF)
    results = call(
        bind(attend_kernel, outer),
        pos,
        [*kv_pieces, kv_before, kv_after, *bars, *qg_pieces],
        [struct((tokens_here, heads * head_size), BF)] * inner
        + [struct((heads * rows, pair), BF)] * outer
        + [struct((group + 2 * margin, width), FL), edge, edge],
        [
            pltpu.VMEM((group + 2 * margin, width), BF),
            pltpu.VMEM((heads, rank, pair), BF),
            pltpu.VMEM((group, width), BF),
            pltpu.VMEM((heads, rank, pair), FL),
            pltpu.VMEM((group, heads * head_size), BF),
        ],
    )
    dq_send = results[:inner]
    dbar_send = results[inner : inner + outer]
    wg, wg_before, wg_after = results[inner + outer :]
    dbar_parts = exchange(dbar_send, devices, inner)
    wg_from_before, wg_from_after = swap_edges(wg_after, wg_before, devices, inner)
    (dbar_half,) = call(
        bind(combine_grad_kernel),
        pos,
        [bar_full, *dbar_parts],
        [struct((heads * rows + DOT_ROWS, pair), BF)],
    )
    dbars = exchange([dbar_half] * outer, devices, inner)
    dq_pieces = exchange(dq_send, devices, 1)

    dkv_pieces, logit_grads = [None] * inner, []
    for wave in waves:
        *dkv_send, logit_grad = call(
            bind(finish_kernel, wave),
            pos,
            [*(kv_pieces[k] for k in wave), weight, stats, wg, wg_from_before, wg_from_after, *dbars],
            [piece] * len(wave) + [struct((len(wave) * tokens_here, heads * rank), BF)],
            [pltpu.VMEM((heads, rank, pair), BF), pltpu.VMEM((heads, SEG, pair), FL)],
        )
        logit_grads.append(logit_grad)
        put(dkv_pieces, wave, exchange(dkv_send, devices, 1, wave))
    proj_send = call(
        bind(proj_kernel, waves),
        pos,
        [*kv_pieces, *logit_grads],
        [struct((heads * head_size // outer, rank), FL)] * outer,
        [pltpu.VMEM((heads * head_size, rank), FL)],
    )
    proj_parts = exchange(proj_send, devices, inner)
    proj_sum = proj_parts[0]
    for part in proj_parts[1:]:
        proj_sum = proj_sum + part
    place = [(o * inner + p, p * outer + o) for o in range(outer) for p in range(inner)]
    proj_here = lax.ppermute(proj_sum, "seq", place)
    whole = struct((tokens_here, row_width), BF)
    (grad_queries,) = call(bind(unpack_kernel), pos, dq_pieces, [whole], copies=inner, far="outs")
    grad_keys, grad_values, grad_proj = call(
        bind(unpack_pair_kernel),
        pos,
        [*dkv_pieces, proj_here],
        [whole, whole, struct(proj_here.shape, FL)],
        copies=2 * inner * heads + 1,
        far="outs",
    )
    return (grad_queries, grad_keys, grad_values, grad_proj)


def solution(mesh):
    in_specs = (P("seq", None), P("seq", None), P("seq", None), P("seq", None), P())
    out_specs = (P("seq", None), P("seq", None), P("seq", None), P("seq", None))
    return jax.shard_map(
        per_device, mesh=mesh, in_specs=in_specs, out_specs=out_specs, check_vma=False
    )
```

time: 174 us -> 171 us (0.983)
  local copies, waits for them, and re-layouts: 10.3 us -> 2.15 us
  waiting for transfers between devices: 54 us -> 57.7 us
    unnamed x35 -> x8, local copies, waits for them, and re-layouts: 10.3 us -> 2.14 us
    ppermute x44, waiting for transfers between devices: 54 us -> 57.7 us  [the longest x43 57.7 us: exchange(): out.append(lax.ppermute(field, 'seq', flip) if k else field)]
    pallas_call x10 -> x13, Pallas kernels: 38.5 us -> 39.2 us  [call(): pl.pallas_call(kernel, in_specs=[pl.BlockSpec(memory_space=pltpu.SMEM)] +...]
where the time goes in v1:
time: 171 us; the launch traced here: 170 us
  starting transfers between devices  70.4 us (41%)
  waiting for transfers between devices  57.7 us (34%)
  Pallas kernels  39.2 us (23%)
  local copies, waits for them, and re-layouts  2.15 us (1%)
    ppermute x43, starting transfers between devices, exchange(): out.append(lax.ppermute(field, 'seq', flip) if k else field)  62.9 us
    ppermute x43, waiting for transfers between devices, exchange(): out.append(lax.ppermute(field, 'seq', flip) if k else field)  57.7 us
    pallas_call x13, Pallas kernels, call(): pl.pallas_call(kernel, in_specs=[pl.BlockSpec(memory_space=pltpu.SMEM)] +...  39.2 us
    ppermute x2, starting transfers between devices, swap_edges(): lax.ppermute(upward, 'seq', up)  4.23 us
  transfers between devices with their start and end apart: 48, of which 12 were waited for; matrix products, arithmetic and copies ran while one was open for 0% of the time, Pallas kernels for 11%

profile of v1, /device:TPU:0, one launch (start us, length us, event | category | flops | bytes accessed | tf_op | source)
XLA Modules:
  0.0 170.4 jit_solution(11214684456023433427)
XLA Ops:
  0.7 3.1 %shard_map.84 = (bf16[256,512]{1,0:T(8,128)(2,1)S(1)}, bf16[256,512]{1,0:T(8,128)(2,1)S(1)}, bf16[256,512]{1,0:T(8,128)(2,1)S(1)}, bf16[256,512]{1,0:T(8,128)(2,...) custom-call(s32[2]{0:T(128)S(1)} %pad_add_fusion.pos_ref, ...), custom_call_target="tpu_custom_call" | custom-call | tf_op jit(solution)/shard_map/pallas_call | solution.py:51
  4.5 2.6 %collective-permute-start.1 = (bf16[256,512]{1,0:T(8,128)(2,1)S(1)}, bf16[256,512]{1,0:T(8,128)(2,1)S(1)}, u32[]{:S(2)}, u32[]{:S(2)}) collective-permute-start(bf16[256,512]{1,0:T(8,128)(2,1)S(1)} %get-tuple-element.66), channel_id=1, source_target_pairs={{0,2},{1,3},{2,0},{3,1},{4,6},{5,7},{6,4},{7,5},{8,10},{9,11},{10,... | collective-permute-start | bytes 786440 | tf_op jit(solution)/shard_map/ppermute | solution.py:440
  8.8 2.6 %collective-permute-start.5 = (bf16[256,512]{1,0:T(8,128)(2,1)S(1)}, bf16[256,512]{1,0:T(8,128)(2,1)S(1)}, u32[]{:S(2)}, u32[]{:S(2)}) collective-permute-start(bf16[256,512]{1,0:T(8,128)(2,1)S(1)} %get-tuple-element.70), channel_id=1, source_target_pairs={{0,6},{1,7},{2,4},{3,5},{4,2},{5,3},{6,0},{7,1},{8,14},{9,15},{10,... | collective-permute-start | bytes 786440 | tf_op jit(solution)/shard_map/ppermute | solution.py:440
  11.5 2.7 %collective-permute-done.1.refs_2_.refs_0_ = bf16[256,512]{1,0:T(8,128)(2,1)S(1)} collective-permute-done((bf16[256,512]{1,0:T(8,128)(2,1)S(1)}, bf16[256,512]{1,0:T(8,128)(2,1)S(1)}, u32[]{:S(2)}, u32[]{:S(2)}) %collective-permute-start.1) | collective-permute-done | bytes 262176 | tf_op jit(solution)/shard_map/ppermute | solution.py:440
  15.8 3.4 %shard_map.88 = (bf16[256,512]{1,0:T(8,128)(2,1)S(1)}, bf16[256,512]{1,0:T(8,128)(2,1)}, bf16[256,512]{1,0:T(8,128)(2,1)}, bf16[256,512]{1,0:T(8,128)(2,1)}, bf1...) custom-call(s32[2]{0:T(128)S(1)} %pad_add_fusion.pos_ref, ...), custom_call_target="tpu_custom_call" | custom-call | tf_op jit(solution)/shard_map/pallas_call | solution.py:51
  23.4 8.4 %collective-permute-done.4.refs_5_.refs_3_ = bf16[256,512]{1,0:T(8,128)(2,1)S(1)} collective-permute-done((bf16[256,512]{1,0:T(8,128)(2,1)S(1)}, bf16[256,512]{1,0:T(8,128)(2,1)S(1)}, u32[]{:S(2)}, u32[]{:S(2)}) %collective-permute-start.4) | collective-permute-done | bytes 262176 | tf_op jit(solution)/shard_map/ppermute | solution.py:440
  31.8 2.3 %collective-permute-start.17 = (bf16[256,512]{1,0:T(8,128)(2,1)}, bf16[256,512]{1,0:T(8,128)(2,1)}, u32[]{:S(2)}, u32[]{:S(2)}) collective-permute-start(bf16[256,512]{1,0:T(8,128)(2,1)} %get-tuple-element.84), channel_id=1, source_target_pairs={{0,3},{1,2},{2,1},{3,0},{4,7},{5,6},{6,5},{7,4},{8,11},{9,10},{10,... | collective-permute-start | bytes 786440 | tf_op jit(solution)/shard_map/ppermute | solution.py:440
  35.6 2.5 %shard_map.85 = (f32[2,256,256]{2,1,0:T(8,128)S(1)}, f32[8,256]{1,0:T(8,128)S(1)}) custom-call(s32[2]{0:T(128)S(1)} %pad_add_fusion.pos_ref, bf16[256,512]{1,0:T(8,128)(2,1)S(1)} %get-tuple-element.64.refs_0_, bf16[256,512]{1,0:T(8,128)(2,1)S(1)} %collective-permute-done.refs_1_, bf16[256,512]{1,0:T(8,128)(2,1)S(1)} %collective-permute-done.1.refs_2_.refs_0_, ...), custom_call_target="tpu_custom_call" | custom-call | tf_op jit(solution)/shard_map/pallas_call | solution.py:51
  44.8 2.6 %collective-permute-start.10 = (f32[136,256]{1,0:T(8,128)S(1)}, f32[136,256]{1,0:T(8,128)S(1)}, u32[]{:S(2)}, u32[]{:S(2)}) collective-permute-start(f32[136,256]{1,0:T(8,128)S(1)} %get-tuple-element.78), channel_id=1, source_target_pairs={{0,16},{1,17},{2,18},{3,19},{4,20},{5,21},{6,22},{7,23},{8,24},{9,... | collective-permute-start | bytes 417800 | tf_op jit(solution)/shard_map/ppermute | solution.py:440
  49.0 9.0 %collective-permute-done.10.refs_2_ = f32[136,256]{1,0:T(8,128)S(1)} collective-permute-done((f32[136,256]{1,0:T(8,128)S(1)}, f32[136,256]{1,0:T(8,128)S(1)}, u32[]{:S(2)}, u32[]{:S(2)}) %collective-permute-start.10) | collective-permute-done | bytes 139296 | tf_op jit(solution)/shard_map/ppermute | solution.py:440
  62.2 5.5 %collective-permute-start.14 = (bf16[128,256]{1,0:T(8,128)(2,1)S(1)}, bf16[128,256]{1,0:T(8,128)(2,1)S(1)}, u32[]{:S(2)}, u32[]{:S(2)}) collective-permute-start(bf16[128,256]{1,0:T(8,128)(2,1)S(1)} %get-tuple-element.80.refs_10_), channel_id=1, source_target_pairs={{0,24},{1,25},{2,26},{3,27},{4,28},{5,29},{6,30},{7,31},{8,16},{9,... | collective-permute-start | bytes 196616 | tf_op jit(solution)/shard_map/ppermute | solution.py:440
  68.4 3.2 %collective-permute-done.14.refs_13_ = bf16[128,256]{1,0:T(8,128)(2,1)S(1)} collective-permute-done((bf16[128,256]{1,0:T(8,128)(2,1)S(1)}, bf16[128,256]{1,0:T(8,128)(2,1)S(1)}, u32[]{:S(2)}, u32[]{:S(2)}) %collective-permute-start.14) | collective-permute-done | bytes 65568 | tf_op jit(solution)/shard_map/ppermute | solution.py:440
  73.3 15.3 %shard_map.89 = (bf16[256,256]{1,0:T(8,128)(2,1)S(1)}, bf16[256,256]{1,0:T(8,128)(2,1)S(1)}, bf16[256,256]{1,0:T(8,128)(2,1)S(1)}, bf16[256,256]{1,0:T(8,128)(2,...) custom-call(s32[2]{0:T(128)S(1)} %pad_add_fusion.pos_ref, ...), custom_call_target="tpu_custom_call" | custom-call | tf_op jit(solution)/shard_map/pallas_call | solution.py:51
  92.8 2.4 %collective-permute-start.33 = (bf16[128,256]{1,0:T(8,128)(2,1)S(1)}, bf16[128,256]{1,0:T(8,128)(2,1)S(1)}, u32[]{:S(2)}, u32[]{:S(2)}) collective-permute-start(bf16[128,256]{1,0:T(8,128)(2,1)S(1)} %get-tuple-element.105), channel_id=1, source_target_pairs={{0,24},{1,25},{2,26},{3,27},{4,28},{5,29},{6,30},{7,31},{8,16},{9,... | collective-permute-start | bytes 196616 | tf_op jit(solution)/shard_map/ppermute | solution.py:440
  96.6 3.3 %collective-permute-done.32.refs_3_ = bf16[128,256]{1,0:T(8,128)(2,1)S(1)} collective-permute-done((bf16[128,256]{1,0:T(8,128)(2,1)S(1)}, bf16[128,256]{1,0:T(8,128)(2,1)S(1)}, u32[]{:S(2)}, u32[]{:S(2)}) %collective-permute-start.32) | collective-permute-done | bytes 65568 | tf_op jit(solution)/shard_map/ppermute | solution.py:440
  102.2 3.4 %collective-permute-start.35 = (bf16[144,256]{1,0:T(8,128)(2,1)S(1)}, bf16[144,256]{1,0:T(8,128)(2,1)S(1)}, u32[]{:S(2)}, u32[]{:S(2)}) collective-permute-start(bf16[144,256]{1,0:T(8,128)(2,1)S(1)} %shard_map.91.refs_7_.refs_9_), channel_id=1, source_target_pairs={{0,16},{1,17},{2,18},{3,19},{4,20},{5,21},{6,22},{7,23},{8,24},{9,... | collective-permute-start | bytes 221192 | tf_op jit(solution)/shard_map/ppermute | solution.py:440
  114.6 2.9 %shard_map.93 = (bf16[256,512]{1,0:T(8,128)(2,1)S(1)}, bf16[256,512]{1,0:T(8,128)(2,1)S(1)}, bf16[256,512]{1,0:T(8,128)(2,1)S(1)}, bf16[256,512]{1,0:T(8,128)(2,1)S(1)}, bf16[1024,512]{1,0:T(8,128)(2,1)S(1)}) custom-call(s32[2]{0:T(128)S(1)} %pad_add_fusion.pos_ref, bf16[256,512]{1,0:T(8,128)(2,1)S(1)} %collective-permute-done.1.refs_2_.refs_0_, ...), custom_call_target="tpu_custom_call" | custom-call | tf_op jit(solution)/shard_map/pallas_call | solution.py:51
  119.9 3.1 %collective-permute-start.46 = (f32[64,256]{1,0:T(8,128)S(1)}, f32[64,256]{1,0:T(8,128)S(1)}, u32[]{:S(2)}, u32[]{:S(2)}) collective-permute-start(f32[64,256]{1,0:T(8,128)S(1)} %get-tuple-element.120), channel_id=1, source_target_pairs={{0,24},{1,25},{2,26},{3,27},{4,28},{5,29},{6,30},{7,31},{8,16},{9,... | collective-permute-start | bytes 196616 | tf_op jit(solution)/shard_map/ppermute | solution.py:440
  128.5 16.6 %collective-permute-done.26.refs_5_ = bf16[256,256]{1,0:T(8,128)(2,1)S(1)} collective-permute-done((bf16[256,256]{1,0:T(8,128)(2,1)S(1)}, bf16[256,256]{1,0:T(8,128)(2,1)S(1)}, u32[]{:S(2)}, u32[]{:S(2)}) %collective-permute-start.26) | collective-permute-done | bytes 131104 | tf_op jit(solution)/shard_map/ppermute | solution.py:440
  145.7 2.7 %collective-permute-start.37 = (bf16[256,512]{1,0:T(8,128)(2,1)S(1)}, bf16[256,512]{1,0:T(8,128)(2,1)S(1)}, u32[]{:S(2)}, u32[]{:S(2)}) collective-permute-start(bf16[256,512]{1,0:T(8,128)(2,1)S(1)} %get-tuple-element.107), channel_id=1, source_target_pairs={{0,1},{1,0},{2,3},{3,2},{4,5},{5,4},{6,7},{7,6},{8,9},{9,8},{10,11... | collective-permute-start | bytes 786440 | tf_op jit(solution)/shard_map/ppermute | solution.py:440
  148.9 4.0 %collective-permute-start.39 = (bf16[256,512]{1,0:T(8,128)(2,1)S(1)}, bf16[256,512]{1,0:T(8,128)(2,1)S(1)}, u32[]{:S(2)}, u32[]{:S(2)}) collective-permute-start(bf16[256,512]{1,0:T(8,128)(2,1)S(1)} %get-tuple-element.109), channel_id=1, source_target_pairs={{0,3},{1,2},{2,1},{3,0},{4,7},{5,6},{6,5},{7,4},{8,11},{9,10},{10,... | collective-permute-start | bytes 786440 | tf_op jit(solution)/shard_map/ppermute | solution.py:440
  152.9 2.6 %collective-permute-start.40 = (bf16[256,512]{1,0:T(8,128)(2,1)S(1)}, bf16[256,512]{1,0:T(8,128)(2,1)S(1)}, u32[]{:S(2)}, u32[]{:S(2)}) collective-permute-start(bf16[256,512]{1,0:T(8,128)(2,1)S(1)} %get-tuple-element.110), channel_id=1, source_target_pairs={{0,4},{1,5},{2,6},{3,7},{4,0},{5,1},{6,2},{7,3},{8,12},{9,13},{10,... | collective-permute-start | bytes 786440 | tf_op jit(solution)/shard_map/ppermute | solution.py:440
  158.6 4.5 %collective-permute-done.39.refs_3_ = bf16[256,512]{1,0:T(8,128)(2,1)S(1)} collective-permute-done((bf16[256,512]{1,0:T(8,128)(2,1)S(1)}, bf16[256,512]{1,0:T(8,128)(2,1)S(1)}, u32[]{:S(2)}, u32[]{:S(2)}) %collective-permute-start.39) | collective-permute-done | bytes 262176 | tf_op jit(solution)/shard_map/ppermute | solution.py:440
  163.1 5.2 %collective-permute-done.41.refs_5_ = bf16[256,512]{1,0:T(8,128)(2,1)S(1)} collective-permute-done((bf16[256,512]{1,0:T(8,128)(2,1)S(1)}, bf16[256,512]{1,0:T(8,128)(2,1)S(1)}, u32[]{:S(2)}, u32[]{:S(2)}) %collective-permute-start.41) | collective-permute-done | bytes 262176 | tf_op jit(solution)/shard_map/ppermute | solution.py:440
  (96 shorter events, 55.5 us)
Async XLA Ops:
  7.0 14.3 %collective-permute-start.2 = (bf16[256,512]{1,0:T(8,128)(2,1)S(1)}, bf16[256,512]{1,0:T(8,128)(2,1)S(1)}, u32[]{:S(2)}, u32[]{:S(2)}) collective-permute-start(bf16[256,512]{1,0:T(8,128)(2,1)S(1)} %get-tuple-element.67), channel_id=1, source_target_pairs={{0,3},{1,2},{2,1},{3,0},{4,7},{5,6},{6,5},{7,4},{8,11},{9,10},{10,... | collective-permute-start | bytes 786440 | tf_op jit(solution)/shard_map/ppermute | solution.py:440
  7.0 15.8 %collective-permute-start.3 = (bf16[256,512]{1,0:T(8,128)(2,1)S(1)}, bf16[256,512]{1,0:T(8,128)(2,1)S(1)}, u32[]{:S(2)}, u32[]{:S(2)}) collective-permute-start(bf16[256,512]{1,0:T(8,128)(2,1)S(1)} %get-tuple-element.68), channel_id=1, source_target_pairs={{0,4},{1,5},{2,6},{3,7},{4,0},{5,1},{6,2},{7,3},{8,12},{9,13},{10,... | collective-permute-start | bytes 786440 | tf_op jit(solution)/shard_map/ppermute | solution.py:440
  8.8 22.9 %collective-permute-start.4 = (bf16[256,512]{1,0:T(8,128)(2,1)S(1)}, bf16[256,512]{1,0:T(8,128)(2,1)S(1)}, u32[]{:S(2)}, u32[]{:S(2)}) collective-permute-start(bf16[256,512]{1,0:T(8,128)(2,1)S(1)} %get-tuple-element.69), channel_id=1, source_target_pairs={{0,5},{1,4},{2,7},{3,6},{4,1},{5,0},{6,3},{7,2},{8,13},{9,12},{10,... | collective-permute-start | bytes 786440 | tf_op jit(solution)/shard_map/ppermute | solution.py:440
  8.8 25.2 %collective-permute-start.5 = (bf16[256,512]{1,0:T(8,128)(2,1)S(1)}, bf16[256,512]{1,0:T(8,128)(2,1)S(1)}, u32[]{:S(2)}, u32[]{:S(2)}) collective-permute-start(bf16[256,512]{1,0:T(8,128)(2,1)S(1)} %get-tuple-element.70), channel_id=1, source_target_pairs={{0,6},{1,7},{2,4},{3,5},{4,2},{5,3},{6,0},{7,1},{8,14},{9,15},{10,... | collective-permute-start | bytes 786440 | tf_op jit(solution)/shard_map/ppermute | solution.py:440
  14.2 24.0 %collective-permute-start.6 = (bf16[256,512]{1,0:T(8,128)(2,1)}, bf16[256,512]{1,0:T(8,128)(2,1)S(1)}, u32[]{:S(2)}, u32[]{:S(2)}) collective-permute-start(bf16[256,512]{1,0:T(8,128)(2,1)} %get-tuple-element.71), channel_id=1, source_target_pairs={{0,7},{1,6},{2,5},{3,4},{4,3},{5,2},{6,1},{7,0},{8,15},{9,14},{10,... | collective-permute-start | bytes 786440 | tf_op jit(solution)/shard_map/ppermute | solution.py:440
  21.4 20.6 %collective-permute-start.15 = (bf16[256,512]{1,0:T(8,128)(2,1)}, bf16[256,512]{1,0:T(8,128)(2,1)}, u32[]{:S(2)}, u32[]{:S(2)}) collective-permute-start(bf16[256,512]{1,0:T(8,128)(2,1)} %get-tuple-element.82), channel_id=1, source_target_pairs={{0,1},{1,0},{2,3},{3,2},{4,5},{5,4},{6,7},{7,6},{8,9},{9,8},{10,11... | collective-permute-start | bytes 786440 | tf_op jit(solution)/shard_map/ppermute | solution.py:440
  22.8 19.1 %collective-permute-start.16 = (bf16[256,512]{1,0:T(8,128)(2,1)}, bf16[256,512]{1,0:T(8,128)(2,1)}, u32[]{:S(2)}, u32[]{:S(2)}) collective-permute-start(bf16[256,512]{1,0:T(8,128)(2,1)} %get-tuple-element.83), channel_id=1, source_target_pairs={{0,2},{1,3},{2,0},{3,1},{4,6},{5,7},{6,4},{7,5},{8,10},{9,11},{10,... | collective-permute-start | bytes 786440 | tf_op jit(solution)/shard_map/ppermute | solution.py:440
  41.9 20.3 %collective-permute-start.19 = (bf16[256,512]{1,0:T(8,128)(2,1)}, bf16[256,512]{1,0:T(8,128)(2,1)S(1)}, u32[]{:S(2)}, u32[]{:S(2)}) collective-permute-start(bf16[256,512]{1,0:T(8,128)(2,1)} %copy-done.3), channel_id=1, source_target_pairs={{0,5},{1,4},{2,7},{3,6},{4,1},{5,0},{6,3},{7,2},{8,13},{9,12},{10,... | collective-permute-start | bytes 786440 | tf_op jit(solution)/shard_map/ppermute | solution.py:440
  41.9 25.8 %collective-permute-start.20 = (bf16[256,512]{1,0:T(8,128)(2,1)}, bf16[256,512]{1,0:T(8,128)(2,1)S(1)}, u32[]{:S(2)}, u32[]{:S(2)}) collective-permute-start(bf16[256,512]{1,0:T(8,128)(2,1)} %copy-done.2), channel_id=1, source_target_pairs={{0,6},{1,7},{2,4},{3,5},{4,2},{5,3},{6,0},{7,1},{8,14},{9,15},{10,... | collective-permute-start | bytes 786440 | tf_op jit(solution)/shard_map/ppermute | solution.py:440
  42.9 24.9 %collective-permute-start.21 = (bf16[256,512]{1,0:T(8,128)(2,1)}, bf16[256,512]{1,0:T(8,128)(2,1)S(1)}, u32[]{:S(2)}, u32[]{:S(2)}) collective-permute-start(bf16[256,512]{1,0:T(8,128)(2,1)} %copy-done.1), channel_id=1, source_target_pairs={{0,7},{1,6},{2,5},{3,4},{4,3},{5,2},{6,1},{7,0},{8,15},{9,14},{10,... | collective-permute-start | bytes 786440 | tf_op jit(solution)/shard_map/ppermute | solution.py:440
  44.8 13.2 %collective-permute-start.10 = (f32[136,256]{1,0:T(8,128)S(1)}, f32[136,256]{1,0:T(8,128)S(1)}, u32[]{:S(2)}, u32[]{:S(2)}) collective-permute-start(f32[136,256]{1,0:T(8,128)S(1)} %get-tuple-element.78), channel_id=1, source_target_pairs={{0,16},{1,17},{2,18},{3,19},{4,20},{5,21},{6,22},{7,23},{8,24},{9,... | collective-permute-start | bytes 417800 | tf_op jit(solution)/shard_map/ppermute | solution.py:440
  47.4 12.8 %collective-permute-start.11 = (f32[136,256]{1,0:T(8,128)S(1)}, f32[136,256]{1,0:T(8,128)S(1)}, u32[]{:S(2)}, u32[]{:S(2)}) collective-permute-start(f32[136,256]{1,0:T(8,128)S(1)} %get-tuple-element.79), channel_id=1, source_target_pairs={{0,24},{1,25},{2,26},{3,27},{4,28},{5,29},{6,30},{7,31},{8,16},{9,... | collective-permute-start | bytes 417800 | tf_op jit(solution)/shard_map/ppermute | solution.py:440
  88.7 16.9 %collective-permute-start.29 = (bf16[128,512]{1,0:T(8,128)(2,1)S(1)}, bf16[128,512]{1,0:T(8,128)(2,1)S(1)}, u32[]{:S(2)}, u32[]{:S(2)}) collective-permute-start(bf16[128,512]{1,0:T(8,128)(2,1)S(1)} %get-tuple-element.99), channel_id=1, source_target_pairs={{0,8},{1,9},{2,10},{3,11},{4,12},{5,13},{6,14},{7,15},{8,16},{9,17... | collective-permute-start | bytes 393224 | tf_op jit(solution)/shard_map/ppermute | solution.py:447
  105.6 13.5 %collective-permute-start.22 = (bf16[256,256]{1,0:T(8,128)(2,1)S(1)}, bf16[256,256]{1,0:T(8,128)(2,1)S(1)}, u32[]{:S(2)}, u32[]{:S(2)}) collective-permute-start(bf16[256,256]{1,0:T(8,128)(2,1)S(1)} %get-tuple-element.90), channel_id=1, source_target_pairs={{0,1},{1,0},{2,3},{3,2},{4,5},{5,4},{6,7},{7,6},{8,9},{9,8},{10,11... | collective-permute-start | bytes 393224 | tf_op jit(solution)/shard_map/ppermute | solution.py:440
  105.6 14.3 %collective-permute-start.23 = (bf16[256,256]{1,0:T(8,128)(2,1)S(1)}, bf16[256,256]{1,0:T(8,128)(2,1)S(1)}, u32[]{:S(2)}, u32[]{:S(2)}) collective-permute-start(bf16[256,256]{1,0:T(8,128)(2,1)S(1)} %get-tuple-element.91), channel_id=1, source_target_pairs={{0,2},{1,3},{2,0},{3,1},{4,6},{5,7},{6,4},{7,5},{8,10},{9,11},{10,... | collective-permute-start | bytes 393224 | tf_op jit(solution)/shard_map/ppermute | solution.py:440
  106.8 16.3 %collective-permute-start.24 = (bf16[256,256]{1,0:T(8,128)(2,1)S(1)}, bf16[256,256]{1,0:T(8,128)(2,1)S(1)}, u32[]{:S(2)}, u32[]{:S(2)}) collective-permute-start(bf16[256,256]{1,0:T(8,128)(2,1)S(1)} %get-tuple-element.92), channel_id=1, source_target_pairs={{0,3},{1,2},{2,1},{3,0},{4,7},{5,6},{6,5},{7,4},{8,11},{9,10},{10,... | collective-permute-start | bytes 393224 | tf_op jit(solution)/shard_map/ppermute | solution.py:440
  109.6 13.4 %collective-permute-start.25 = (bf16[256,256]{1,0:T(8,128)(2,1)S(1)}, bf16[256,256]{1,0:T(8,128)(2,1)S(1)}, u32[]{:S(2)}, u32[]{:S(2)}) collective-permute-start(bf16[256,256]{1,0:T(8,128)(2,1)S(1)} %get-tuple-element.93), channel_id=1, source_target_pairs={{0,4},{1,5},{2,6},{3,7},{4,0},{5,1},{6,2},{7,3},{8,12},{9,13},{10,... | collective-permute-start | bytes 393224 | tf_op jit(solution)/shard_map/ppermute | solution.py:440
  123.1 22.0 %collective-permute-start.26 = (bf16[256,256]{1,0:T(8,128)(2,1)S(1)}, bf16[256,256]{1,0:T(8,128)(2,1)S(1)}, u32[]{:S(2)}, u32[]{:S(2)}) collective-permute-start(bf16[256,256]{1,0:T(8,128)(2,1)S(1)} %get-tuple-element.94), channel_id=1, source_target_pairs={{0,5},{1,4},{2,7},{3,6},{4,1},{5,0},{6,3},{7,2},{8,13},{9,12},{10,... | collective-permute-start | bytes 393224 | tf_op jit(solution)/shard_map/ppermute | solution.py:440
  123.1 22.6 %collective-permute-start.27 = (bf16[256,256]{1,0:T(8,128)(2,1)S(1)}, bf16[256,256]{1,0:T(8,128)(2,1)S(1)}, u32[]{:S(2)}, u32[]{:S(2)}) collective-permute-start(bf16[256,256]{1,0:T(8,128)(2,1)S(1)} %get-tuple-element.95), channel_id=1, source_target_pairs={{0,6},{1,7},{2,4},{3,5},{4,2},{5,3},{6,0},{7,1},{8,14},{9,15},{10,... | collective-permute-start | bytes 393224 | tf_op jit(solution)/shard_map/ppermute | solution.py:440
  124.3 24.1 %collective-permute-start.28 = (bf16[256,256]{1,0:T(8,128)(2,1)S(1)}, bf16[256,256]{1,0:T(8,128)(2,1)S(1)}, u32[]{:S(2)}, u32[]{:S(2)}) collective-permute-start(bf16[256,256]{1,0:T(8,128)(2,1)S(1)} %get-tuple-element.96), channel_id=1, source_target_pairs={{0,7},{1,6},{2,5},{3,4},{4,3},{5,2},{6,1},{7,0},{8,15},{9,14},{10,... | collective-permute-start | bytes 393224 | tf_op jit(solution)/shard_map/ppermute | solution.py:440
  126.7 26.2 %collective-permute-start.42 = (bf16[256,512]{1,0:T(8,128)(2,1)S(1)}, bf16[256,512]{1,0:T(8,128)(2,1)S(1)}, u32[]{:S(2)}, u32[]{:S(2)}) collective-permute-start(bf16[256,512]{1,0:T(8,128)(2,1)S(1)} %get-tuple-element.112), channel_id=1, source_target_pairs={{0,6},{1,7},{2,4},{3,5},{4,2},{5,3},{6,0},{7,1},{8,14},{9,15},{10,... | collective-permute-start | bytes 786440 | tf_op jit(solution)/shard_map/ppermute | solution.py:440
  128.1 27.4 %collective-permute-start.43 = (bf16[256,512]{1,0:T(8,128)(2,1)S(1)}, bf16[256,512]{1,0:T(8,128)(2,1)S(1)}, u32[]{:S(2)}, u32[]{:S(2)}) collective-permute-start(bf16[256,512]{1,0:T(8,128)(2,1)S(1)} %get-tuple-element.113), channel_id=1, source_target_pairs={{0,7},{1,6},{2,5},{3,4},{4,3},{5,2},{6,1},{7,0},{8,15},{9,14},{10,... | collective-permute-start | bytes 786440 | tf_op jit(solution)/shard_map/ppermute | solution.py:440
  145.7 12.9 %collective-permute-start.37 = (bf16[256,512]{1,0:T(8,128)(2,1)S(1)}, bf16[256,512]{1,0:T(8,128)(2,1)S(1)}, u32[]{:S(2)}, u32[]{:S(2)}) collective-permute-start(bf16[256,512]{1,0:T(8,128)(2,1)S(1)} %get-tuple-element.107), channel_id=1, source_target_pairs={{0,1},{1,0},{2,3},{3,2},{4,5},{5,4},{6,7},{7,6},{8,9},{9,8},{10,11... | collective-permute-start | bytes 786440 | tf_op jit(solution)/shard_map/ppermute | solution.py:440
  148.9 14.2 %collective-permute-start.39 = (bf16[256,512]{1,0:T(8,128)(2,1)S(1)}, bf16[256,512]{1,0:T(8,128)(2,1)S(1)}, u32[]{:S(2)}, u32[]{:S(2)}) collective-permute-start(bf16[256,512]{1,0:T(8,128)(2,1)S(1)} %get-tuple-element.109), channel_id=1, source_target_pairs={{0,3},{1,2},{2,1},{3,0},{4,7},{5,6},{6,5},{7,4},{8,11},{9,10},{10,... | collective-permute-start | bytes 786440 | tf_op jit(solution)/shard_map/ppermute | solution.py:440
  (28 other events, 227.7 us)

commit v2 on v1

--- a/solution.py
+++ b/solution.py
@@ -38,24 +38,25 @@
     return math.prod(x.shape) * dtype.itemsize
 
 
-def call(kernel, pos, ins, outs, scratch=(), spare=4, copies=0, far=""):
+def call(kernel, pos, ins, outs, scratch=(), spare=4, far=""):
     near = pl.BlockSpec(memory_space=pltpu.VMEM)
     hbm = pl.BlockSpec(memory_space=pltpu.HBM)
-    if copies:
-        scratch = [pltpu.SemaphoreType.DMA((copies,))]
-        need = sum(size_of(x) for x in (ins if far == "outs" else outs))
+    held = [x for x in scratch if hasattr(x.dtype, "itemsize")]
+    if "ins" in far:
+        ins = [pltpu.with_memory_space_constraint(x, pltpu.HBM) for x in ins]
     else:
-        need = sum(size_of(x) for x in (*ins, *outs, *scratch))
-    if far == "ins":
-        ins = [pltpu.with_memory_space_constraint(x, pltpu.HBM) for x in ins]
+        held += ins
+    if "outs" not in far:
+        held += outs
     return pl.pallas_call(
         kernel,
-        in_specs=[pl.BlockSpec(memory_space=pltpu.SMEM)]
-        + [hbm if far == "ins" else near] * len(ins),
-        out_specs=[hbm if far == "outs" else near] * len(outs),
+        in_specs=[pl.BlockSpec(memory_space=pltpu.SMEM)] + [hbm if "ins" in far else near] * len(ins),
+        out_specs=[hbm if "outs" in far else near] * len(outs),
         out_shape=list(outs),
         scratch_shapes=list(scratch),
-        compiler_params=pltpu.CompilerParams(vmem_limit_bytes=need + spare * 2**20),
+        compiler_params=pltpu.CompilerParams(
+            vmem_limit_bytes=sum(map(size_of, held)) + spare * 2**20
+        ),
     )(pos, *ins)
 
 
@@ -64,6 +65,7 @@
         self.inner = math.gcd(head_count // HEADS_PER_DEVICE, devices)
         self.outer = devices // self.inner
         self.heads = head_count // self.inner
+        self.devices = devices
         self.tokens = tokens_here
         self.group = tokens_here * self.inner
         self.head_size = head_size
@@ -88,15 +90,30 @@
 
 
 def pack_kernel(plan, pos, a_ref, b_ref, *refs):
-    outs, sems = refs[:-1], refs[-1]
+    outs, (in_sems, out_sems, buffer) = refs[: plan.inner], refs[plan.inner :]
     hd = plan.head_size
-    moves = []
+    coming, leaving = [], []
     for k, out in enumerate(outs):
         for h in range(plan.heads):
             cols = head_slices(plan, pos[1] ^ k, h)
-            moves.append((a_ref.at[:, cols], out.at[:, pl.ds(2 * h * hd, hd)]))
-            moves.append((b_ref.at[:, cols], out.at[:, pl.ds((2 * h + 1) * hd, hd)]))
-    run_copies(sems, moves)
+            for side, src in enumerate((a_ref, b_ref)):
+                at = 2 * h + side
+                coming.append(
+                    pltpu.make_async_copy(
+                        src.at[:, cols],
+                        buffer.at[k, :, pl.ds(at * hd, hd)],
+                        in_sems.at[2 * plan.heads * k + at],
+                    )
+                )
+        leaving.append(pltpu.make_async_copy(buffer.at[k], out, out_sems.at[k]))
+    for copy in coming:
+        copy.start()
+    for k in range(plan.inner):
+        for copy in coming[2 * plan.heads * k : 2 * plan.heads * (k + 1)]:
+            copy.wait()
+        leaving[k].start()
+    for copy in leaving:
+        copy.wait()
 
 
 def unpack_pair_kernel(plan, pos, *refs):
@@ -472,8 +489,12 @@
             pos,
             [first, second],
             [piece] * inner,
-            copies=2 * inner * heads,
-            far="ins",
+            [
+                pltpu.SemaphoreType.DMA((2 * inner * heads,)),
+                pltpu.SemaphoreType.DMA((inner,)),
+                pltpu.VMEM((inner, tokens_here, width), BF),
+            ],
+            far="ins outs",
         )
 
     kv_pieces = exchange(pack(keys, values), devices, 1)
@@ -536,13 +557,13 @@
     dbar_parts = exchange(dbar_send, devices, inner)
     wg_from_before, wg_from_after = swap_edges(wg_after, wg_before, devices, inner)
     (dbar_half,) = call(
-        bind(combine_grad_kernel),
-        pos,
-        [bar_full, *dbar_parts],
-        [struct((heads * rows + DOT_ROWS, pair), BF)],
+        bind(combine_grad_kernel), pos, [bar_full, *dbar_parts], [struct((heads * rows + DOT_ROWS, pair), BF)]
     )
     dbars = exchange([dbar_half] * outer, devices, inner)
-    dq_pieces = exchange(dq_send, devices, 1)
+    dq_pieces = [None] * inner
+    first, others = waves[0], tuple(k for k in range(inner) if k not in waves[0])
+    put(dq_pieces, first, exchange([dq_send[k] for k in first], devices, 1, first))
+    put(dq_pieces, others, exchange([dq_send[k] for k in others], devices, 1, others))
 
     dkv_pieces, logit_grads = [None] * inner, []
     for wave in waves:
@@ -569,13 +590,15 @@
     place = [(o * inner + p, p * outer + o) for o in range(outer) for p in range(inner)]
     proj_here = lax.ppermute(proj_sum, "seq", place)
     whole = struct((tokens_here, row_width), BF)
-    (grad_queries,) = call(bind(unpack_kernel), pos, dq_pieces, [whole], copies=inner, far="outs")
+    (grad_queries,) = call(
+        bind(unpack_kernel), pos, dq_pieces, [whole], [pltpu.SemaphoreType.DMA((inner,))], far="outs"
+    )
     grad_keys, grad_values, grad_proj = call(
         bind(unpack_pair_kernel),
         pos,
         [*dkv_pieces, proj_here],
         [whole, whole, struct(proj_here.shape, FL)],
-        copies=2 * inner * heads + 1,
+        [pltpu.SemaphoreType.DMA((2 * inner * heads + 1,))],
         far="outs",
     )
     return (grad_queries, grad_keys, grad_values, grad_proj)
@@ -584,6 +607,4 @@
 def solution(mesh):
     in_specs = (P("seq", None), P("seq", None), P("seq", None), P("seq", None), P())
     out_specs = (P("seq", None), P("seq", None), P("seq", None), P("seq", None))
-    return jax.shard_map(
-        per_device, mesh=mesh, in_specs=in_specs, out_specs=out_specs, check_vma=False
-    )
+    return jax.shard_map(per_device, mesh=mesh, in_specs=in_specs, out_specs=out_specs, check_vma=False)

time: 171 us -> 171 us (level)
  no operation moved by 1% of the time
where the time goes in v2:
time: 171 us
  starting transfers between devices  70.4 us (41%)
  waiting for transfers between devices  58.2 us (34%)
  Pallas kernels  38.9 us (23%)
  local copies, waits for them, and re-layouts  2.15 us (1%)
    ppermute x43, starting transfers between devices, exchange(): out.append(lax.ppermute(field, 'seq', flip) if k else field)  62.9 us
    ppermute x43, waiting for transfers between devices, exchange(): out.append(lax.ppermute(field, 'seq', flip) if k else field)  58.1 us
    pallas_call x13, Pallas kernels, call(): pl.pallas_call(kernel, in_specs=[pl.BlockSpec(memory_space=pltpu.SMEM)] +...  38.9 us
    ppermute x2, starting transfers between devices, swap_edges(): lax.ppermute(upward, 'seq', up)  4.24 us
  transfers between devices with their start and end apart: 48, of which 12 were waited for; matrix products, arithmetic and copies ran while one was open for 0% of the time, Pallas kernels for 11%

profile of v2, /device:TPU:0, one launch (start us, length us, event | category | flops | bytes accessed | tf_op | source)
XLA Modules:
  0.0 170.8 jit_solution(2018426673920659322)
XLA Ops:
  0.7 3.2 %shard_map.84 = (bf16[256,512]{1,0:T(8,128)(2,1)S(1)}, bf16[256,512]{1,0:T(8,128)(2,1)S(1)}, bf16[256,512]{1,0:T(8,128)(2,1)S(1)}, bf16[256,512]{1,0:T(8,128)(2,...) custom-call(s32[2]{0:T(128)S(1)} %pad_add_fusion.pos_ref, ...), custom_call_target="tpu_custom_call" | custom-call | tf_op jit(solution)/shard_map/pallas_call | solution.py:51
  4.5 2.6 %collective-permute-start.1 = (bf16[256,512]{1,0:T(8,128)(2,1)S(1)}, bf16[256,512]{1,0:T(8,128)(2,1)S(1)}, u32[]{:S(2)}, u32[]{:S(2)}) collective-permute-start(bf16[256,512]{1,0:T(8,128)(2,1)S(1)} %get-tuple-element.66), channel_id=1, source_target_pairs={{0,2},{1,3},{2,0},{3,1},{4,6},{5,7},{6,4},{7,5},{8,10},{9,11},{10,... | collective-permute-start | bytes 786440 | tf_op jit(solution)/shard_map/ppermute | solution.py:457
  8.9 2.6 %collective-permute-start.5 = (bf16[256,512]{1,0:T(8,128)(2,1)S(1)}, bf16[256,512]{1,0:T(8,128)(2,1)S(1)}, u32[]{:S(2)}, u32[]{:S(2)}) collective-permute-start(bf16[256,512]{1,0:T(8,128)(2,1)S(1)} %get-tuple-element.70), channel_id=1, source_target_pairs={{0,6},{1,7},{2,4},{3,5},{4,2},{5,3},{6,0},{7,1},{8,14},{9,15},{10,... | collective-permute-start | bytes 786440 | tf_op jit(solution)/shard_map/ppermute | solution.py:457
  11.5 2.7 %collective-permute-done.1.refs_2_.refs_0_ = bf16[256,512]{1,0:T(8,128)(2,1)S(1)} collective-permute-done((bf16[256,512]{1,0:T(8,128)(2,1)S(1)}, bf16[256,512]{1,0:T(8,128)(2,1)S(1)}, u32[]{:S(2)}, u32[]{:S(2)}) %collective-permute-start.1) | collective-permute-done | bytes 262176 | tf_op jit(solution)/shard_map/ppermute | solution.py:457
  15.9 3.0 %shard_map.88 = (bf16[256,512]{1,0:T(8,128)(2,1)S(1)}, bf16[256,512]{1,0:T(8,128)(2,1)}, bf16[256,512]{1,0:T(8,128)(2,1)}, bf16[256,512]{1,0:T(8,128)(2,1)}, bf1...) custom-call(s32[2]{0:T(128)S(1)} %pad_add_fusion.pos_ref, ...), custom_call_target="tpu_custom_call" | custom-call | tf_op jit(solution)/shard_map/pallas_call | solution.py:51
  23.0 8.8 %collective-permute-done.4.refs_5_.refs_3_ = bf16[256,512]{1,0:T(8,128)(2,1)S(1)} collective-permute-done((bf16[256,512]{1,0:T(8,128)(2,1)S(1)}, bf16[256,512]{1,0:T(8,128)(2,1)S(1)}, u32[]{:S(2)}, u32[]{:S(2)}) %collective-permute-start.4) | collective-permute-done | bytes 262176 | tf_op jit(solution)/shard_map/ppermute | solution.py:457
  31.8 2.3 %collective-permute-start.17 = (bf16[256,512]{1,0:T(8,128)(2,1)}, bf16[256,512]{1,0:T(8,128)(2,1)}, u32[]{:S(2)}, u32[]{:S(2)}) collective-permute-start(bf16[256,512]{1,0:T(8,128)(2,1)} %get-tuple-element.84), channel_id=1, source_target_pairs={{0,3},{1,2},{2,1},{3,0},{4,7},{5,6},{6,5},{7,4},{8,11},{9,10},{10,... | collective-permute-start | bytes 786440 | tf_op jit(solution)/shard_map/ppermute | solution.py:457
  35.7 2.5 %shard_map.85 = (f32[2,256,256]{2,1,0:T(8,128)S(1)}, f32[8,256]{1,0:T(8,128)S(1)}) custom-call(s32[2]{0:T(128)S(1)} %pad_add_fusion.pos_ref, bf16[256,512]{1,0:T(8,128)(2,1)S(1)} %get-tuple-element.64.refs_0_, bf16[256,512]{1,0:T(8,128)(2,1)S(1)} %collective-permute-done.refs_1_, bf16[256,512]{1,0:T(8,128)(2,1)S(1)} %collective-permute-done.1.refs_2_.refs_0_, ...), custom_call_target="tpu_custom_call" | custom-call | tf_op jit(solution)/shard_map/pallas_call | solution.py:51
  44.9 2.6 %collective-permute-start.10 = (f32[136,256]{1,0:T(8,128)S(1)}, f32[136,256]{1,0:T(8,128)S(1)}, u32[]{:S(2)}, u32[]{:S(2)}) collective-permute-start(f32[136,256]{1,0:T(8,128)S(1)} %get-tuple-element.78), channel_id=1, source_target_pairs={{0,16},{1,17},{2,18},{3,19},{4,20},{5,21},{6,22},{7,23},{8,24},{9,... | collective-permute-start | bytes 417800 | tf_op jit(solution)/shard_map/ppermute | solution.py:457
  49.1 9.0 %collective-permute-done.10.refs_2_ = f32[136,256]{1,0:T(8,128)S(1)} collective-permute-done((f32[136,256]{1,0:T(8,128)S(1)}, f32[136,256]{1,0:T(8,128)S(1)}, u32[]{:S(2)}, u32[]{:S(2)}) %collective-permute-start.10) | collective-permute-done | bytes 139296 | tf_op jit(solution)/shard_map/ppermute | solution.py:457
  62.3 5.5 %collective-permute-start.14 = (bf16[128,256]{1,0:T(8,128)(2,1)S(1)}, bf16[128,256]{1,0:T(8,128)(2,1)S(1)}, u32[]{:S(2)}, u32[]{:S(2)}) collective-permute-start(bf16[128,256]{1,0:T(8,128)(2,1)S(1)} %get-tuple-element.80.refs_10_), channel_id=1, source_target_pairs={{0,24},{1,25},{2,26},{3,27},{4,28},{5,29},{6,30},{7,31},{8,16},{9,... | collective-permute-start | bytes 196616 | tf_op jit(solution)/shard_map/ppermute | solution.py:457
  68.5 3.2 %collective-permute-done.14.refs_13_ = bf16[128,256]{1,0:T(8,128)(2,1)S(1)} collective-permute-done((bf16[128,256]{1,0:T(8,128)(2,1)S(1)}, bf16[128,256]{1,0:T(8,128)(2,1)S(1)}, u32[]{:S(2)}, u32[]{:S(2)}) %collective-permute-start.14) | collective-permute-done | bytes 65568 | tf_op jit(solution)/shard_map/ppermute | solution.py:457
  73.4 15.3 %shard_map.89 = (bf16[256,256]{1,0:T(8,128)(2,1)S(1)}, bf16[256,256]{1,0:T(8,128)(2,1)S(1)}, bf16[256,256]{1,0:T(8,128)(2,1)S(1)}, bf16[256,256]{1,0:T(8,128)(2,...) custom-call(s32[2]{0:T(128)S(1)} %pad_add_fusion.pos_ref, ...), custom_call_target="tpu_custom_call" | custom-call | tf_op jit(solution)/shard_map/pallas_call | solution.py:51
  92.9 2.4 %collective-permute-start.33 = (bf16[128,256]{1,0:T(8,128)(2,1)S(1)}, bf16[128,256]{1,0:T(8,128)(2,1)S(1)}, u32[]{:S(2)}, u32[]{:S(2)}) collective-permute-start(bf16[128,256]{1,0:T(8,128)(2,1)S(1)} %get-tuple-element.105), channel_id=1, source_target_pairs={{0,24},{1,25},{2,26},{3,27},{4,28},{5,29},{6,30},{7,31},{8,16},{9,... | collective-permute-start | bytes 196616 | tf_op jit(solution)/shard_map/ppermute | solution.py:457
  96.6 3.3 %collective-permute-done.32.refs_3_ = bf16[128,256]{1,0:T(8,128)(2,1)S(1)} collective-permute-done((bf16[128,256]{1,0:T(8,128)(2,1)S(1)}, bf16[128,256]{1,0:T(8,128)(2,1)S(1)}, u32[]{:S(2)}, u32[]{:S(2)}) %collective-permute-start.32) | collective-permute-done | bytes 65568 | tf_op jit(solution)/shard_map/ppermute | solution.py:457
  102.3 3.4 %collective-permute-start.35 = (bf16[144,256]{1,0:T(8,128)(2,1)S(1)}, bf16[144,256]{1,0:T(8,128)(2,1)S(1)}, u32[]{:S(2)}, u32[]{:S(2)}) collective-permute-start(bf16[144,256]{1,0:T(8,128)(2,1)S(1)} %shard_map.91.refs_7_.refs_9_), channel_id=1, source_target_pairs={{0,16},{1,17},{2,18},{3,19},{4,20},{5,21},{6,22},{7,23},{8,24},{9,... | collective-permute-start | bytes 221192 | tf_op jit(solution)/shard_map/ppermute | solution.py:457
  114.7 3.1 %shard_map.93 = (bf16[256,512]{1,0:T(8,128)(2,1)S(1)}, bf16[256,512]{1,0:T(8,128)(2,1)S(1)}, bf16[256,512]{1,0:T(8,128)(2,1)S(1)}, bf16[256,512]{1,0:T(8,128)(2,1)S(1)}, bf16[1024,512]{1,0:T(8,128)(2,1)S(1)}) custom-call(s32[2]{0:T(128)S(1)} %pad_add_fusion.pos_ref, bf16[256,512]{1,0:T(8,128)(2,1)S(1)} %collective-permute-done.1.refs_2_.refs_0_, ...), custom_call_target="tpu_custom_call" | custom-call | tf_op jit(solution)/shard_map/pallas_call | solution.py:51
  120.2 3.1 %collective-permute-start.46 = (f32[64,256]{1,0:T(8,128)S(1)}, f32[64,256]{1,0:T(8,128)S(1)}, u32[]{:S(2)}, u32[]{:S(2)}) collective-permute-start(f32[64,256]{1,0:T(8,128)S(1)} %get-tuple-element.120), channel_id=1, source_target_pairs={{0,24},{1,25},{2,26},{3,27},{4,28},{5,29},{6,30},{7,31},{8,16},{9,... | collective-permute-start | bytes 196616 | tf_op jit(solution)/shard_map/ppermute | solution.py:457
  128.7 16.6 %collective-permute-done.26.refs_5_ = bf16[256,256]{1,0:T(8,128)(2,1)S(1)} collective-permute-done((bf16[256,256]{1,0:T(8,128)(2,1)S(1)}, bf16[256,256]{1,0:T(8,128)(2,1)S(1)}, u32[]{:S(2)}, u32[]{:S(2)}) %collective-permute-start.26) | collective-permute-done | bytes 131104 | tf_op jit(solution)/shard_map/ppermute | solution.py:457
  145.9 2.7 %collective-permute-start.37 = (bf16[256,512]{1,0:T(8,128)(2,1)S(1)}, bf16[256,512]{1,0:T(8,128)(2,1)S(1)}, u32[]{:S(2)}, u32[]{:S(2)}) collective-permute-start(bf16[256,512]{1,0:T(8,128)(2,1)S(1)} %get-tuple-element.107), channel_id=1, source_target_pairs={{0,1},{1,0},{2,3},{3,2},{4,5},{5,4},{6,7},{7,6},{8,9},{9,8},{10,11... | collective-permute-start | bytes 786440 | tf_op jit(solution)/shard_map/ppermute | solution.py:457
  149.1 4.0 %collective-permute-start.39 = (bf16[256,512]{1,0:T(8,128)(2,1)S(1)}, bf16[256,512]{1,0:T(8,128)(2,1)S(1)}, u32[]{:S(2)}, u32[]{:S(2)}) collective-permute-start(bf16[256,512]{1,0:T(8,128)(2,1)S(1)} %get-tuple-element.109), channel_id=1, source_target_pairs={{0,3},{1,2},{2,1},{3,0},{4,7},{5,6},{6,5},{7,4},{8,11},{9,10},{10,... | collective-permute-start | bytes 786440 | tf_op jit(solution)/shard_map/ppermute | solution.py:457
  153.1 2.6 %collective-permute-start.40 = (bf16[256,512]{1,0:T(8,128)(2,1)S(1)}, bf16[256,512]{1,0:T(8,128)(2,1)S(1)}, u32[]{:S(2)}, u32[]{:S(2)}) collective-permute-start(bf16[256,512]{1,0:T(8,128)(2,1)S(1)} %get-tuple-element.110), channel_id=1, source_target_pairs={{0,4},{1,5},{2,6},{3,7},{4,0},{5,1},{6,2},{7,3},{8,12},{9,13},{10,... | collective-permute-start | bytes 786440 | tf_op jit(solution)/shard_map/ppermute | solution.py:457
  158.8 4.5 %collective-permute-done.39.refs_3_ = bf16[256,512]{1,0:T(8,128)(2,1)S(1)} collective-permute-done((bf16[256,512]{1,0:T(8,128)(2,1)S(1)}, bf16[256,512]{1,0:T(8,128)(2,1)S(1)}, u32[]{:S(2)}, u32[]{:S(2)}) %collective-permute-start.39) | collective-permute-done | bytes 262176 | tf_op jit(solution)/shard_map/ppermute | solution.py:457
  163.3 5.2 %collective-permute-done.41.refs_5_ = bf16[256,512]{1,0:T(8,128)(2,1)S(1)} collective-permute-done((bf16[256,512]{1,0:T(8,128)(2,1)S(1)}, bf16[256,512]{1,0:T(8,128)(2,1)S(1)}, u32[]{:S(2)}, u32[]{:S(2)}) %collective-permute-start.41) | collective-permute-done | bytes 262176 | tf_op jit(solution)/shard_map/ppermute | solution.py:457
  (96 shorter events, 55.5 us)
Async XLA Ops:
  7.1 13.9 %collective-permute-start.2 = (bf16[256,512]{1,0:T(8,128)(2,1)S(1)}, bf16[256,512]{1,0:T(8,128)(2,1)S(1)}, u32[]{:S(2)}, u32[]{:S(2)}) collective-permute-start(bf16[256,512]{1,0:T(8,128)(2,1)S(1)} %get-tuple-element.67), channel_id=1, source_target_pairs={{0,3},{1,2},{2,1},{3,0},{4,7},{5,6},{6,5},{7,4},{8,11},{9,10},{10,... | collective-permute-start | bytes 786440 | tf_op jit(solution)/shard_map/ppermute | solution.py:457
  7.1 15.3 %collective-permute-start.3 = (bf16[256,512]{1,0:T(8,128)(2,1)S(1)}, bf16[256,512]{1,0:T(8,128)(2,1)S(1)}, u32[]{:S(2)}, u32[]{:S(2)}) collective-permute-start(bf16[256,512]{1,0:T(8,128)(2,1)S(1)} %get-tuple-element.68), channel_id=1, source_target_pairs={{0,4},{1,5},{2,6},{3,7},{4,0},{5,1},{6,2},{7,3},{8,12},{9,13},{10,... | collective-permute-start | bytes 786440 | tf_op jit(solution)/shard_map/ppermute | solution.py:457
  8.9 22.9 %collective-permute-start.4 = (bf16[256,512]{1,0:T(8,128)(2,1)S(1)}, bf16[256,512]{1,0:T(8,128)(2,1)S(1)}, u32[]{:S(2)}, u32[]{:S(2)}) collective-permute-start(bf16[256,512]{1,0:T(8,128)(2,1)S(1)} %get-tuple-element.69), channel_id=1, source_target_pairs={{0,5},{1,4},{2,7},{3,6},{4,1},{5,0},{6,3},{7,2},{8,13},{9,12},{10,... | collective-permute-start | bytes 786440 | tf_op jit(solution)/shard_map/ppermute | solution.py:457
  8.9 25.2 %collective-permute-start.5 = (bf16[256,512]{1,0:T(8,128)(2,1)S(1)}, bf16[256,512]{1,0:T(8,128)(2,1)S(1)}, u32[]{:S(2)}, u32[]{:S(2)}) collective-permute-start(bf16[256,512]{1,0:T(8,128)(2,1)S(1)} %get-tuple-element.70), channel_id=1, source_target_pairs={{0,6},{1,7},{2,4},{3,5},{4,2},{5,3},{6,0},{7,1},{8,14},{9,15},{10,... | collective-permute-start | bytes 786440 | tf_op jit(solution)/shard_map/ppermute | solution.py:457
  14.2 24.0 %collective-permute-start.6 = (bf16[256,512]{1,0:T(8,128)(2,1)}, bf16[256,512]{1,0:T(8,128)(2,1)S(1)}, u32[]{:S(2)}, u32[]{:S(2)}) collective-permute-start(bf16[256,512]{1,0:T(8,128)(2,1)} %get-tuple-element.71), channel_id=1, source_target_pairs={{0,7},{1,6},{2,5},{3,4},{4,3},{5,2},{6,1},{7,0},{8,15},{9,14},{10,... | collective-permute-start | bytes 786440 | tf_op jit(solution)/shard_map/ppermute | solution.py:457
  21.0 21.0 %collective-permute-start.15 = (bf16[256,512]{1,0:T(8,128)(2,1)}, bf16[256,512]{1,0:T(8,128)(2,1)}, u32[]{:S(2)}, u32[]{:S(2)}) collective-permute-start(bf16[256,512]{1,0:T(8,128)(2,1)} %get-tuple-element.82), channel_id=1, source_target_pairs={{0,1},{1,0},{2,3},{3,2},{4,5},{5,4},{6,7},{7,6},{8,9},{9,8},{10,11... | collective-permute-start | bytes 786440 | tf_op jit(solution)/shard_map/ppermute | solution.py:457
  22.5 19.6 %collective-permute-start.16 = (bf16[256,512]{1,0:T(8,128)(2,1)}, bf16[256,512]{1,0:T(8,128)(2,1)}, u32[]{:S(2)}, u32[]{:S(2)}) collective-permute-start(bf16[256,512]{1,0:T(8,128)(2,1)} %get-tuple-element.83), channel_id=1, source_target_pairs={{0,2},{1,3},{2,0},{3,1},{4,6},{5,7},{6,4},{7,5},{8,10},{9,11},{10,... | collective-permute-start | bytes 786440 | tf_op jit(solution)/shard_map/ppermute | solution.py:457
  42.0 20.3 %collective-permute-start.19 = (bf16[256,512]{1,0:T(8,128)(2,1)}, bf16[256,512]{1,0:T(8,128)(2,1)S(1)}, u32[]{:S(2)}, u32[]{:S(2)}) collective-permute-start(bf16[256,512]{1,0:T(8,128)(2,1)} %copy-done.3), channel_id=1, source_target_pairs={{0,5},{1,4},{2,7},{3,6},{4,1},{5,0},{6,3},{7,2},{8,13},{9,12},{10,... | collective-permute-start | bytes 786440 | tf_op jit(solution)/shard_map/ppermute | solution.py:457
  42.0 25.8 %collective-permute-start.20 = (bf16[256,512]{1,0:T(8,128)(2,1)}, bf16[256,512]{1,0:T(8,128)(2,1)S(1)}, u32[]{:S(2)}, u32[]{:S(2)}) collective-permute-start(bf16[256,512]{1,0:T(8,128)(2,1)} %copy-done.2), channel_id=1, source_target_pairs={{0,6},{1,7},{2,4},{3,5},{4,2},{5,3},{6,0},{7,1},{8,14},{9,15},{10,... | collective-permute-start | bytes 786440 | tf_op jit(solution)/shard_map/ppermute | solution.py:457
  42.9 24.9 %collective-permute-start.21 = (bf16[256,512]{1,0:T(8,128)(2,1)}, bf16[256,512]{1,0:T(8,128)(2,1)S(1)}, u32[]{:S(2)}, u32[]{:S(2)}) collective-permute-start(bf16[256,512]{1,0:T(8,128)(2,1)} %copy-done.1), channel_id=1, source_target_pairs={{0,7},{1,6},{2,5},{3,4},{4,3},{5,2},{6,1},{7,0},{8,15},{9,14},{10,... | collective-permute-start | bytes 786440 | tf_op jit(solution)/shard_map/ppermute | solution.py:457
  44.9 13.2 %collective-permute-start.10 = (f32[136,256]{1,0:T(8,128)S(1)}, f32[136,256]{1,0:T(8,128)S(1)}, u32[]{:S(2)}, u32[]{:S(2)}) collective-permute-start(f32[136,256]{1,0:T(8,128)S(1)} %get-tuple-element.78), channel_id=1, source_target_pairs={{0,16},{1,17},{2,18},{3,19},{4,20},{5,21},{6,22},{7,23},{8,24},{9,... | collective-permute-start | bytes 417800 | tf_op jit(solution)/shard_map/ppermute | solution.py:457
  47.5 12.8 %collective-permute-start.11 = (f32[136,256]{1,0:T(8,128)S(1)}, f32[136,256]{1,0:T(8,128)S(1)}, u32[]{:S(2)}, u32[]{:S(2)}) collective-permute-start(f32[136,256]{1,0:T(8,128)S(1)} %get-tuple-element.79), channel_id=1, source_target_pairs={{0,24},{1,25},{2,26},{3,27},{4,28},{5,29},{6,30},{7,31},{8,16},{9,... | collective-permute-start | bytes 417800 | tf_op jit(solution)/shard_map/ppermute | solution.py:457
  88.7 16.9 %collective-permute-start.29 = (bf16[128,512]{1,0:T(8,128)(2,1)S(1)}, bf16[128,512]{1,0:T(8,128)(2,1)S(1)}, u32[]{:S(2)}, u32[]{:S(2)}) collective-permute-start(bf16[128,512]{1,0:T(8,128)(2,1)S(1)} %get-tuple-element.99), channel_id=1, source_target_pairs={{0,8},{1,9},{2,10},{3,11},{4,12},{5,13},{6,14},{7,15},{8,16},{9,17... | collective-permute-start | bytes 393224 | tf_op jit(solution)/shard_map/ppermute | solution.py:464
  105.7 13.7 %collective-permute-start.22 = (bf16[256,256]{1,0:T(8,128)(2,1)S(1)}, bf16[256,256]{1,0:T(8,128)(2,1)S(1)}, u32[]{:S(2)}, u32[]{:S(2)}) collective-permute-start(bf16[256,256]{1,0:T(8,128)(2,1)S(1)} %get-tuple-element.90), channel_id=1, source_target_pairs={{0,1},{1,0},{2,3},{3,2},{4,5},{5,4},{6,7},{7,6},{8,9},{9,8},{10,11... | collective-permute-start | bytes 393224 | tf_op jit(solution)/shard_map/ppermute | solution.py:457
  105.7 14.5 %collective-permute-start.23 = (bf16[256,256]{1,0:T(8,128)(2,1)S(1)}, bf16[256,256]{1,0:T(8,128)(2,1)S(1)}, u32[]{:S(2)}, u32[]{:S(2)}) collective-permute-start(bf16[256,256]{1,0:T(8,128)(2,1)S(1)} %get-tuple-element.91), channel_id=1, source_target_pairs={{0,2},{1,3},{2,0},{3,1},{4,6},{5,7},{6,4},{7,5},{8,10},{9,11},{10,... | collective-permute-start | bytes 393224 | tf_op jit(solution)/shard_map/ppermute | solution.py:457
  106.8 16.5 %collective-permute-start.24 = (bf16[256,256]{1,0:T(8,128)(2,1)S(1)}, bf16[256,256]{1,0:T(8,128)(2,1)S(1)}, u32[]{:S(2)}, u32[]{:S(2)}) collective-permute-start(bf16[256,256]{1,0:T(8,128)(2,1)S(1)} %get-tuple-element.92), channel_id=1, source_target_pairs={{0,3},{1,2},{2,1},{3,0},{4,7},{5,6},{6,5},{7,4},{8,11},{9,10},{10,... | collective-permute-start | bytes 393224 | tf_op jit(solution)/shard_map/ppermute | solution.py:457
  109.7 13.6 %collective-permute-start.25 = (bf16[256,256]{1,0:T(8,128)(2,1)S(1)}, bf16[256,256]{1,0:T(8,128)(2,1)S(1)}, u32[]{:S(2)}, u32[]{:S(2)}) collective-permute-start(bf16[256,256]{1,0:T(8,128)(2,1)S(1)} %get-tuple-element.93), channel_id=1, source_target_pairs={{0,4},{1,5},{2,6},{3,7},{4,0},{5,1},{6,2},{7,3},{8,12},{9,13},{10,... | collective-permute-start | bytes 393224 | tf_op jit(solution)/shard_map/ppermute | solution.py:457
  123.3 22.0 %collective-permute-start.26 = (bf16[256,256]{1,0:T(8,128)(2,1)S(1)}, bf16[256,256]{1,0:T(8,128)(2,1)S(1)}, u32[]{:S(2)}, u32[]{:S(2)}) collective-permute-start(bf16[256,256]{1,0:T(8,128)(2,1)S(1)} %get-tuple-element.94), channel_id=1, source_target_pairs={{0,5},{1,4},{2,7},{3,6},{4,1},{5,0},{6,3},{7,2},{8,13},{9,12},{10,... | collective-permute-start | bytes 393224 | tf_op jit(solution)/shard_map/ppermute | solution.py:457
  123.3 22.6 %collective-permute-start.27 = (bf16[256,256]{1,0:T(8,128)(2,1)S(1)}, bf16[256,256]{1,0:T(8,128)(2,1)S(1)}, u32[]{:S(2)}, u32[]{:S(2)}) collective-permute-start(bf16[256,256]{1,0:T(8,128)(2,1)S(1)} %get-tuple-element.95), channel_id=1, source_target_pairs={{0,6},{1,7},{2,4},{3,5},{4,2},{5,3},{6,0},{7,1},{8,14},{9,15},{10,... | collective-permute-start | bytes 393224 | tf_op jit(solution)/shard_map/ppermute | solution.py:457
  124.6 24.1 %collective-permute-start.28 = (bf16[256,256]{1,0:T(8,128)(2,1)S(1)}, bf16[256,256]{1,0:T(8,128)(2,1)S(1)}, u32[]{:S(2)}, u32[]{:S(2)}) collective-permute-start(bf16[256,256]{1,0:T(8,128)(2,1)S(1)} %get-tuple-element.96), channel_id=1, source_target_pairs={{0,7},{1,6},{2,5},{3,4},{4,3},{5,2},{6,1},{7,0},{8,15},{9,14},{10,... | collective-permute-start | bytes 393224 | tf_op jit(solution)/shard_map/ppermute | solution.py:457
  126.9 26.2 %collective-permute-start.42 = (bf16[256,512]{1,0:T(8,128)(2,1)S(1)}, bf16[256,512]{1,0:T(8,128)(2,1)S(1)}, u32[]{:S(2)}, u32[]{:S(2)}) collective-permute-start(bf16[256,512]{1,0:T(8,128)(2,1)S(1)} %get-tuple-element.112), channel_id=1, source_target_pairs={{0,6},{1,7},{2,4},{3,5},{4,2},{5,3},{6,0},{7,1},{8,14},{9,15},{10,... | collective-permute-start | bytes 786440 | tf_op jit(solution)/shard_map/ppermute | solution.py:457
  128.3 27.4 %collective-permute-start.43 = (bf16[256,512]{1,0:T(8,128)(2,1)S(1)}, bf16[256,512]{1,0:T(8,128)(2,1)S(1)}, u32[]{:S(2)}, u32[]{:S(2)}) collective-permute-start(bf16[256,512]{1,0:T(8,128)(2,1)S(1)} %get-tuple-element.113), channel_id=1, source_target_pairs={{0,7},{1,6},{2,5},{3,4},{4,3},{5,2},{6,1},{7,0},{8,15},{9,14},{10,... | collective-permute-start | bytes 786440 | tf_op jit(solution)/shard_map/ppermute | solution.py:457
  145.9 12.9 %collective-permute-start.37 = (bf16[256,512]{1,0:T(8,128)(2,1)S(1)}, bf16[256,512]{1,0:T(8,128)(2,1)S(1)}, u32[]{:S(2)}, u32[]{:S(2)}) collective-permute-start(bf16[256,512]{1,0:T(8,128)(2,1)S(1)} %get-tuple-element.107), channel_id=1, source_target_pairs={{0,1},{1,0},{2,3},{3,2},{4,5},{5,4},{6,7},{7,6},{8,9},{9,8},{10,11... | collective-permute-start | bytes 786440 | tf_op jit(solution)/shard_map/ppermute | solution.py:457
  149.1 14.2 %collective-permute-start.39 = (bf16[256,512]{1,0:T(8,128)(2,1)S(1)}, bf16[256,512]{1,0:T(8,128)(2,1)S(1)}, u32[]{:S(2)}, u32[]{:S(2)}) collective-permute-start(bf16[256,512]{1,0:T(8,128)(2,1)S(1)} %get-tuple-element.109), channel_id=1, source_target_pairs={{0,3},{1,2},{2,1},{3,0},{4,7},{5,6},{6,5},{7,4},{8,11},{9,10},{10,... | collective-permute-start | bytes 786440 | tf_op jit(solution)/shard_map/ppermute | solution.py:457
  (28 other events, 227.7 us)

commit v3 on v2

--- a/solution.py
+++ b/solution.py
@@ -38,22 +38,24 @@
     return math.prod(x.shape) * dtype.itemsize
 
 
-def call(kernel, pos, ins, outs, scratch=(), spare=4, far=""):
+def call(kernel, pos, ins, outs, scratch=(), spare=4, far="", aliases=()):
     near = pl.BlockSpec(memory_space=pltpu.VMEM)
     hbm = pl.BlockSpec(memory_space=pltpu.HBM)
     held = [x for x in scratch if hasattr(x.dtype, "itemsize")]
     if "ins" in far:
         ins = [pltpu.with_memory_space_constraint(x, pltpu.HBM) for x in ins]
     else:
-        held += ins
+        held += [x for i, x in enumerate(ins) if i not in dict(aliases)]
     if "outs" not in far:
         held += outs
     return pl.pallas_call(
         kernel,
-        in_specs=[pl.BlockSpec(memory_space=pltpu.SMEM)] + [hbm if "ins" in far else near] * len(ins),
+        in_specs=[pl.BlockSpec(memory_space=pltpu.SMEM)]
+        + [hbm if "ins" in far or i in dict(aliases) else near for i in range(len(ins))],
         out_specs=[hbm if "outs" in far else near] * len(outs),
         out_shape=list(outs),
         scratch_shapes=list(scratch),
+        input_output_aliases={i + 1: o for i, o in aliases},
         compiler_params=pltpu.CompilerParams(
             vmem_limit_bytes=sum(map(size_of, held)) + spare * 2**20
         ),
@@ -116,11 +118,16 @@
         copy.wait()
 
 
-def unpack_pair_kernel(plan, pos, *refs):
-    ins, proj_ref, (a_ref, b_ref, out_ref, sems) = refs[: plan.inner], refs[plan.inner], refs[plan.inner + 1 :]
+def unpack_pair_kernel(plan, which, last, pos, *refs):
+    ins, refs = refs[: len(which)], refs[len(which) :]
+    moves = []
+    if last:
+        proj_ref, _, _, a_ref, b_ref, out_ref, sems = refs
+        moves.append((proj_ref, out_ref))
+    else:
+        a_ref, b_ref, sems = refs
     hd = plan.head_size
-    moves = [(proj_ref, out_ref)]
-    for k, src in enumerate(ins):
+    for k, src in zip(which, ins):
         for h in range(plan.heads):
             cols = head_slices(plan, pos[1] ^ k, h)
             moves.append((src.at[:, pl.ds(2 * h * hd, hd)], a_ref.at[:, cols]))
@@ -557,7 +564,10 @@
     dbar_parts = exchange(dbar_send, devices, inner)
     wg_from_before, wg_from_after = swap_edges(wg_after, wg_before, devices, inner)
     (dbar_half,) = call(
-        bind(combine_grad_kernel), pos, [bar_full, *dbar_parts], [struct((heads * rows + DOT_ROWS, pair), BF)]
+        bind(combine_grad_kernel),
+        pos,
+        [bar_full, *dbar_parts],
+        [struct((heads * rows + DOT_ROWS, pair), BF)],
     )
     dbars = exchange([dbar_half] * outer, devices, inner)
     dq_pieces = [None] * inner
@@ -593,13 +603,24 @@
     (grad_queries,) = call(
         bind(unpack_kernel), pos, dq_pieces, [whole], [pltpu.SemaphoreType.DMA((inner,))], far="outs"
     )
+    sooner, later = waves[2] + waves[0], waves[1]
+    grads = call(
+        bind(unpack_pair_kernel, sooner, False),
+        pos,
+        [dkv_pieces[k] for k in sooner],
+        [whole, whole],
+        [pltpu.SemaphoreType.DMA((2 * len(sooner) * heads,))],
+        far="outs",
+    )
+    count = len(later)
     grad_keys, grad_values, grad_proj = call(
-        bind(unpack_pair_kernel),
-        pos,
-        [*dkv_pieces, proj_here],
+        bind(unpack_pair_kernel, later, True),
+        pos,
+        [*(dkv_pieces[k] for k in later), proj_here, *grads],
         [whole, whole, struct(proj_here.shape, FL)],
-        [pltpu.SemaphoreType.DMA((2 * inner * heads + 1,))],
+        [pltpu.SemaphoreType.DMA((2 * count * heads + 1,))],
         far="outs",
+        aliases=((count + 1, 0), (count + 2, 1)),
     )
     return (grad_queries, grad_keys, grad_values, grad_proj)
 
@@ -607,4 +628,6 @@
 def solution(mesh):
     in_specs = (P("seq", None), P("seq", None), P("seq", None), P("seq", None), P())
     out_specs = (P("seq", None), P("seq", None), P("seq", None), P("seq", None))
-    return jax.shard_map(per_device, mesh=mesh, in_specs=in_specs, out_specs=out_specs, check_vma=False)
+    return jax.shard_map(
+        per_device, mesh=mesh, in_specs=in_specs, out_specs=out_specs, check_vma=False
+    )

time: 171 us -> 160 us (0.936)
  starting transfers between devices: 70.4 us -> 62.5 us
  waiting for transfers between devices: 58.2 us -> 53.8 us
    ppermute x43, starting transfers between devices: 62.9 us -> 55.1 us  [exchange(): out.append(lax.ppermute(field, 'seq', flip) if k else field)]
    ppermute x43, waiting for transfers between devices: 58.1 us -> 53.8 us  [exchange(): out.append(lax.ppermute(field, 'seq', flip) if k else field)]
    pallas_call x13 -> x14, Pallas kernels: 38.9 us -> 40.1 us  [call(): pl.pallas_call(kernel, in_specs=[pl.BlockSpec(memory_space=pltpu.SMEM)] +...]
  transfers between devices with their start and end apart: 48 -> 48, of which waited for: 12 -> 13; matrix products, arithmetic and copies ran while one was open for 0% -> 0% of each run, Pallas kernels for 11% -> 12%
where the time goes in v3:
time: 160 us
  starting transfers between devices  62.5 us (39%)
  waiting for transfers between devices  53.8 us (34%)
  Pallas kernels  40.1 us (25%)
  local copies, waits for them, and re-layouts  2.16 us (1%)
    ppermute x43, starting transfers between devices, exchange(): out.append(lax.ppermute(field, 'seq', flip) if k else field)  55.1 us
    ppermute x43, waiting for transfers between devices, exchange(): out.append(lax.ppermute(field, 'seq', flip) if k else field)  53.8 us
    pallas_call x14, Pallas kernels, call(): pl.pallas_call(kernel, in_specs=[pl.BlockSpec(memory_space=pltpu.SMEM)] +...  40.1 us
    ppermute x2, starting transfers between devices, swap_edges(): lax.ppermute(upward, 'seq', up)  4.24 us
  transfers between devices with their start and end apart: 48, of which 13 were waited for; matrix products, arithmetic and copies ran while one was open for 0% of the time, Pallas kernels for 12%

profile of v3, /device:TPU:0, one launch (start us, length us, event | category | flops | bytes accessed | tf_op | source)
XLA Modules:
  0.0 159.8 jit_solution(17413906544695108710)
XLA Ops:
  0.7 3.2 %shard_map.84 = (bf16[256,512]{1,0:T(8,128)(2,1)S(1)}, bf16[256,512]{1,0:T(8,128)(2,1)S(1)}, bf16[256,512]{1,0:T(8,128)(2,1)S(1)}, bf16[256,512]{1,0:T(8,128)(2,...) custom-call(s32[2]{0:T(128)S(1)} %pad_add_fusion.pos_ref, ...), custom_call_target="tpu_custom_call" | custom-call | tf_op jit(solution)/shard_map/pallas_call | solution.py:51
  4.5 2.6 %collective-permute-start.1 = (bf16[256,512]{1,0:T(8,128)(2,1)S(1)}, bf16[256,512]{1,0:T(8,128)(2,1)S(1)}, u32[]{:S(2)}, u32[]{:S(2)}) collective-permute-start(bf16[256,512]{1,0:T(8,128)(2,1)S(1)} %get-tuple-element.68), channel_id=1, source_target_pairs={{0,2},{1,3},{2,0},{3,1},{4,6},{5,7},{6,4},{7,5},{8,10},{9,11},{10,... | collective-permute-start | bytes 786440 | tf_op jit(solution)/shard_map/ppermute | solution.py:464
  8.9 2.6 %collective-permute-start.5 = (bf16[256,512]{1,0:T(8,128)(2,1)S(1)}, bf16[256,512]{1,0:T(8,128)(2,1)S(1)}, u32[]{:S(2)}, u32[]{:S(2)}) collective-permute-start(bf16[256,512]{1,0:T(8,128)(2,1)S(1)} %get-tuple-element.72), channel_id=1, source_target_pairs={{0,6},{1,7},{2,4},{3,5},{4,2},{5,3},{6,0},{7,1},{8,14},{9,15},{10,... | collective-permute-start | bytes 786440 | tf_op jit(solution)/shard_map/ppermute | solution.py:464
  11.5 2.7 %collective-permute-done.1.refs_2_.refs_0_ = bf16[256,512]{1,0:T(8,128)(2,1)S(1)} collective-permute-done((bf16[256,512]{1,0:T(8,128)(2,1)S(1)}, bf16[256,512]{1,0:T(8,128)(2,1)S(1)}, u32[]{:S(2)}, u32[]{:S(2)}) %collective-permute-start.1) | collective-permute-done | bytes 262176 | tf_op jit(solution)/shard_map/ppermute | solution.py:464
  15.9 3.0 %shard_map.88 = (bf16[256,512]{1,0:T(8,128)(2,1)S(1)}, bf16[256,512]{1,0:T(8,128)(2,1)}, bf16[256,512]{1,0:T(8,128)(2,1)}, bf16[256,512]{1,0:T(8,128)(2,1)}, bf1...) custom-call(s32[2]{0:T(128)S(1)} %pad_add_fusion.pos_ref, ...), custom_call_target="tpu_custom_call" | custom-call | tf_op jit(solution)/shard_map/pallas_call | solution.py:51
  23.0 8.8 %collective-permute-done.4.refs_5_.refs_3_ = bf16[256,512]{1,0:T(8,128)(2,1)S(1)} collective-permute-done((bf16[256,512]{1,0:T(8,128)(2,1)S(1)}, bf16[256,512]{1,0:T(8,128)(2,1)S(1)}, u32[]{:S(2)}, u32[]{:S(2)}) %collective-permute-start.4) | collective-permute-done | bytes 262176 | tf_op jit(solution)/shard_map/ppermute | solution.py:464
  31.8 2.3 %collective-permute-start.17 = (bf16[256,512]{1,0:T(8,128)(2,1)}, bf16[256,512]{1,0:T(8,128)(2,1)}, u32[]{:S(2)}, u32[]{:S(2)}) collective-permute-start(bf16[256,512]{1,0:T(8,128)(2,1)} %get-tuple-element.86), channel_id=1, source_target_pairs={{0,3},{1,2},{2,1},{3,0},{4,7},{5,6},{6,5},{7,4},{8,11},{9,10},{10,... | collective-permute-start | bytes 786440 | tf_op jit(solution)/shard_map/ppermute | solution.py:464
  35.7 2.5 %shard_map.85 = (f32[2,256,256]{2,1,0:T(8,128)S(1)}, f32[8,256]{1,0:T(8,128)S(1)}) custom-call(s32[2]{0:T(128)S(1)} %pad_add_fusion.pos_ref, bf16[256,512]{1,0:T(8,128)(2,1)S(1)} %get-tuple-element.66.refs_0_, bf16[256,512]{1,0:T(8,128)(2,1)S(1)} %collective-permute-done.refs_1_, bf16[256,512]{1,0:T(8,128)(2,1)S(1)} %collective-permute-done.1.refs_2_.refs_0_, ...), custom_call_target="tpu_custom_call" | custom-call | tf_op jit(solution)/shard_map/pallas_call | solution.py:51
  38.2 2.1 %shard_map.86 = (bf16[128,512]{1,0:T(8,128)(2,1)S(1)}, bf16[128,512]{1,0:T(8,128)(2,1)S(1)}, f32[136,256]{1,0:T(8,128)S(1)}, f32[136,256]{1,0:T(8,128)S(1)}, f32...) custom-call(s32[2]{0:T(128)S(1)} %pad_add_fusion.pos_ref, bf16[256,512]{1,0:T(8,128)(2,1)S(1)} %get-tuple-element.66.refs_0_, ...), custom_call_target="tpu_custom_call" | custom-call | tf_op jit(solution)/shard_map/pallas_call | solution.py:51
  44.9 2.6 %collective-permute-start.10 = (f32[136,256]{1,0:T(8,128)S(1)}, f32[136,256]{1,0:T(8,128)S(1)}, u32[]{:S(2)}, u32[]{:S(2)}) collective-permute-start(f32[136,256]{1,0:T(8,128)S(1)} %get-tuple-element.80), channel_id=1, source_target_pairs={{0,16},{1,17},{2,18},{3,19},{4,20},{5,21},{6,22},{7,23},{8,24},{9,... | collective-permute-start | bytes 417800 | tf_op jit(solution)/shard_map/ppermute | solution.py:464
  49.1 9.0 %collective-permute-done.10.refs_2_ = f32[136,256]{1,0:T(8,128)S(1)} collective-permute-done((f32[136,256]{1,0:T(8,128)S(1)}, f32[136,256]{1,0:T(8,128)S(1)}, u32[]{:S(2)}, u32[]{:S(2)}) %collective-permute-start.10) | collective-permute-done | bytes 139296 | tf_op jit(solution)/shard_map/ppermute | solution.py:464
  58.0 2.2 %collective-permute-start.7 = (bf16[128,512]{1,0:T(8,128)(2,1)S(1)}, bf16[128,512]{1,0:T(8,128)(2,1)S(1)}, u32[]{:S(2)}, u32[]{:S(2)}) collective-permute-start(bf16[128,512]{1,0:T(8,128)(2,1)S(1)} %get-tuple-element.76), channel_id=1, source_target_pairs={{0,8},{1,9},{2,10},{3,11},{4,12},{5,13},{6,14},{7,15},{8,16},{9,17... | collective-permute-start | bytes 393224 | tf_op jit(solution)/shard_map/ppermute | solution.py:471
  62.3 5.5 %collective-permute-start.14 = (bf16[128,256]{1,0:T(8,128)(2,1)S(1)}, bf16[128,256]{1,0:T(8,128)(2,1)S(1)}, u32[]{:S(2)}, u32[]{:S(2)}) collective-permute-start(bf16[128,256]{1,0:T(8,128)(2,1)S(1)} %get-tuple-element.82.refs_10_), channel_id=1, source_target_pairs={{0,24},{1,25},{2,26},{3,27},{4,28},{5,29},{6,30},{7,31},{8,16},{9,... | collective-permute-start | bytes 196616 | tf_op jit(solution)/shard_map/ppermute | solution.py:464
  68.5 3.2 %collective-permute-done.14.refs_13_ = bf16[128,256]{1,0:T(8,128)(2,1)S(1)} collective-permute-done((bf16[128,256]{1,0:T(8,128)(2,1)S(1)}, bf16[128,256]{1,0:T(8,128)(2,1)S(1)}, u32[]{:S(2)}, u32[]{:S(2)}) %collective-permute-start.14) | collective-permute-done | bytes 65568 | tf_op jit(solution)/shard_map/ppermute | solution.py:464
  73.4 15.3 %shard_map.89 = (bf16[256,256]{1,0:T(8,128)(2,1)S(1)}, bf16[256,256]{1,0:T(8,128)(2,1)S(1)}, bf16[256,256]{1,0:T(8,128)(2,1)S(1)}, bf16[256,256]{1,0:T(8,128)(2,...) custom-call(s32[2]{0:T(128)S(1)} %pad_add_fusion.pos_ref, ...), custom_call_target="tpu_custom_call" | custom-call | tf_op jit(solution)/shard_map/pallas_call | solution.py:51
  92.9 2.4 %collective-permute-start.33 = (bf16[128,256]{1,0:T(8,128)(2,1)S(1)}, bf16[128,256]{1,0:T(8,128)(2,1)S(1)}, u32[]{:S(2)}, u32[]{:S(2)}) collective-permute-start(bf16[128,256]{1,0:T(8,128)(2,1)S(1)} %get-tuple-element.107), channel_id=1, source_target_pairs={{0,24},{1,25},{2,26},{3,27},{4,28},{5,29},{6,30},{7,31},{8,16},{9,... | collective-permute-start | bytes 196616 | tf_op jit(solution)/shard_map/ppermute | solution.py:464
  96.6 3.3 %collective-permute-done.32.refs_3_ = bf16[128,256]{1,0:T(8,128)(2,1)S(1)} collective-permute-done((bf16[128,256]{1,0:T(8,128)(2,1)S(1)}, bf16[128,256]{1,0:T(8,128)(2,1)S(1)}, u32[]{:S(2)}, u32[]{:S(2)}) %collective-permute-start.32) | collective-permute-done | bytes 65568 | tf_op jit(solution)/shard_map/ppermute | solution.py:464
  102.3 3.4 %collective-permute-start.35 = (bf16[144,256]{1,0:T(8,128)(2,1)S(1)}, bf16[144,256]{1,0:T(8,128)(2,1)S(1)}, u32[]{:S(2)}, u32[]{:S(2)}) collective-permute-start(bf16[144,256]{1,0:T(8,128)(2,1)S(1)} %shard_map.91.refs_9_.refs_7_), channel_id=1, source_target_pairs={{0,16},{1,17},{2,18},{3,19},{4,20},{5,21},{6,22},{7,23},{8,24},{9,... | collective-permute-start | bytes 221192 | tf_op jit(solution)/shard_map/ppermute | solution.py:464
  119.6 3.1 %shard_map.92 = (bf16[256,512]{1,0:T(8,128)(2,1)S(1)}, bf16[256,512]{1,0:T(8,128)(2,1)S(1)}, bf16[256,512]{1,0:T(8,128)(2,1)S(1)}, bf16[256,512]{1,0:T(8,128)(2,1)S(1)}, bf16[1024,512]{1,0:T(8,128)(2,1)S(1)}) custom-call(s32[2]{0:T(128)S(1)} %pad_add_fusion.pos_ref, bf16[256,512]{1,0:T(8,128)(2,1)S(1)} %collective-permute-done.1.refs_2_.refs_0_, ...), custom_call_target="tpu_custom_call" | custom-call | tf_op jit(solution)/shard_map/pallas_call | solution.py:51
  123.8 9.1 %collective-permute-done.26.refs_5_ = bf16[256,256]{1,0:T(8,128)(2,1)S(1)} collective-permute-done((bf16[256,256]{1,0:T(8,128)(2,1)S(1)}, bf16[256,256]{1,0:T(8,128)(2,1)S(1)}, u32[]{:S(2)}, u32[]{:S(2)}) %collective-permute-start.26) | collective-permute-done | bytes 131104 | tf_op jit(solution)/shard_map/ppermute | solution.py:464
  134.1 3.1 %collective-permute-start.43 = (f32[64,256]{1,0:T(8,128)S(1)}, f32[64,256]{1,0:T(8,128)S(1)}, u32[]{:S(2)}, u32[]{:S(2)}) collective-permute-start(f32[64,256]{1,0:T(8,128)S(1)} %get-tuple-element.118), channel_id=1, source_target_pairs={{0,24},{1,25},{2,26},{3,27},{4,28},{5,29},{6,30},{7,31},{8,16},{9,... | collective-permute-start | bytes 196616 | tf_op jit(solution)/shard_map/ppermute | solution.py:464
  137.8 3.7 %collective-permute-done.42 = f32[64,256]{1,0:T(8,128)S(1)} collective-permute-done((f32[64,256]{1,0:T(8,128)S(1)}, f32[64,256]{1,0:T(8,128)S(1)}, u32[]{:S(2)}, u32[]{:S(2)}) %collective-permute-start.42) | collective-permute-done | bytes 65568 | tf_op jit(solution)/shard_map/ppermute | solution.py:464
  145.1 2.1 %collective-permute-done.47.refs_3_ = bf16[256,512]{1,0:T(8,128)(2,1)S(1)} collective-permute-done((bf16[256,512]{1,0:T(8,128)(2,1)S(1)}, bf16[256,512]{1,0:T(8,128)(2,1)S(1)}, u32[]{:S(2)}, u32[]{:S(2)}) %collective-permute-start.47) | collective-permute-done | bytes 262176 | tf_op jit(solution)/shard_map/ppermute | solution.py:464
  151.1 6.9 %collective-permute-done.38.refs_1_ = bf16[256,512]{1,0:T(8,128)(2,1)S(1)} collective-permute-done((bf16[256,512]{1,0:T(8,128)(2,1)S(1)}, bf16[256,512]{1,0:T(8,128)(2,1)S(1)}, u32[]{:S(2)}, u32[]{:S(2)}) %collective-permute-start.38) | collective-permute-done | bytes 262176 | tf_op jit(solution)/shard_map/ppermute | solution.py:464
  (97 shorter events, 53.9 us)
Async XLA Ops:
  7.1 13.9 %collective-permute-start.2 = (bf16[256,512]{1,0:T(8,128)(2,1)S(1)}, bf16[256,512]{1,0:T(8,128)(2,1)S(1)}, u32[]{:S(2)}, u32[]{:S(2)}) collective-permute-start(bf16[256,512]{1,0:T(8,128)(2,1)S(1)} %get-tuple-element.69), channel_id=1, source_target_pairs={{0,3},{1,2},{2,1},{3,0},{4,7},{5,6},{6,5},{7,4},{8,11},{9,10},{10,... | collective-permute-start | bytes 786440 | tf_op jit(solution)/shard_map/ppermute | solution.py:464
  7.1 15.3 %collective-permute-start.3 = (bf16[256,512]{1,0:T(8,128)(2,1)S(1)}, bf16[256,512]{1,0:T(8,128)(2,1)S(1)}, u32[]{:S(2)}, u32[]{:S(2)}) collective-permute-start(bf16[256,512]{1,0:T(8,128)(2,1)S(1)} %get-tuple-element.70), channel_id=1, source_target_pairs={{0,4},{1,5},{2,6},{3,7},{4,0},{5,1},{6,2},{7,3},{8,12},{9,13},{10,... | collective-permute-start | bytes 786440 | tf_op jit(solution)/shard_map/ppermute | solution.py:464
  8.9 22.9 %collective-permute-start.4 = (bf16[256,512]{1,0:T(8,128)(2,1)S(1)}, bf16[256,512]{1,0:T(8,128)(2,1)S(1)}, u32[]{:S(2)}, u32[]{:S(2)}) collective-permute-start(bf16[256,512]{1,0:T(8,128)(2,1)S(1)} %get-tuple-element.71), channel_id=1, source_target_pairs={{0,5},{1,4},{2,7},{3,6},{4,1},{5,0},{6,3},{7,2},{8,13},{9,12},{10,... | collective-permute-start | bytes 786440 | tf_op jit(solution)/shard_map/ppermute | solution.py:464
  8.9 25.2 %collective-permute-start.5 = (bf16[256,512]{1,0:T(8,128)(2,1)S(1)}, bf16[256,512]{1,0:T(8,128)(2,1)S(1)}, u32[]{:S(2)}, u32[]{:S(2)}) collective-permute-start(bf16[256,512]{1,0:T(8,128)(2,1)S(1)} %get-tuple-element.72), channel_id=1, source_target_pairs={{0,6},{1,7},{2,4},{3,5},{4,2},{5,3},{6,0},{7,1},{8,14},{9,15},{10,... | collective-permute-start | bytes 786440 | tf_op jit(solution)/shard_map/ppermute | solution.py:464
  14.2 24.0 %collective-permute-start.6 = (bf16[256,512]{1,0:T(8,128)(2,1)}, bf16[256,512]{1,0:T(8,128)(2,1)S(1)}, u32[]{:S(2)}, u32[]{:S(2)}) collective-permute-start(bf16[256,512]{1,0:T(8,128)(2,1)} %get-tuple-element.73), channel_id=1, source_target_pairs={{0,7},{1,6},{2,5},{3,4},{4,3},{5,2},{6,1},{7,0},{8,15},{9,14},{10,... | collective-permute-start | bytes 786440 | tf_op jit(solution)/shard_map/ppermute | solution.py:464
  21.0 21.0 %collective-permute-start.15 = (bf16[256,512]{1,0:T(8,128)(2,1)}, bf16[256,512]{1,0:T(8,128)(2,1)}, u32[]{:S(2)}, u32[]{:S(2)}) collective-permute-start(bf16[256,512]{1,0:T(8,128)(2,1)} %get-tuple-element.84), channel_id=1, source_target_pairs={{0,1},{1,0},{2,3},{3,2},{4,5},{5,4},{6,7},{7,6},{8,9},{9,8},{10,11... | collective-permute-start | bytes 786440 | tf_op jit(solution)/shard_map/ppermute | solution.py:464
  22.5 19.6 %collective-permute-start.16 = (bf16[256,512]{1,0:T(8,128)(2,1)}, bf16[256,512]{1,0:T(8,128)(2,1)}, u32[]{:S(2)}, u32[]{:S(2)}) collective-permute-start(bf16[256,512]{1,0:T(8,128)(2,1)} %get-tuple-element.85), channel_id=1, source_target_pairs={{0,2},{1,3},{2,0},{3,1},{4,6},{5,7},{6,4},{7,5},{8,10},{9,11},{10,... | collective-permute-start | bytes 786440 | tf_op jit(solution)/shard_map/ppermute | solution.py:464
  31.8 11.1 %collective-permute-start.17 = (bf16[256,512]{1,0:T(8,128)(2,1)}, bf16[256,512]{1,0:T(8,128)(2,1)}, u32[]{:S(2)}, u32[]{:S(2)}) collective-permute-start(bf16[256,512]{1,0:T(8,128)(2,1)} %get-tuple-element.86), channel_id=1, source_target_pairs={{0,3},{1,2},{2,1},{3,0},{4,7},{5,6},{6,5},{7,4},{8,11},{9,10},{10,... | collective-permute-start | bytes 786440 | tf_op jit(solution)/shard_map/ppermute | solution.py:464
  34.1 10.8 %collective-permute-start.18 = (bf16[256,512]{1,0:T(8,128)(2,1)}, bf16[256,512]{1,0:T(8,128)(2,1)}, u32[]{:S(2)}, u32[]{:S(2)}) collective-permute-start(bf16[256,512]{1,0:T(8,128)(2,1)} %get-tuple-element.87), channel_id=1, source_target_pairs={{0,4},{1,5},{2,6},{3,7},{4,0},{5,1},{6,2},{7,3},{8,12},{9,13},{10,... | collective-permute-start | bytes 786440 | tf_op jit(solution)/shard_map/ppermute | solution.py:464
  42.0 20.3 %collective-permute-start.19 = (bf16[256,512]{1,0:T(8,128)(2,1)}, bf16[256,512]{1,0:T(8,128)(2,1)S(1)}, u32[]{:S(2)}, u32[]{:S(2)}) collective-permute-start(bf16[256,512]{1,0:T(8,128)(2,1)} %copy-done.3), channel_id=1, source_target_pairs={{0,5},{1,4},{2,7},{3,6},{4,1},{5,0},{6,3},{7,2},{8,13},{9,12},{10,... | collective-permute-start | bytes 786440 | tf_op jit(solution)/shard_map/ppermute | solution.py:464
  42.0 25.8 %collective-permute-start.20 = (bf16[256,512]{1,0:T(8,128)(2,1)}, bf16[256,512]{1,0:T(8,128)(2,1)S(1)}, u32[]{:S(2)}, u32[]{:S(2)}) collective-permute-start(bf16[256,512]{1,0:T(8,128)(2,1)} %copy-done.2), channel_id=1, source_target_pairs={{0,6},{1,7},{2,4},{3,5},{4,2},{5,3},{6,0},{7,1},{8,14},{9,15},{10,... | collective-permute-start | bytes 786440 | tf_op jit(solution)/shard_map/ppermute | solution.py:464
  42.9 24.9 %collective-permute-start.21 = (bf16[256,512]{1,0:T(8,128)(2,1)}, bf16[256,512]{1,0:T(8,128)(2,1)S(1)}, u32[]{:S(2)}, u32[]{:S(2)}) collective-permute-start(bf16[256,512]{1,0:T(8,128)(2,1)} %copy-done.1), channel_id=1, source_target_pairs={{0,7},{1,6},{2,5},{3,4},{4,3},{5,2},{6,1},{7,0},{8,15},{9,14},{10,... | collective-permute-start | bytes 786440 | tf_op jit(solution)/shard_map/ppermute | solution.py:464
  44.9 13.2 %collective-permute-start.10 = (f32[136,256]{1,0:T(8,128)S(1)}, f32[136,256]{1,0:T(8,128)S(1)}, u32[]{:S(2)}, u32[]{:S(2)}) collective-permute-start(f32[136,256]{1,0:T(8,128)S(1)} %get-tuple-element.80), channel_id=1, source_target_pairs={{0,16},{1,17},{2,18},{3,19},{4,20},{5,21},{6,22},{7,23},{8,24},{9,... | collective-permute-start | bytes 417800 | tf_op jit(solution)/shard_map/ppermute | solution.py:464
  47.5 12.8 %collective-permute-start.11 = (f32[136,256]{1,0:T(8,128)S(1)}, f32[136,256]{1,0:T(8,128)S(1)}, u32[]{:S(2)}, u32[]{:S(2)}) collective-permute-start(f32[136,256]{1,0:T(8,128)S(1)} %get-tuple-element.81), channel_id=1, source_target_pairs={{0,24},{1,25},{2,26},{3,27},{4,28},{5,29},{6,30},{7,31},{8,16},{9,... | collective-permute-start | bytes 417800 | tf_op jit(solution)/shard_map/ppermute | solution.py:464
  88.7 16.9 %collective-permute-start.29 = (bf16[128,512]{1,0:T(8,128)(2,1)S(1)}, bf16[128,512]{1,0:T(8,128)(2,1)S(1)}, u32[]{:S(2)}, u32[]{:S(2)}) collective-permute-start(bf16[128,512]{1,0:T(8,128)(2,1)S(1)} %get-tuple-element.101), channel_id=1, source_target_pairs={{0,8},{1,9},{2,10},{3,11},{4,12},{5,13},{6,14},{7,15},{8,16},{9,17... | collective-permute-start | bytes 393224 | tf_op jit(solution)/shard_map/ppermute | solution.py:471
  95.3 10.9 %collective-permute-start.30 = (bf16[128,512]{1,0:T(8,128)(2,1)S(1)}, bf16[128,512]{1,0:T(8,128)(2,1)S(1)}, u32[]{:S(2)}, u32[]{:S(2)}) collective-permute-start(bf16[128,512]{1,0:T(8,128)(2,1)S(1)} %get-tuple-element.102), channel_id=1, source_target_pairs={{8,0},{9,1},{10,2},{11,3},{12,4},{13,5},{14,6},{15,7},{16,8},{17,9... | collective-permute-start | bytes 393224 | tf_op jit(solution)/shard_map/ppermute | solution.py:471
  112.9 29.4 %collective-permute-start.45 = (bf16[256,512]{1,0:T(8,128)(2,1)S(1)}, bf16[256,512]{1,0:T(8,128)(2,1)S(1)}, u32[]{:S(2)}, u32[]{:S(2)}) collective-permute-start(bf16[256,512]{1,0:T(8,128)(2,1)S(1)} %get-tuple-element.120), channel_id=1, source_target_pairs={{0,1},{1,0},{2,3},{3,2},{4,5},{5,4},{6,7},{7,6},{8,9},{9,8},{10,11... | collective-permute-start | bytes 786440 | tf_op jit(solution)/shard_map/ppermute | solution.py:464
  114.8 28.7 %collective-permute-start.46 = (bf16[256,512]{1,0:T(8,128)(2,1)S(1)}, bf16[256,512]{1,0:T(8,128)(2,1)S(1)}, u32[]{:S(2)}, u32[]{:S(2)}) collective-permute-start(bf16[256,512]{1,0:T(8,128)(2,1)S(1)} %get-tuple-element.121), channel_id=1, source_target_pairs={{0,6},{1,7},{2,4},{3,5},{4,2},{5,3},{6,0},{7,1},{8,14},{9,15},{10,... | collective-permute-start | bytes 786440 | tf_op jit(solution)/shard_map/ppermute | solution.py:464
  116.0 16.8 %collective-permute-start.26 = (bf16[256,256]{1,0:T(8,128)(2,1)S(1)}, bf16[256,256]{1,0:T(8,128)(2,1)S(1)}, u32[]{:S(2)}, u32[]{:S(2)}) collective-permute-start(bf16[256,256]{1,0:T(8,128)(2,1)S(1)} %get-tuple-element.96), channel_id=1, source_target_pairs={{0,5},{1,4},{2,7},{3,6},{4,1},{5,0},{6,3},{7,2},{8,13},{9,12},{10,... | collective-permute-start | bytes 393224 | tf_op jit(solution)/shard_map/ppermute | solution.py:464
  117.1 16.2 %collective-permute-start.27 = (bf16[256,256]{1,0:T(8,128)(2,1)S(1)}, bf16[256,256]{1,0:T(8,128)(2,1)S(1)}, u32[]{:S(2)}, u32[]{:S(2)}) collective-permute-start(bf16[256,256]{1,0:T(8,128)(2,1)S(1)} %get-tuple-element.97), channel_id=1, source_target_pairs={{0,6},{1,7},{2,4},{3,5},{4,2},{5,3},{6,0},{7,1},{8,14},{9,15},{10,... | collective-permute-start | bytes 393224 | tf_op jit(solution)/shard_map/ppermute | solution.py:464
  118.3 15.8 %collective-permute-start.28 = (bf16[256,256]{1,0:T(8,128)(2,1)S(1)}, bf16[256,256]{1,0:T(8,128)(2,1)S(1)}, u32[]{:S(2)}, u32[]{:S(2)}) collective-permute-start(bf16[256,256]{1,0:T(8,128)(2,1)S(1)} %get-tuple-element.98), channel_id=1, source_target_pairs={{0,7},{1,6},{2,5},{3,4},{4,3},{5,2},{6,1},{7,0},{8,15},{9,14},{10,... | collective-permute-start | bytes 393224 | tf_op jit(solution)/shard_map/ppermute | solution.py:464
  142.3 15.7 %collective-permute-start.38 = (bf16[256,512]{1,0:T(8,128)(2,1)S(1)}, bf16[256,512]{1,0:T(8,128)(2,1)S(1)}, u32[]{:S(2)}, u32[]{:S(2)}) collective-permute-start(bf16[256,512]{1,0:T(8,128)(2,1)S(1)} %get-tuple-element.109), channel_id=1, source_target_pairs={{0,3},{1,2},{2,1},{3,0},{4,7},{5,6},{6,5},{7,4},{8,11},{9,10},{10,... | collective-permute-start | bytes 786440 | tf_op jit(solution)/shard_map/ppermute | solution.py:464
  142.3 15.6 %collective-permute-start.39 = (bf16[256,512]{1,0:T(8,128)(2,1)S(1)}, bf16[256,512]{1,0:T(8,128)(2,1)S(1)}, u32[]{:S(2)}, u32[]{:S(2)}) collective-permute-start(bf16[256,512]{1,0:T(8,128)(2,1)S(1)} %get-tuple-element.110), channel_id=1, source_target_pairs={{0,4},{1,5},{2,6},{3,7},{4,0},{5,1},{6,2},{7,3},{8,12},{9,13},{10,... | collective-permute-start | bytes 786440 | tf_op jit(solution)/shard_map/ppermute | solution.py:464
  143.5 14.5 %collective-permute-start.40 = (bf16[256,512]{1,0:T(8,128)(2,1)S(1)}, bf16[256,512]{1,0:T(8,128)(2,1)S(1)}, u32[]{:S(2)}, u32[]{:S(2)}) collective-permute-start(bf16[256,512]{1,0:T(8,128)(2,1)S(1)} %get-tuple-element.111), channel_id=1, source_target_pairs={{0,5},{1,4},{2,7},{3,6},{4,1},{5,0},{6,3},{7,2},{8,13},{9,12},{10,... | collective-permute-start | bytes 786440 | tf_op jit(solution)/shard_map/ppermute | solution.py:464
  (28 other events, 219.1 us)

commit v4 on v3

--- a/solution.py
+++ b/solution.py
@@ -122,8 +122,12 @@
     ins, refs = refs[: len(which)], refs[len(which) :]
     moves = []
     if last:
-        proj_ref, _, _, a_ref, b_ref, out_ref, sems = refs
-        moves.append((proj_ref, out_ref))
+        parts, (_, _, a_ref, b_ref, out_ref, sems, sum_ref) = refs[: plan.outer], refs[plan.outer :]
+        total = parts[0][...]
+        for part in parts[1:]:
+            total = total + part[...]
+        sum_ref[...] = total
+        moves.append((sum_ref, out_ref))
     else:
         a_ref, b_ref, sems = refs
     hd = plan.head_size
@@ -593,12 +597,10 @@
         [struct((heads * head_size // outer, rank), FL)] * outer,
         [pltpu.VMEM((heads * head_size, rank), FL)],
     )
-    proj_parts = exchange(proj_send, devices, inner)
-    proj_sum = proj_parts[0]
-    for part in proj_parts[1:]:
-        proj_sum = proj_sum + part
-    place = [(o * inner + p, p * outer + o) for o in range(outer) for p in range(inner)]
-    proj_here = lax.ppermute(proj_sum, "seq", place)
+    proj_parts = []
+    for k in range(outer):
+        place = [(o * inner + p, p * outer + (o ^ k)) for o in range(outer) for p in range(inner)]
+        proj_parts.append(lax.ppermute(proj_send[k], "seq", place))
     whole = struct((tokens_here, row_width), BF)
     (grad_queries,) = call(
         bind(unpack_kernel), pos, dq_pieces, [whole], [pltpu.SemaphoreType.DMA((inner,))], far="outs"
@@ -616,11 +618,11 @@
     grad_keys, grad_values, grad_proj = call(
         bind(unpack_pair_kernel, later, True),
         pos,
-        [*(dkv_pieces[k] for k in later), proj_here, *grads],
-        [whole, whole, struct(proj_here.shape, FL)],
-        [pltpu.SemaphoreType.DMA((2 * count * heads + 1,))],
+        [*(dkv_pieces[k] for k in later), *proj_parts, *grads],
+        [whole, whole, struct(proj_parts[0].shape, FL)],
+        [pltpu.SemaphoreType.DMA((2 * count * heads + 1,)), pltpu.VMEM(proj_parts[0].shape, FL)],
         far="outs",
-        aliases=((count + 1, 0), (count + 2, 1)),
+        aliases=((count + outer, 0), (count + outer + 1, 1)),
     )
     return (grad_queries, grad_keys, grad_values, grad_proj)
 

time: 160 us -> 161 us (level)
  starting transfers between devices: 62.5 us -> 65 us
  waiting for transfers between devices: 53.8 us -> 52.1 us
    ppermute x43 -> x40, waiting for transfers between devices: 53.8 us -> 38.5 us  [exchange(): out.append(lax.ppermute(field, 'seq', flip) if k else field)]
    ppermute x1 -> x4, waiting for transfers between devices: 0.01 us -> 13.6 us  [per_device(): proj_parts.append(lax.ppermute(proj_send[k], 'seq', place))]
    ppermute x1 -> x4, starting transfers between devices: 0.65 us -> 3.86 us  [per_device(): proj_parts.append(lax.ppermute(proj_send[k], 'seq', place))]
    ppermute x43 -> x40, starting transfers between devices: 55.1 us -> 54.4 us  [exchange(): out.append(lax.ppermute(field, 'seq', flip) if k else field)]
where the time goes in v4:
time: 161 us
  starting transfers between devices  65 us (40%)
  waiting for transfers between devices  52.1 us (32%)
  Pallas kernels  40.1 us (25%)
  local copies, waits for them, and re-layouts  2.16 us (1%)
    ppermute x40, starting transfers between devices, exchange(): out.append(lax.ppermute(field, 'seq', flip) if k else field)  54.4 us
    pallas_call x14, Pallas kernels, call(): pl.pallas_call(kernel, in_specs=[pl.BlockSpec(memory_space=pltpu.SMEM)] +...  40.1 us
    ppermute x40, waiting for transfers between devices, exchange(): out.append(lax.ppermute(field, 'seq', flip) if k else field)  38.5 us
    ppermute x4, waiting for transfers between devices, per_device(): proj_parts.append(lax.ppermute(proj_send[k], 'seq', place))  13.6 us
    ppermute x2, starting transfers between devices, swap_edges(): lax.ppermute(upward, 'seq', up)  4.24 us
    ppermute x4, starting transfers between devices, per_device(): proj_parts.append(lax.ppermute(proj_send[k], 'seq', place))  3.86 us
  transfers between devices with their start and end apart: 48, of which 13 were waited for; matrix products, arithmetic and copies ran while one was open for 0% of the time, Pallas kernels for 12%

profile of v4, /device:TPU:0, one launch (start us, length us, event | category | flops | bytes accessed | tf_op | source)
XLA Modules:
  0.0 160.5 jit_solution(12292740265622033785)
XLA Ops:
  0.7 3.2 %shard_map.84 = (bf16[256,512]{1,0:T(8,128)(2,1)S(1)}, bf16[256,512]{1,0:T(8,128)(2,1)S(1)}, bf16[256,512]{1,0:T(8,128)(2,1)S(1)}, bf16[256,512]{1,0:T(8,128)(2,...) custom-call(s32[2]{0:T(128)S(1)} %pad_add_fusion.pos_ref, ...), custom_call_target="tpu_custom_call" | custom-call | tf_op jit(solution)/shard_map/pallas_call | solution.py:51
  4.5 2.6 %collective-permute-start.1 = (bf16[256,512]{1,0:T(8,128)(2,1)S(1)}, bf16[256,512]{1,0:T(8,128)(2,1)S(1)}, u32[]{:S(2)}, u32[]{:S(2)}) collective-permute-start(bf16[256,512]{1,0:T(8,128)(2,1)S(1)} %get-tuple-element.68), channel_id=1, source_target_pairs={{0,2},{1,3},{2,0},{3,1},{4,6},{5,7},{6,4},{7,5},{8,10},{9,11},{10,... | collective-permute-start | bytes 786440 | tf_op jit(solution)/shard_map/ppermute | solution.py:468
  8.9 2.6 %collective-permute-start.5 = (bf16[256,512]{1,0:T(8,128)(2,1)S(1)}, bf16[256,512]{1,0:T(8,128)(2,1)S(1)}, u32[]{:S(2)}, u32[]{:S(2)}) collective-permute-start(bf16[256,512]{1,0:T(8,128)(2,1)S(1)} %get-tuple-element.72), channel_id=1, source_target_pairs={{0,6},{1,7},{2,4},{3,5},{4,2},{5,3},{6,0},{7,1},{8,14},{9,15},{10,... | collective-permute-start | bytes 786440 | tf_op jit(solution)/shard_map/ppermute | solution.py:468
  11.5 2.7 %collective-permute-done.1.refs_2_.refs_0_ = bf16[256,512]{1,0:T(8,128)(2,1)S(1)} collective-permute-done((bf16[256,512]{1,0:T(8,128)(2,1)S(1)}, bf16[256,512]{1,0:T(8,128)(2,1)S(1)}, u32[]{:S(2)}, u32[]{:S(2)}) %collective-permute-start.1) | collective-permute-done | bytes 262176 | tf_op jit(solution)/shard_map/ppermute | solution.py:468
  15.9 3.0 %shard_map.88 = (bf16[256,512]{1,0:T(8,128)(2,1)S(1)}, bf16[256,512]{1,0:T(8,128)(2,1)}, bf16[256,512]{1,0:T(8,128)(2,1)}, bf16[256,512]{1,0:T(8,128)(2,1)}, bf1...) custom-call(s32[2]{0:T(128)S(1)} %pad_add_fusion.pos_ref, ...), custom_call_target="tpu_custom_call" | custom-call | tf_op jit(solution)/shard_map/pallas_call | solution.py:51
  23.0 8.8 %collective-permute-done.4.refs_5_.refs_3_ = bf16[256,512]{1,0:T(8,128)(2,1)S(1)} collective-permute-done((bf16[256,512]{1,0:T(8,128)(2,1)S(1)}, bf16[256,512]{1,0:T(8,128)(2,1)S(1)}, u32[]{:S(2)}, u32[]{:S(2)}) %collective-permute-start.4) | collective-permute-done | bytes 262176 | tf_op jit(solution)/shard_map/ppermute | solution.py:468
  31.8 2.3 %collective-permute-start.17 = (bf16[256,512]{1,0:T(8,128)(2,1)}, bf16[256,512]{1,0:T(8,128)(2,1)}, u32[]{:S(2)}, u32[]{:S(2)}) collective-permute-start(bf16[256,512]{1,0:T(8,128)(2,1)} %get-tuple-element.86), channel_id=1, source_target_pairs={{0,3},{1,2},{2,1},{3,0},{4,7},{5,6},{6,5},{7,4},{8,11},{9,10},{10,... | collective-permute-start | bytes 786440 | tf_op jit(solution)/shard_map/ppermute | solution.py:468
  35.7 2.5 %shard_map.85 = (f32[2,256,256]{2,1,0:T(8,128)S(1)}, f32[8,256]{1,0:T(8,128)S(1)}) custom-call(s32[2]{0:T(128)S(1)} %pad_add_fusion.pos_ref, bf16[256,512]{1,0:T(8,128)(2,1)S(1)} %get-tuple-element.66.refs_0_, bf16[256,512]{1,0:T(8,128)(2,1)S(1)} %collective-permute-done.refs_1_, bf16[256,512]{1,0:T(8,128)(2,1)S(1)} %collective-permute-done.1.refs_2_.refs_0_, ...), custom_call_target="tpu_custom_call" | custom-call | tf_op jit(solution)/shard_map/pallas_call | solution.py:51
  38.2 2.1 %shard_map.86 = (bf16[128,512]{1,0:T(8,128)(2,1)S(1)}, bf16[128,512]{1,0:T(8,128)(2,1)S(1)}, f32[136,256]{1,0:T(8,128)S(1)}, f32[136,256]{1,0:T(8,128)S(1)}, f32...) custom-call(s32[2]{0:T(128)S(1)} %pad_add_fusion.pos_ref, bf16[256,512]{1,0:T(8,128)(2,1)S(1)} %get-tuple-element.66.refs_0_, ...), custom_call_target="tpu_custom_call" | custom-call | tf_op jit(solution)/shard_map/pallas_call | solution.py:51
  44.9 2.6 %collective-permute-start.10 = (f32[136,256]{1,0:T(8,128)S(1)}, f32[136,256]{1,0:T(8,128)S(1)}, u32[]{:S(2)}, u32[]{:S(2)}) collective-permute-start(f32[136,256]{1,0:T(8,128)S(1)} %get-tuple-element.80), channel_id=1, source_target_pairs={{0,16},{1,17},{2,18},{3,19},{4,20},{5,21},{6,22},{7,23},{8,24},{9,... | collective-permute-start | bytes 417800 | tf_op jit(solution)/shard_map/ppermute | solution.py:468
  49.1 9.0 %collective-permute-done.10.refs_2_ = f32[136,256]{1,0:T(8,128)S(1)} collective-permute-done((f32[136,256]{1,0:T(8,128)S(1)}, f32[136,256]{1,0:T(8,128)S(1)}, u32[]{:S(2)}, u32[]{:S(2)}) %collective-permute-start.10) | collective-permute-done | bytes 139296 | tf_op jit(solution)/shard_map/ppermute | solution.py:468
  58.0 2.2 %collective-permute-start.7 = (bf16[128,512]{1,0:T(8,128)(2,1)S(1)}, bf16[128,512]{1,0:T(8,128)(2,1)S(1)}, u32[]{:S(2)}, u32[]{:S(2)}) collective-permute-start(bf16[128,512]{1,0:T(8,128)(2,1)S(1)} %get-tuple-element.76), channel_id=1, source_target_pairs={{0,8},{1,9},{2,10},{3,11},{4,12},{5,13},{6,14},{7,15},{8,16},{9,17... | collective-permute-start | bytes 393224 | tf_op jit(solution)/shard_map/ppermute | solution.py:475
  62.3 5.5 %collective-permute-start.14 = (bf16[128,256]{1,0:T(8,128)(2,1)S(1)}, bf16[128,256]{1,0:T(8,128)(2,1)S(1)}, u32[]{:S(2)}, u32[]{:S(2)}) collective-permute-start(bf16[128,256]{1,0:T(8,128)(2,1)S(1)} %get-tuple-element.82.refs_10_), channel_id=1, source_target_pairs={{0,24},{1,25},{2,26},{3,27},{4,28},{5,29},{6,30},{7,31},{8,16},{9,... | collective-permute-start | bytes 196616 | tf_op jit(solution)/shard_map/ppermute | solution.py:468
  68.5 3.2 %collective-permute-done.14.refs_13_ = bf16[128,256]{1,0:T(8,128)(2,1)S(1)} collective-permute-done((bf16[128,256]{1,0:T(8,128)(2,1)S(1)}, bf16[128,256]{1,0:T(8,128)(2,1)S(1)}, u32[]{:S(2)}, u32[]{:S(2)}) %collective-permute-start.14) | collective-permute-done | bytes 65568 | tf_op jit(solution)/shard_map/ppermute | solution.py:468
  73.4 15.3 %shard_map.89 = (bf16[256,256]{1,0:T(8,128)(2,1)S(1)}, bf16[256,256]{1,0:T(8,128)(2,1)S(1)}, bf16[256,256]{1,0:T(8,128)(2,1)S(1)}, bf16[256,256]{1,0:T(8,128)(2,...) custom-call(s32[2]{0:T(128)S(1)} %pad_add_fusion.pos_ref, ...), custom_call_target="tpu_custom_call" | custom-call | tf_op jit(solution)/shard_map/pallas_call | solution.py:51
  92.9 2.4 %collective-permute-start.33 = (bf16[128,256]{1,0:T(8,128)(2,1)S(1)}, bf16[128,256]{1,0:T(8,128)(2,1)S(1)}, u32[]{:S(2)}, u32[]{:S(2)}) collective-permute-start(bf16[128,256]{1,0:T(8,128)(2,1)S(1)} %get-tuple-element.107), channel_id=1, source_target_pairs={{0,24},{1,25},{2,26},{3,27},{4,28},{5,29},{6,30},{7,31},{8,16},{9,... | collective-permute-start | bytes 196616 | tf_op jit(solution)/shard_map/ppermute | solution.py:468
  96.6 3.3 %collective-permute-done.32.refs_3_ = bf16[128,256]{1,0:T(8,128)(2,1)S(1)} collective-permute-done((bf16[128,256]{1,0:T(8,128)(2,1)S(1)}, bf16[128,256]{1,0:T(8,128)(2,1)S(1)}, u32[]{:S(2)}, u32[]{:S(2)}) %collective-permute-start.32) | collective-permute-done | bytes 65568 | tf_op jit(solution)/shard_map/ppermute | solution.py:468
  102.3 3.4 %collective-permute-start.35 = (bf16[144,256]{1,0:T(8,128)(2,1)S(1)}, bf16[144,256]{1,0:T(8,128)(2,1)S(1)}, u32[]{:S(2)}, u32[]{:S(2)}) collective-permute-start(bf16[144,256]{1,0:T(8,128)(2,1)S(1)} %shard_map.91.refs_9_.refs_7_), channel_id=1, source_target_pairs={{0,16},{1,17},{2,18},{3,19},{4,20},{5,21},{6,22},{7,23},{8,24},{9,... | collective-permute-start | bytes 221192 | tf_op jit(solution)/shard_map/ppermute | solution.py:468
  119.4 3.1 %shard_map.92 = (bf16[256,512]{1,0:T(8,128)(2,1)S(1)}, bf16[256,512]{1,0:T(8,128)(2,1)S(1)}, bf16[256,512]{1,0:T(8,128)(2,1)S(1)}, bf16[256,512]{1,0:T(8,128)(2,1)S(1)}, bf16[1024,512]{1,0:T(8,128)(2,1)S(1)}) custom-call(s32[2]{0:T(128)S(1)} %pad_add_fusion.pos_ref, bf16[256,512]{1,0:T(8,128)(2,1)S(1)} %collective-permute-done.1.refs_2_.refs_0_, ...), custom_call_target="tpu_custom_call" | custom-call | tf_op jit(solution)/shard_map/pallas_call | solution.py:51
  124.2 4.3 %collective-permute-done.27.refs_6_ = bf16[256,256]{1,0:T(8,128)(2,1)S(1)} collective-permute-done((bf16[256,256]{1,0:T(8,128)(2,1)S(1)}, bf16[256,256]{1,0:T(8,128)(2,1)S(1)}, u32[]{:S(2)}, u32[]{:S(2)}) %collective-permute-start.27) | collective-permute-done | bytes 131104 | tf_op jit(solution)/shard_map/ppermute | solution.py:468
  130.5 3.9 %collective-permute-start.47 = (bf16[256,512]{1,0:T(8,128)(2,1)S(1)}, bf16[256,512]{1,0:T(8,128)(2,1)S(1)}, u32[]{:S(2)}, u32[]{:S(2)}) collective-permute-start(bf16[256,512]{1,0:T(8,128)(2,1)S(1)} %get-tuple-element.122), channel_id=1, source_target_pairs={{0,7},{1,6},{2,5},{3,4},{4,3},{5,2},{6,1},{7,0},{8,15},{9,14},{10,... | collective-permute-start | bytes 786440 | tf_op jit(solution)/shard_map/ppermute | solution.py:468
  134.4 6.4 %collective-permute-done.42.refs_5_ = f32[64,256]{1,0:T(8,128)S(1)} collective-permute-done((f32[64,256]{1,0:T(8,128)S(1)}, f32[64,256]{1,0:T(8,128)S(1)}, u32[]{:S(2)}, u32[]{:S(2)}) %collective-permute-start.42) | collective-permute-done | bytes 65568 | tf_op jit(solution)/shard_map/ppermute | solution.py:603
  144.3 2.2 %collective-permute-start.44 = (f32[64,256]{1,0:T(8,128)S(1)}, f32[64,256]{1,0:T(8,128)S(1)}, u32[]{:S(2)}, u32[]{:S(2)}) collective-permute-start(f32[64,256]{1,0:T(8,128)S(1)} %get-tuple-element.118), channel_id=1, source_target_pairs={{0,3},{1,7},{2,11},{3,15},{4,19},{5,23},{6,27},{7,31},{8,2},{9,6},... | collective-permute-start | bytes 196616 | tf_op jit(solution)/shard_map/ppermute | solution.py:603
  149.8 7.2 %collective-permute-done.44.refs_7_ = f32[64,256]{1,0:T(8,128)S(1)} collective-permute-done((f32[64,256]{1,0:T(8,128)S(1)}, f32[64,256]{1,0:T(8,128)S(1)}, u32[]{:S(2)}, u32[]{:S(2)}) %collective-permute-start.44) | collective-permute-done | bytes 65568 | tf_op jit(solution)/shard_map/ppermute | solution.py:603
  (96 shorter events, 55.5 us)
Async XLA Ops:
  7.1 13.9 %collective-permute-start.2 = (bf16[256,512]{1,0:T(8,128)(2,1)S(1)}, bf16[256,512]{1,0:T(8,128)(2,1)S(1)}, u32[]{:S(2)}, u32[]{:S(2)}) collective-permute-start(bf16[256,512]{1,0:T(8,128)(2,1)S(1)} %get-tuple-element.69), channel_id=1, source_target_pairs={{0,3},{1,2},{2,1},{3,0},{4,7},{5,6},{6,5},{7,4},{8,11},{9,10},{10,... | collective-permute-start | bytes 786440 | tf_op jit(solution)/shard_map/ppermute | solution.py:468
  7.1 15.3 %collective-permute-start.3 = (bf16[256,512]{1,0:T(8,128)(2,1)S(1)}, bf16[256,512]{1,0:T(8,128)(2,1)S(1)}, u32[]{:S(2)}, u32[]{:S(2)}) collective-permute-start(bf16[256,512]{1,0:T(8,128)(2,1)S(1)} %get-tuple-element.70), channel_id=1, source_target_pairs={{0,4},{1,5},{2,6},{3,7},{4,0},{5,1},{6,2},{7,3},{8,12},{9,13},{10,... | collective-permute-start | bytes 786440 | tf_op jit(solution)/shard_map/ppermute | solution.py:468
  8.9 22.9 %collective-permute-start.4 = (bf16[256,512]{1,0:T(8,128)(2,1)S(1)}, bf16[256,512]{1,0:T(8,128)(2,1)S(1)}, u32[]{:S(2)}, u32[]{:S(2)}) collective-permute-start(bf16[256,512]{1,0:T(8,128)(2,1)S(1)} %get-tuple-element.71), channel_id=1, source_target_pairs={{0,5},{1,4},{2,7},{3,6},{4,1},{5,0},{6,3},{7,2},{8,13},{9,12},{10,... | collective-permute-start | bytes 786440 | tf_op jit(solution)/shard_map/ppermute | solution.py:468
  8.9 25.2 %collective-permute-start.5 = (bf16[256,512]{1,0:T(8,128)(2,1)S(1)}, bf16[256,512]{1,0:T(8,128)(2,1)S(1)}, u32[]{:S(2)}, u32[]{:S(2)}) collective-permute-start(bf16[256,512]{1,0:T(8,128)(2,1)S(1)} %get-tuple-element.72), channel_id=1, source_target_pairs={{0,6},{1,7},{2,4},{3,5},{4,2},{5,3},{6,0},{7,1},{8,14},{9,15},{10,... | collective-permute-start | bytes 786440 | tf_op jit(solution)/shard_map/ppermute | solution.py:468
  14.2 24.0 %collective-permute-start.6 = (bf16[256,512]{1,0:T(8,128)(2,1)}, bf16[256,512]{1,0:T(8,128)(2,1)S(1)}, u32[]{:S(2)}, u32[]{:S(2)}) collective-permute-start(bf16[256,512]{1,0:T(8,128)(2,1)} %get-tuple-element.73), channel_id=1, source_target_pairs={{0,7},{1,6},{2,5},{3,4},{4,3},{5,2},{6,1},{7,0},{8,15},{9,14},{10,... | collective-permute-start | bytes 786440 | tf_op jit(solution)/shard_map/ppermute | solution.py:468
  21.0 21.0 %collective-permute-start.15 = (bf16[256,512]{1,0:T(8,128)(2,1)}, bf16[256,512]{1,0:T(8,128)(2,1)}, u32[]{:S(2)}, u32[]{:S(2)}) collective-permute-start(bf16[256,512]{1,0:T(8,128)(2,1)} %get-tuple-element.84), channel_id=1, source_target_pairs={{0,1},{1,0},{2,3},{3,2},{4,5},{5,4},{6,7},{7,6},{8,9},{9,8},{10,11... | collective-permute-start | bytes 786440 | tf_op jit(solution)/shard_map/ppermute | solution.py:468
  22.5 19.6 %collective-permute-start.16 = (bf16[256,512]{1,0:T(8,128)(2,1)}, bf16[256,512]{1,0:T(8,128)(2,1)}, u32[]{:S(2)}, u32[]{:S(2)}) collective-permute-start(bf16[256,512]{1,0:T(8,128)(2,1)} %get-tuple-element.85), channel_id=1, source_target_pairs={{0,2},{1,3},{2,0},{3,1},{4,6},{5,7},{6,4},{7,5},{8,10},{9,11},{10,... | collective-permute-start | bytes 786440 | tf_op jit(solution)/shard_map/ppermute | solution.py:468
  42.0 20.3 %collective-permute-start.19 = (bf16[256,512]{1,0:T(8,128)(2,1)}, bf16[256,512]{1,0:T(8,128)(2,1)S(1)}, u32[]{:S(2)}, u32[]{:S(2)}) collective-permute-start(bf16[256,512]{1,0:T(8,128)(2,1)} %copy-done.3), channel_id=1, source_target_pairs={{0,5},{1,4},{2,7},{3,6},{4,1},{5,0},{6,3},{7,2},{8,13},{9,12},{10,... | collective-permute-start | bytes 786440 | tf_op jit(solution)/shard_map/ppermute | solution.py:468
  42.0 25.8 %collective-permute-start.20 = (bf16[256,512]{1,0:T(8,128)(2,1)}, bf16[256,512]{1,0:T(8,128)(2,1)S(1)}, u32[]{:S(2)}, u32[]{:S(2)}) collective-permute-start(bf16[256,512]{1,0:T(8,128)(2,1)} %copy-done.2), channel_id=1, source_target_pairs={{0,6},{1,7},{2,4},{3,5},{4,2},{5,3},{6,0},{7,1},{8,14},{9,15},{10,... | collective-permute-start | bytes 786440 | tf_op jit(solution)/shard_map/ppermute | solution.py:468
  42.9 24.9 %collective-permute-start.21 = (bf16[256,512]{1,0:T(8,128)(2,1)}, bf16[256,512]{1,0:T(8,128)(2,1)S(1)}, u32[]{:S(2)}, u32[]{:S(2)}) collective-permute-start(bf16[256,512]{1,0:T(8,128)(2,1)} %copy-done.1), channel_id=1, source_target_pairs={{0,7},{1,6},{2,5},{3,4},{4,3},{5,2},{6,1},{7,0},{8,15},{9,14},{10,... | collective-permute-start | bytes 786440 | tf_op jit(solution)/shard_map/ppermute | solution.py:468
  44.9 13.2 %collective-permute-start.10 = (f32[136,256]{1,0:T(8,128)S(1)}, f32[136,256]{1,0:T(8,128)S(1)}, u32[]{:S(2)}, u32[]{:S(2)}) collective-permute-start(f32[136,256]{1,0:T(8,128)S(1)} %get-tuple-element.80), channel_id=1, source_target_pairs={{0,16},{1,17},{2,18},{3,19},{4,20},{5,21},{6,22},{7,23},{8,24},{9,... | collective-permute-start | bytes 417800 | tf_op jit(solution)/shard_map/ppermute | solution.py:468
  47.5 12.8 %collective-permute-start.11 = (f32[136,256]{1,0:T(8,128)S(1)}, f32[136,256]{1,0:T(8,128)S(1)}, u32[]{:S(2)}, u32[]{:S(2)}) collective-permute-start(f32[136,256]{1,0:T(8,128)S(1)} %get-tuple-element.81), channel_id=1, source_target_pairs={{0,24},{1,25},{2,26},{3,27},{4,28},{5,29},{6,30},{7,31},{8,16},{9,... | collective-permute-start | bytes 417800 | tf_op jit(solution)/shard_map/ppermute | solution.py:468
  88.7 16.9 %collective-permute-start.29 = (bf16[128,512]{1,0:T(8,128)(2,1)S(1)}, bf16[128,512]{1,0:T(8,128)(2,1)S(1)}, u32[]{:S(2)}, u32[]{:S(2)}) collective-permute-start(bf16[128,512]{1,0:T(8,128)(2,1)S(1)} %get-tuple-element.101), channel_id=1, source_target_pairs={{0,8},{1,9},{2,10},{3,11},{4,12},{5,13},{6,14},{7,15},{8,16},{9,17... | collective-permute-start | bytes 393224 | tf_op jit(solution)/shard_map/ppermute | solution.py:475
  111.2 12.4 %collective-permute-start.26 = (bf16[256,256]{1,0:T(8,128)(2,1)S(1)}, bf16[256,256]{1,0:T(8,128)(2,1)S(1)}, u32[]{:S(2)}, u32[]{:S(2)}) collective-permute-start(bf16[256,256]{1,0:T(8,128)(2,1)S(1)} %get-tuple-element.96), channel_id=1, source_target_pairs={{0,5},{1,4},{2,7},{3,6},{4,1},{5,0},{6,3},{7,2},{8,13},{9,12},{10,... | collective-permute-start | bytes 393224 | tf_op jit(solution)/shard_map/ppermute | solution.py:468
  114.7 28.4 %collective-permute-start.45 = (bf16[256,512]{1,0:T(8,128)(2,1)S(1)}, bf16[256,512]{1,0:T(8,128)(2,1)S(1)}, u32[]{:S(2)}, u32[]{:S(2)}) collective-permute-start(bf16[256,512]{1,0:T(8,128)(2,1)S(1)} %get-tuple-element.120), channel_id=1, source_target_pairs={{0,1},{1,0},{2,3},{3,2},{4,5},{5,4},{6,7},{7,6},{8,9},{9,8},{10,11... | collective-permute-start | bytes 786440 | tf_op jit(solution)/shard_map/ppermute | solution.py:468
  115.6 28.3 %collective-permute-start.46 = (bf16[256,512]{1,0:T(8,128)(2,1)S(1)}, bf16[256,512]{1,0:T(8,128)(2,1)S(1)}, u32[]{:S(2)}, u32[]{:S(2)}) collective-permute-start(bf16[256,512]{1,0:T(8,128)(2,1)S(1)} %get-tuple-element.121), channel_id=1, source_target_pairs={{0,6},{1,7},{2,4},{3,5},{4,2},{5,3},{6,0},{7,1},{8,14},{9,15},{10,... | collective-permute-start | bytes 786440 | tf_op jit(solution)/shard_map/ppermute | solution.py:468
  128.5 12.3 %collective-permute-start.42 = (f32[64,256]{1,0:T(8,128)S(1)}, f32[64,256]{1,0:T(8,128)S(1)}, u32[]{:S(2)}, u32[]{:S(2)}) collective-permute-start(f32[64,256]{1,0:T(8,128)S(1)} %get-tuple-element.116), channel_id=1, source_target_pairs={{0,1},{1,5},{2,9},{3,13},{4,17},{5,21},{6,25},{7,29},{8,0},{9,4},{... | collective-permute-start | bytes 196616 | tf_op jit(solution)/shard_map/ppermute | solution.py:603
  129.6 12.3 %collective-permute-start.43 = (f32[64,256]{1,0:T(8,128)S(1)}, f32[64,256]{1,0:T(8,128)S(1)}, u32[]{:S(2)}, u32[]{:S(2)}) collective-permute-start(f32[64,256]{1,0:T(8,128)S(1)} %get-tuple-element.117), channel_id=1, source_target_pairs={{0,2},{1,6},{2,10},{3,14},{4,18},{5,22},{6,26},{7,30},{8,3},{9,7},... | collective-permute-start | bytes 196616 | tf_op jit(solution)/shard_map/ppermute | solution.py:603
  130.5 13.8 %collective-permute-start.47 = (bf16[256,512]{1,0:T(8,128)(2,1)S(1)}, bf16[256,512]{1,0:T(8,128)(2,1)S(1)}, u32[]{:S(2)}, u32[]{:S(2)}) collective-permute-start(bf16[256,512]{1,0:T(8,128)(2,1)S(1)} %get-tuple-element.122), channel_id=1, source_target_pairs={{0,7},{1,6},{2,5},{3,4},{4,3},{5,2},{6,1},{7,0},{8,15},{9,14},{10,... | collective-permute-start | bytes 786440 | tf_op jit(solution)/shard_map/ppermute | solution.py:468
  140.8 16.2 %collective-permute-start.37 = (bf16[256,512]{1,0:T(8,128)(2,1)S(1)}, bf16[256,512]{1,0:T(8,128)(2,1)S(1)}, u32[]{:S(2)}, u32[]{:S(2)}) collective-permute-start(bf16[256,512]{1,0:T(8,128)(2,1)S(1)} %get-tuple-element.108), channel_id=1, source_target_pairs={{0,2},{1,3},{2,0},{3,1},{4,6},{5,7},{6,4},{7,5},{8,10},{9,11},{10,... | collective-permute-start | bytes 786440 | tf_op jit(solution)/shard_map/ppermute | solution.py:468
  141.9 15.1 %collective-permute-start.38 = (bf16[256,512]{1,0:T(8,128)(2,1)S(1)}, bf16[256,512]{1,0:T(8,128)(2,1)S(1)}, u32[]{:S(2)}, u32[]{:S(2)}) collective-permute-start(bf16[256,512]{1,0:T(8,128)(2,1)S(1)} %get-tuple-element.109), channel_id=1, source_target_pairs={{0,3},{1,2},{2,1},{3,0},{4,7},{5,6},{6,5},{7,4},{8,11},{9,10},{10,... | collective-permute-start | bytes 786440 | tf_op jit(solution)/shard_map/ppermute | solution.py:468
  143.1 13.9 %collective-permute-start.39 = (bf16[256,512]{1,0:T(8,128)(2,1)S(1)}, bf16[256,512]{1,0:T(8,128)(2,1)S(1)}, u32[]{:S(2)}, u32[]{:S(2)}) collective-permute-start(bf16[256,512]{1,0:T(8,128)(2,1)S(1)} %get-tuple-element.110), channel_id=1, source_target_pairs={{0,4},{1,5},{2,6},{3,7},{4,0},{5,1},{6,2},{7,3},{8,12},{9,13},{10,... | collective-permute-start | bytes 786440 | tf_op jit(solution)/shard_map/ppermute | solution.py:468
  143.9 14.8 %collective-permute-start.40 = (bf16[256,512]{1,0:T(8,128)(2,1)S(1)}, bf16[256,512]{1,0:T(8,128)(2,1)S(1)}, u32[]{:S(2)}, u32[]{:S(2)}) collective-permute-start(bf16[256,512]{1,0:T(8,128)(2,1)S(1)} %get-tuple-element.111), channel_id=1, source_target_pairs={{0,5},{1,4},{2,7},{3,6},{4,1},{5,0},{6,3},{7,2},{8,13},{9,12},{10,... | collective-permute-start | bytes 786440 | tf_op jit(solution)/shard_map/ppermute | solution.py:468
  144.3 12.7 %collective-permute-start.44 = (f32[64,256]{1,0:T(8,128)S(1)}, f32[64,256]{1,0:T(8,128)S(1)}, u32[]{:S(2)}, u32[]{:S(2)}) collective-permute-start(f32[64,256]{1,0:T(8,128)S(1)} %get-tuple-element.118), channel_id=1, source_target_pairs={{0,3},{1,7},{2,11},{3,15},{4,19},{5,23},{6,27},{7,31},{8,2},{9,6},... | collective-permute-start | bytes 196616 | tf_op jit(solution)/shard_map/ppermute | solution.py:603
  (28 other events, 236.8 us)
